TPU v7x, 768 devices: a whole 4x8x12 slice. The times are simulated.
768 devices in a mesh: gx: 8 (over y_lo, core), gy: 96 (over y_hi, z, x).
Axes of the slice: x: 4, y: 8 (y_hi: 2, y_lo: 4; y = y_hi * 4 + y_lo), z: 12, core: 2. Of those that a mesh axis runs over, the one named last changes fastest.
Arguments:
- positions: float32 [3, 8, 96, 512], P(None, 'gx', 'gy'), may hold values from 0 to 32, as said below
- species: int32 [8, 96, 512], P('gx', 'gy'), may hold values from 0 to 4
- send_index: int32 [8, 96, 384], P('gx', 'gy'), may hold values from 0 to 511, as said below
- edge_centers: int32 [8, 96, 512], P('gx', 'gy'), may hold values from 0 to 511, as said below
- edge_neighbours: int32 [8, 96, 512], P('gx', 'gy'), may hold values from 0 to 3967, as said below
- block_counts: int32 [8, 96, 4], P('gx', 'gy'), may hold values from 1 to 128, as said below
- emb_center: float32 [5, 128], replicated, may hold values from -5 to 5
- emb_neighbour: float32 [5, 128], replicated, may hold values from -5 to 5
- radial_w: float32 [8, 128], replicated, may hold values from -2 to 2
- env_w: float32 [2, 128, 128], replicated, may hold values from -0.5 to 0.5
- mix_w: float32 [2, 128, 128], replicated, may hold values from -0.5 to 0.5
- out_w: float32 [128], replicated, may hold values from -0.5 to 0.5
Outputs:
- forces: float32 [3, 8, 96, 512], P(None, 'gx', 'gy')
- grad_mix: float32 [2, 128, 128], replicated
- grad_out: float32 [128], replicated
- mean_energy: float32 [], replicated
Inputs may be any that keep to these rules, and one draw needn't show every extreme that they name: `positions`: each atom lies within its device's block; every edge's neighbour lies within 6 of its centre in the pool's coordinates. `send_index`: within one block the 384 entries are distinct atoms, in rising order: those within two lattice columns of the block's four side faces. `edge_centers`: within one block the centres are non-decreasing along the edge slots. `edge_neighbours`: pool index into the block's pool; slot 4 (the block itself) is never named: the value lies in [0, 512) or in [512 + s * 384, 512 + (s + 1) * 384) with s != 4; it never names the centre itself. `block_counts`: the first edge block of every device is full.
All inputs are finite; a program needn't handle non-finite values.
Results may differ from a plain program's by a relative error of at most 0.0003.
Values sent between devices are 32-bit elements; how exact they have to be, the bound alone decides.
No kernel may reach another device: no remote copies, remote signals or barrier semaphores. Data moves between devices by JAX's collectives and lax.ppermute only.
A program may use at most 32 MiB of HBM per device.

v0:
```python
import functools

import jax
import jax.numpy as jnp
from jax import lax
from jax.sharding import Mesh
from jax.sharding import PartitionSpec as P

BLOCK_EDGES = 128
LAT = 8
GX_GY = ("gx_0", "gx_1", "gy_0", "gy_1", "gy_2")
GX = ("gx_0", "gx_1")
GY = ("gy_0", "gy_1", "gy_2")


CUTOFF = 6.0
SOFTENING = 0.25
SPACING = 1.7
PRECISE = lax.Precision.HIGHEST


def extended(shard, sides, width):
    for axis, dim in sides:
        devices, length = (lax.axis_size(axis), shard.shape[dim])
        up = [(i, (i + 1) % devices) for i in range(devices)]
        down = [(j, i) for i, j in up]
        last = lax.slice_in_dim(shard, length - width, length, axis=dim)
        leading = lax.slice_in_dim(shard, 0, width, axis=dim)
        before = lax.ppermute(last, axis, up)
        after = lax.ppermute(leading, axis, down)
        shard = jnp.concatenate([before, shard, after], axis=dim)
    return shard


def passed_along(block, axis, distance):
    devices = range(lax.axis_size(axis))
    route = [((i - distance) % len(devices), i) for i in devices]
    return lax.ppermute(block, axis, route)


def over_axes(shard, axes):
    return functools.reduce(lax.psum, axes, shard)


def device_energy(
    own_pos,
    ghost_pos,
    ghost_species,
    own_species,
    centers,
    neighbours,
    counts,
    emb_center,
    emb_neighbour,
    radial_w,
    env_w,
    mix_w,
    out_w,
):
    block_side = SPACING * LAT
    atom_count = own_pos.shape[1]
    ghost_total = ghost_pos.shape[1]
    per_slot = ghost_total // 9
    slot_ids = jnp.arange(ghost_total) // per_slot
    shift_x = (slot_ids // 3 - 1).astype(jnp.float32) * block_side
    shift_y = (slot_ids % 3 - 1).astype(jnp.float32) * block_side
    offset = jnp.stack([shift_x, shift_y, jnp.zeros_like(shift_x)])
    pool_pos = jnp.concatenate([own_pos, ghost_pos + offset], axis=1)
    pool_species = jnp.concatenate([own_species, ghost_species])
    edge_total = centers.shape[0]
    offset_vec = pool_pos[:, neighbours] - own_pos[:, centers]
    radius = jnp.sqrt(jnp.sum(offset_vec * offset_vec, axis=0) + SOFTENING)
    unit_vec = offset_vec / radius
    ratio = radius / CUTOFF
    smooth = (1.0 - ratio * ratio) ** 2
    slot_in_block = jnp.arange(edge_total) % BLOCK_EDGES
    block_of = jnp.arange(edge_total) // BLOCK_EDGES
    live_mask = (slot_in_block < counts[block_of]).astype(jnp.float32)
    orders = jnp.arange(1, radial_w.shape[0] + 1).astype(jnp.float32)
    radial_basis = jnp.sin(orders[None, :] * jnp.pi * radius[:, None] / CUTOFF) / radius[:, None]
    kinds = jnp.arange(emb_center.shape[0]).astype(jnp.float32)
    centre_hot = (own_species[centers][:, None] == kinds[None, :]).astype(jnp.float32)
    neighbour_hot = (pool_species[neighbours][:, None] == kinds[None, :]).astype(jnp.float32)
    summed = jnp.dot(centre_hot, emb_center, precision=PRECISE)
    summed = summed + jnp.dot(neighbour_hot, emb_neighbour, precision=PRECISE)
    summed = summed + jnp.dot(radial_basis, radial_w, precision=PRECISE)
    latent = jax.nn.silu(summed) * smooth[:, None]
    for layer in range(env_w.shape[0]):
        weighted = jnp.dot(latent, env_w[layer], precision=PRECISE) * live_mask[:, None]
        back = jnp.zeros_like(latent)
        for comp in range(3):
            environ = jax.ops.segment_sum(
                weighted * unit_vec[comp][:, None],
                centers,
                num_segments=atom_count,
                indices_are_sorted=True,
            )
            back = back + environ[centers] * unit_vec[comp][:, None]
        coupled = latent * back
        latent = latent + jax.nn.silu(jnp.dot(coupled, mix_w[layer], precision=PRECISE))
    readout = jnp.dot(latent, out_w, precision=PRECISE)
    return jnp.sum(live_mask * smooth * readout)


def body(
    positions,
    species,
    send_index,
    edge_centers,
    edge_neighbours,
    block_counts,
    emb_center,
    emb_neighbour,
    radial_w,
    env_w,
    mix_w,
    out_w,
):
    own_pos = positions[:, 0, 0, :]
    own_species = species[0, 0].astype(jnp.float32)
    chosen = send_index[0, 0]
    per_slot = chosen.shape[0]
    atom_count = own_pos.shape[1]
    exported = jnp.concatenate([own_pos[:, chosen], own_species[chosen][None, :]], axis=0)
    ghosts = extended(exported[:, None, None, :], ((GX, 1), (GY, 2)), 1)
    ghosts = ghosts.reshape(4, 9 * per_slot)
    ghost_species = ghosts[3]
    centers = edge_centers[0, 0]
    neighbours = edge_neighbours[0, 0]
    counts = block_counts[0, 0]

    def local_energy(own_part, ghost_part, mix_part, out_part):
        return device_energy(
            own_part,
            ghost_part,
            ghost_species,
            own_species,
            centers,
            neighbours,
            counts,
            emb_center,
            emb_neighbour,
            radial_w,
            env_w,
            mix_part,
            out_part,
        )

    energy, pullback = jax.vjp(local_energy, own_pos, ghosts[:3], mix_w, out_w)
    grad_own, grad_ghost, grad_mixing, grad_readout = pullback(jnp.ones((), jnp.float32))
    grid = grad_ghost.reshape(3, 3, 3, per_slot)
    from_next = passed_along(grid[:, 0], GX, -1)
    from_prev = passed_along(grid[:, 2], GX, 1)
    column = grid[:, 1] + from_next + from_prev
    returned = column[:, 1] + passed_along(column[:, 0], GY, -1)
    returned = returned + passed_along(column[:, 2], GY, 1)
    total_grad = grad_own.at[:, chosen].add(returned)
    forces = (-total_grad).reshape(3, 1, 1, atom_count)
    mix_sum, out_sum, energy_sum = (
        over_axes(grad_mixing, GX_GY),
        over_axes(grad_readout, GX_GY),
        over_axes(energy, GX_GY),
    )
    scale = jnp.float32(lax.axis_size(GX) * lax.axis_size(GY))
    return (forces, mix_sum / scale, out_sum / scale, energy_sum / scale)


def solution(mesh):
    finer = Mesh(mesh.devices.reshape(4, 2, 2, 12, 4), ("gx_0", "gx_1", "gy_0", "gy_1", "gy_2"))
    placed = (
        P(None, GX, GY, None),
        P(GX, GY, None),
        P(GX, GY, None),
        P(GX, GY, None),
        P(GX, GY, None),
        P(GX, GY, None),
        P(),
        P(),
        P(),
        P(),
        P(),
        P(),
    )
    return jax.shard_map(
        body,
        mesh=finer,
        in_specs=placed,
        out_specs=(P(None, GX, GY, None), P(), P(), P()),
        check_vma=False,
    )
```

profile of v0, /device:TPU:1, one launch (start us, length us, event | category | flops | bytes accessed | tf_op | source)
XLA Modules:
  0.0 494.4 jit_solution(17564580914944428461)
XLA Ops:
  8.7 2.8 gather_fusion.2
  12.9 12.4 %collective-permute-start.1 = (f32[4,1,1,384]{3,0,2,1:T(4,128)S(1)}, f32[4,1,1,384]{3,0,2,1:T(4,128)S(1)}, u32[]{:S(2)}, u32[]{:S(2)}) collective-permute-start(f32[4,1,1,384]{3,0,2,1:T(4,128)S(1)} %maximum_bitcast_fusion), channel_id=1, source_target_pairs={{96,0},{192,96},{288,192},{384,288},{480,384},{576,480},{672,576},... | collective-permute-start | bytes 18440 | tf_op jit(solution)/shard_map/ppermute | solution.py:30
  31.2 3.5 gather_fusion
  36.0 13.8 %collective-permute-start.3 = (f32[4,3,1,384]{3,0,2,1:T(4,128)S(1)}, f32[4,3,1,384]{3,0,2,1:T(4,128)S(1)}, u32[]{:S(2)}, u32[]{:S(2)}) collective-permute-start(f32[4,3,1,384]{3,0,2,1:T(4,128)S(1)} %pad_maximum_fusion.5), channel_id=1, source_target_pairs={{1,0},{2,1},{3,2},{4,3},{5,4},{6,5},{7,6},{8,7},{9,8},{10,9},{11,1... | collective-permute-start | bytes 55304 | tf_op jit(solution)/shard_map/ppermute | solution.py:30
  53.9 8.9 %collective-permute-done.2 = f32[4,3,1,384]{3,0,2,1:T(4,128)S(1)} collective-permute-done((f32[4,3,1,384]{3,0,2,1:T(4,128)S(1)}, f32[4,3,1,384]{3,0,2,1:T(4,128)S(1)}, u32[]{:S(2)}, u32[]{:S(2)}) %collective-permute-start.2) | collective-permute-done | bytes 18464 | tf_op jit(solution)/shard_map/ppermute | solution.py:29
  66.6 3.1 gather_fusion.3
  73.9 2.6 scatter_custom_fusion
  77.8 3.1 scatter_custom_fusion.2
  82.3 2.7 scatter_custom_fusion.1
  88.8 2.7 scatter_custom_fusion.5
  92.7 2.7 scatter_custom_fusion.4
  96.7 2.8 scatter_custom_fusion.3
  106.0 2.6 scatter_custom_fusion.7
  110.1 2.8 scatter_custom_fusion.8
  114.3 3.0 scatter_custom_fusion.6
  127.5 2.8 scatter_custom_fusion.9
  134.8 3.0 scatter_custom_fusion.11
  143.1 3.3 scatter_custom_fusion.10
  159.5 3.1 scatter_custom_fusion.12
  166.4 3.0 collective-permute-start.5
  173.6 10.5 %all-reduce.16 = (f32[128]{0:T(128)S(1)}, f32[]{:T(128)}) all-reduce(f32[128]{0:T(128)} %convolution_bitcast_fusion.2, f32[]{:T(128)} %get-tuple-element.50), channel_id=1, replica_groups=mesh['gx_0'=4,'gx_1'=2,'gy_0'=2,'gy_1'=12,'gy_2'=4] {'gx_0'}, use_global_device_ids=true, to_apply=%region_37.38 | all-reduce | flops 129 | bytes 1032 | tf_op jit(solution)/shard_map/psum | solution.py:42
  184.1 4.8 all-reduce.18
  188.9 8.3 %all-reduce.17 = (f32[128]{0:T(128)S(1)}, f32[]{:T(128)}) all-reduce(f32[128]{0:T(128)S(1)} %get-tuple-element.48, f32[]{:T(128)} %get-tuple-element.49), channel_id=1, replica_groups=mesh['gx_0'=4,'gx_1'=2,'gy_0'=2,'gy_1'=12,'gy_2'=4] {'gy_0'}, use_global_device_ids=true, to_apply=%region_39.40 | all-reduce | flops 129 | bytes 1032 | tf_op jit(solution)/shard_map/psum | solution.py:42
  197.2 16.0 %all-reduce.14 = (f32[128]{0:T(128)S(1)}, f32[]{:T(128)}) all-reduce(f32[128]{0:T(128)S(1)} %get-tuple-element.46, f32[]{:T(128)} %get-tuple-element.47), channel_id=1, replica_groups=mesh['gx_0'=4,'gx_1'=2,'gy_0'=2,'gy_1'=12,'gy_2'=4] {'gy_1'}, use_global_device_ids=true, to_apply=%region_40.41 | all-reduce | flops 129 | bytes 1032 | tf_op jit(solution)/shard_map/psum | solution.py:42
  213.2 7.2 %all-reduce.15 = (f32[128]{0:T(128)S(1)}, f32[]{:T(128)}) all-reduce(f32[128]{0:T(128)S(1)} %get-tuple-element.40, f32[]{:T(128)} %get-tuple-element.41), channel_id=1, replica_groups=mesh['gx_0'=4,'gx_1'=2,'gy_0'=2,'gy_1'=12,'gy_2'=4] {'gy_2'}, use_global_device_ids=true, to_apply=%region_41.42 | all-reduce | flops 129 | bytes 1032 | tf_op jit(solution)/shard_map/psum | solution.py:42
  221.2 10.7 %collective-permute-start.6 = (f32[3,384]{1,0:T(4,128)S(1)}, f32[3,384]{1,0:T(4,128)S(1)}, u32[]{:S(2)}, u32[]{:S(2)}) collective-permute-start(f32[3,384]{1,0:T(4,128)S(1)} %bitcast.175), channel_id=1, source_target_pairs={{1,0},{2,1},{3,2},{4,3},{5,4},{6,5},{7,6},{8,7},{9,8},{10,9},{11,1... | collective-permute-start | bytes 13832 | tf_op jit(solution)/shard_map/ppermute | solution.py:38
  233.9 33.2 %all-reduce.27.cloned.1.call-done = f32[2,128,128]{2,1,0:T(8,128)} async-done(((f32[2,128,128]{2,1,0:T(8,128)}), f32[2,128,128]{2,1,0:T(8,128)}) %all-reduce.27.cloned.1.call-update) | async-done | bytes 131088 | tf_op jit(solution)/shard_map/psum | solution.py:42
  267.7 3.7 scatter_custom_fusion.13
  272.1 46.2 %all-reduce.29.cloned.1.call-done = f32[2,128,128]{2,1,0:T(8,128)} async-done(((f32[2,128,128]{2,1,0:T(8,128)}), f32[2,128,128]{2,1,0:T(8,128)}) %all-reduce.29.cloned.1.call-update) | async-done | bytes 131088 | tf_op jit(solution)/shard_map/psum | solution.py:42
  318.5 2.7 scatter_fusion
  321.3 100.1 %all-reduce.31.cloned.1.call-done = f32[2,128,128]{2,1,0:T(8,128)} async-done(((f32[2,128,128]{2,1,0:T(8,128)}), f32[2,128,128]{2,1,0:T(8,128)}) %all-reduce.31.cloned.1.call-update) | async-done | bytes 131088 | tf_op jit(solution)/shard_map/psum | solution.py:42
  422.1 62.6 %all-reduce.33.cloned.1.call-done = f32[2,128,128]{2,1,0:T(8,128)} async-done(((f32[2,128,128]{2,1,0:T(8,128)}), f32[2,128,128]{2,1,0:T(8,128)}) %all-reduce.33.cloned.1.call-update) | async-done | bytes 131088 | tf_op jit(solution)/shard_map/psum | solution.py:42
  (246 shorter events, 86.3 us)
Async XLA Ops:
  7.2 64.9 %copy-start = (f32[8,128]{1,0:T(8,128)S(1)}, f32[8,128]{1,0:T(8,128)}, u32[]{:S(2)}) copy-start(f32[8,128]{1,0:T(8,128)} %param.20) | copy-start | bytes 12292
  7.2 20.1 %copy-start.23 = (s32[1,1,512]{2,1,0:T(1,128)S(1)}, s32[1,1,512]{2,1,0:T(1,128)}, u32[]{:S(2)}) copy-start(s32[1,1,512]{2,1,0:T(1,128)} %param.15) | copy-start | bytes 6148
  7.2 20.8 %copy-start.42 = (s32[1,1,512]{2,1,0:T(1,128)S(1)}, s32[1,1,512]{2,1,0:T(1,128)}, u32[]{:S(2)}) copy-start(s32[1,1,512]{2,1,0:T(1,128)} %param.16) | copy-start | bytes 6148
  7.2 20.8 %copy-start.29 = (s32[1,1,4]{2,1,0:T(1,128)S(1)}, s32[1,1,4]{2,1,0:T(1,128)}, u32[]{:S(2)}) copy-start(s32[1,1,4]{2,1,0:T(1,128)} %param.17) | copy-start | bytes 52
  7.2 213.9 %all-reduce.25.cloned.1.call-start = ((), (), s32[]{:S(2)}) async-start(), calls=%async_computation | async-start | bytes 262144 | tf_op jit(solution)/shard_map/psum | solution.py:42
  8.7 26.8 %copy-start.34 = (f32[5,128]{1,0:T(8,128)S(1)}, f32[5,128]{1,0:T(8,128)}, u32[]{:S(2)}) copy-start(f32[5,128]{1,0:T(8,128)} %param.18) | copy-start | bytes 7684
  12.9 23.0 %collective-permute-start.1 = (f32[4,1,1,384]{3,0,2,1:T(4,128)S(1)}, f32[4,1,1,384]{3,0,2,1:T(4,128)S(1)}, u32[]{:S(2)}, u32[]{:S(2)}) collective-permute-start(f32[4,1,1,384]{3,0,2,1:T(4,128)S(1)} %maximum_bitcast_fusion), channel_id=1, source_target_pairs={{96,0},{192,96},{288,192},{384,288},{480,384},{576,480},{672,576},... | collective-permute-start | bytes 18440 | tf_op jit(solution)/shard_map/ppermute | solution.py:30
  25.3 10.6 %collective-permute-start = (f32[4,1,1,384]{3,0,2,1:T(4,128)S(1)}, f32[4,1,1,384]{3,0,2,1:T(4,128)S(1)}, u32[]{:S(2)}, u32[]{:S(2)}) collective-permute-start(f32[4,1,1,384]{3,0,2,1:T(4,128)S(1)} %maximum_bitcast_fusion), channel_id=1, source_target_pairs={{0,96},{96,192},{192,288},{288,384},{384,480},{480,576},{576,672},... | collective-permute-start | bytes 18440 | tf_op jit(solution)/shard_map/ppermute | solution.py:29
  27.8 78.2 %copy-start.27 = (s32[512,1]{0,1:T(1,128)}, s32[512,1]{0,1:T(1,128)S(1)}, u32[]{:S(2)}) copy-start(s32[512,1]{0,1:T(1,128)S(1)} %compare_select_fusion.1) | copy-start | bytes 6148
  28.0 25.9 %copy-start.28 = (s32[512,1]{0,1:T(1,128)}, s32[512,1]{0,1:T(1,128)S(1)}, u32[]{:S(2)}) copy-start(s32[512,1]{0,1:T(1,128)S(1)} %compare_select_fusion.2) | copy-start | bytes 6148
  31.2 56.3 %copy-start.17 = (f32[512]{0:T(512)}, f32[512]{0:T(512)S(1)}, u32[]{:S(2)}) copy-start(f32[512]{0:T(512)S(1)} %get-tuple-element.58) | copy-start | bytes 6148
  31.2 70.4 %copy-start.32 = (pred[512]{0:T(512)(128)(4,1)}, pred[512]{0:T(512)(128)(4,1)S(1)}, u32[]{:S(2)}) copy-start(pred[512]{0:T(512)(128)(4,1)S(1)} %get-tuple-element.59) | copy-start | bytes 1540
  36.0 17.9 %collective-permute-start.3 = (f32[4,3,1,384]{3,0,2,1:T(4,128)S(1)}, f32[4,3,1,384]{3,0,2,1:T(4,128)S(1)}, u32[]{:S(2)}, u32[]{:S(2)}) collective-permute-start(f32[4,3,1,384]{3,0,2,1:T(4,128)S(1)} %pad_maximum_fusion.5), channel_id=1, source_target_pairs={{1,0},{2,1},{3,2},{4,3},{5,4},{6,5},{7,6},{8,7},{9,8},{10,9},{11,1... | collective-permute-start | bytes 55304 | tf_op jit(solution)/shard_map/ppermute | solution.py:30
  49.8 12.9 %collective-permute-start.2 = (f32[4,3,1,384]{3,0,2,1:T(4,128)S(1)}, f32[4,3,1,384]{3,0,2,1:T(4,128)S(1)}, u32[]{:S(2)}, u32[]{:S(2)}) collective-permute-start(f32[4,3,1,384]{3,0,2,1:T(4,128)S(1)} %pad_maximum_fusion.5), channel_id=1, source_target_pairs={{0,1},{1,2},{2,3},{3,4},{4,5},{5,6},{6,7},{7,8},{8,9},{9,10},{10,1... | collective-permute-start | bytes 55304 | tf_op jit(solution)/shard_map/ppermute | solution.py:29
  52.3 19.8 %copy-start.43 = (f32[8]{0:T(128)}, f32[8]{0:T(128)S(1)}, u32[]{:S(2)}) copy-start(f32[8]{0:T(128)S(1)} %get-tuple-element.98) | copy-start | bytes 100
  71.0 30.6 %copy-start.15 = (f32[512]{0:T(512)}, f32[512]{0:T(512)S(1)}, u32[]{:S(2)}) copy-start(f32[512]{0:T(512)S(1)} %get-tuple-element.56) | copy-start | bytes 6148
  71.0 15.2 %copy-start.40 = (f32[512]{0:T(512)}, f32[512]{0:T(512)S(1)}, u32[]{:S(2)}) copy-start(f32[512]{0:T(512)S(1)} %get-tuple-element.80) | copy-start | bytes 6148
  72.5 13.7 %copy-start.6 = (f32[512,128]{0,1:T(8,128)}, f32[512,128]{0,1:T(8,128)S(1)}, u32[]{:S(2)}) copy-start(f32[512,128]{0,1:T(8,128)S(1)} %convolution_add_fusion.2) | copy-start | bytes 786436
  123.7 6.6 %copy-start.12 = (s32[1024]{0:T(1024)S(1)}, s32[1024]{0:T(1024)}, u32[]{:S(2)}) copy-start(s32[1024]{0:T(1024)} %pad_clamp_fusion) | copy-start | bytes 12292
  139.5 10.4 %copy-start.18 = (f32[512]{0:T(512)S(1)}, f32[512]{0:T(512)}, u32[]{:S(2)}) copy-start(f32[512]{0:T(512)} %copy-done.17) | copy-start | bytes 6148
  139.5 10.4 %copy-start.31 = (pred[512]{0:T(512)(128)(4,1)S(1)}, pred[512]{0:T(512)(128)(4,1)}, u32[]{:S(2)}) copy-start(pred[512]{0:T(512)(128)(4,1)} %and_reduce_fusion) | copy-start | bytes 1540
  162.7 9.1 %copy-start.11 = (f32[1,128,128]{2,1,0:T(8,128)S(1)}, f32[1,128,128]{2,1,0:T(8,128)}, u32[]{:S(2)}) copy-start(f32[1,128,128]{2,1,0:T(8,128)} %convolution_bitcast_fusion.1) | copy-start | bytes 196612
  163.6 154.9 %copy-start.25 = (s32[384]{0:T(512)S(1)}, s32[384]{0:T(512)}, u32[]{:S(2)}) copy-start(s32[384]{0:T(512)} %copy-done.24) | copy-start | bytes 4612
  166.4 101.2 %copy-start.2 = (f32[3,512]{0,1:T(8,128)S(1)}, f32[3,512]{0,1:T(8,128)}, u32[]{:S(2)}) copy-start(f32[3,512]{0,1:T(8,128)} %copy-done.1) | copy-start | bytes 18436
  166.4 54.0 %collective-permute-start.5 = (f32[3,3,384]{2,1,0:T(4,128)}, f32[3,3,384]{2,1,0:T(4,128)S(1)}, u32[]{:S(2)}, u32[]{:S(2)}) collective-permute-start(f32[3,3,384]{2,1,0:T(4,128)} %bitcast.149), channel_id=1, source_target_pairs={{672,0},{0,96},{96,192},{192,288},{288,384},{384,480},{480,576},{5... | collective-permute-start | bytes 41480 | tf_op jit(solution)/shard_map/ppermute | solution.py:38
  169.4 51.0 %collective-permute-start.4 = (f32[3,3,384]{2,1,0:T(4,128)}, f32[3,3,384]{2,1,0:T(4,128)S(1)}, u32[]{:S(2)}, u32[]{:S(2)}) collective-permute-start(f32[3,3,384]{2,1,0:T(4,128)} %bitcast.148), channel_id=1, source_target_pairs={{96,0},{192,96},{288,192},{384,288},{480,384},{576,480},{672,576},... | collective-permute-start | bytes 41480 | tf_op jit(solution)/shard_map/ppermute | solution.py:38
  173.3 93.8 %all-reduce.27.cloned.1.call-start = ((), (), s32[]{:S(2)}) async-start(), calls=%async_computation.1 | async-start | bytes 262144 | tf_op jit(solution)/shard_map/psum | solution.py:42
  221.1 97.1 %all-reduce.29.cloned.1.call-start = ((), (), s32[]{:S(2)}) async-start(), calls=%async_computation.2 | async-start | bytes 262144 | tf_op jit(solution)/shard_map/psum | solution.py:42
  221.2 97.1 %collective-permute-start.6 = (f32[3,384]{1,0:T(4,128)S(1)}, f32[3,384]{1,0:T(4,128)S(1)}, u32[]{:S(2)}, u32[]{:S(2)}) collective-permute-start(f32[3,384]{1,0:T(4,128)S(1)} %bitcast.175), channel_id=1, source_target_pairs={{1,0},{2,1},{3,2},{4,3},{5,4},{6,5},{7,6},{8,7},{9,8},{10,9},{11,1... | collective-permute-start | bytes 13832 | tf_op jit(solution)/shard_map/ppermute | solution.py:38
  231.9 86.4 %collective-permute-start.7 = (f32[3,384]{1,0:T(4,128)S(1)}, f32[3,384]{1,0:T(4,128)S(1)}, u32[]{:S(2)}, u32[]{:S(2)}) collective-permute-start(f32[3,384]{1,0:T(4,128)S(1)} %bitcast.174), channel_id=1, source_target_pairs={{95,0},{0,1},{1,2},{2,3},{3,4},{4,5},{5,6},{6,7},{7,8},{8,9},{9,10... | collective-permute-start | bytes 13832 | tf_op jit(solution)/shard_map/ppermute | solution.py:38
  267.1 154.3 %all-reduce.31.cloned.1.call-start = ((), (), s32[]{:S(2)}) async-start(), calls=%async_computation.3 | async-start | bytes 262144 | tf_op jit(solution)/shard_map/psum | solution.py:42
  318.3 166.5 %all-reduce.33.cloned.1.call-start = ((), (), s32[]{:S(2)}) async-start(), calls=%async_computation.4 | async-start | bytes 262144 | tf_op jit(solution)/shard_map/psum | solution.py:42
  (30 other events, 80.6 us)
Sparse Core Ops, SparseCore 0:
  173.4 47.6 all-reduce.24
  224.3 42.7 all-reduce.26
  270.2 48.0 all-reduce.28
  320.5 100.8 all-reduce.30
  423.5 61.1 all-reduce.32
where the time goes:
time: 503 us; the launch traced here: 494 us
  waiting for transfers between devices  252 us (50%)
  other arithmetic  61.8 us (12%)
  local copies, waits for them, and re-layouts  50.1 us (10%)
  starting transfers between devices  48.2 us (10%)
  blocking collectives  46.8 us (9%)
  matrix products  18.3 us (4%)
  between operations  17.4 us (3%)
    psum x5, waiting for transfers between devices, over_axes(): return functools.reduce(lax.psum, axes, shard)  243 us
    psum x5, blocking collectives, over_axes(): return functools.reduce(lax.psum, axes, shard)  46.8 us
    ppermute x2, starting transfers between devices, extended(): after = lax.ppermute(leading, axis, down)  26.2 us
    ppermute x4, starting transfers between devices, passed_along(): return lax.ppermute(block, axis, route)  17.9 us
    scatter-add x6, other arithmetic, device_energy(): back = back + environ[centers] * unit_vec[comp][:, None]  17.5 us
    scatter-add x6, other arithmetic, device_energy(): jax.ops.segment_sum(weighted * unit_vec[comp][:, None], centers, num_segm...  16.5 us
    gather x12, local copies, waits for them, and re-layouts, device_energy(): jax.ops.segment_sum(weighted * unit_vec[comp][:, None], centers, num_segm...  13.6 us
  transfers between devices with their start and end apart: 13, of which 6 were waited for; matrix products, arithmetic and copies ran while one was open for 4% of the time, Pallas kernels for 0%

commit v1 on v0

v1 whole, which is shorter than its diff:
```python
import math

import jax
import jax.numpy as jnp
from jax import lax
from jax.experimental import pallas as pl
from jax.experimental.pallas import tpu as pltpu
from jax.sharding import Mesh
from jax.sharding import PartitionSpec as P

BLOCK_EDGES = 128
LAT = 8
CUTOFF = 6.0
SOFTENING = 0.25
SPACING = 1.7
LANES = 128

GX = ("gx_0", "gx_1")
GY = ("gy_0", "gy_1", "gy_2")
ALL = GX + GY
NEAR = ("gx_1", "gy_2")
MIDDLE = ("gx_0", "gy_0")
FAR = ("gy_1",)

F32 = jnp.float32
BF16 = jnp.bfloat16
NN = ((1,), (0,))
NT = ((1,), (1,))
TN = ((0,), (0,))


def iota(shape, dim):
    return lax.broadcasted_iota(jnp.int32, shape, dim)


def bdot(a, b, dims):
    return lax.dot_general(a, b, (dims, ((), ())), preferred_element_type=F32)


def split2(x):
    hi = x.astype(BF16)
    return hi, (x - hi.astype(F32)).astype(BF16)


def split3(x):
    hi = x.astype(BF16).astype(F32)
    rest = x - hi
    mid = rest.astype(BF16).astype(F32)
    return hi, mid, rest - mid


def mm(a, b, dims):
    return bdot(a[0], b[0], dims) + (bdot(a[0], b[1], dims) + bdot(a[1], b[0], dims))


def mm6(a, b, dims):
    small = bdot(a[0], b[2], dims) + bdot(a[1], b[1], dims) + bdot(a[2], b[0], dims)
    return bdot(a[0], b[0], dims) + (bdot(a[0], b[1], dims) + bdot(a[1], b[0], dims) + small)


def thirds(x):
    return tuple(part.astype(BF16) for part in split3(x))


def sigmoid(x):
    return 1.0 / (1.0 + jnp.exp(-x))


def export_kernel(pos_ref, spec_ref, send_ref, out_ref):
    atoms, count = pos_ref.shape[3], send_ref.shape[2]
    rows = [pos_ref[c, 0] for c in range(3)] + [spec_ref[0].astype(F32)]
    table = jnp.concatenate(rows, axis=0)
    parts = jnp.concatenate(split3(table) + (jnp.zeros_like(table),), axis=0).astype(BF16)
    hot = (iota((atoms, count), 0) == send_ref[0]).astype(F32).astype(BF16)
    found = bdot(parts, hot, NN)
    found = (found[0:4] + found[4:8]) + found[8:12]
    out_ref[...] = jnp.zeros_like(out_ref)
    for j in range(count // LANES):
        for c in range(4):
            out_ref[j : j + 1, c * LANES : (c + 1) * LANES] = found[c : c + 1, j * LANES : (j + 1) * LANES]


def main_kernel(
    counts_ref,
    pos_ref,
    spec_ref,
    x0_ref,
    x2_ref,
    y0_ref,
    y2_ref,
    cent_ref,
    neigh_ref,
    embc_ref,
    embn_ref,
    radw_ref,
    envw_ref,
    mixw_ref,
    outw_ref,
    own_ref,
    a0_ref,
    a1_ref,
    a2_ref,
    pack_ref,
    q_ref,
    w_ref,
    *,
    blocks,
    devices,
):
    atoms = pos_ref.shape[3]
    edges = cent_ref.shape[2]
    own_rows = atoms // LANES
    side = SPACING * LAT

    for c in range(4):
        row = pos_ref[c, 0] if c < 3 else spec_ref[0].astype(F32)
        for h in range(own_rows):
            q_ref[h : h + 1, c * LANES : (c + 1) * LANES] = row[:, h * LANES : (h + 1) * LANES]
    lane = iota((4, 4 * LANES), 1)
    for s in range(9):
        a, b = s // 3, s % 3
        rows = slice(own_rows + 4 * s, own_rows + 4 * s + 4)
        if s == 4:
            q_ref[rows, :] = jnp.zeros((4, 4 * LANES), F32)
            continue
        ghost = (y0_ref[a], None, y2_ref[a])[b] if b != 1 else (x0_ref, x2_ref)[a // 2][...]
        shift = jnp.where(lane < LANES, F32((a - 1) * side), jnp.where(lane < 2 * LANES, F32((b - 1) * side), 0.0))
        q_ref[rows, :] = ghost + shift
    total_rows = q_ref.shape[0]

    ends = jnp.concatenate([neigh_ref[0], cent_ref[0]], axis=1)
    at_row = iota((total_rows, 2 * edges), 0)
    past = at_row - own_rows
    holds = jnp.where(past < 0, at_row, jnp.where(past % 4 == 3, -1, own_rows + 3 * (past // 4) + past % 4))
    hot = (holds == ends // LANES).astype(F32)
    in_lane = iota((LANES, 2 * edges), 0) == ends % LANES
    table = jnp.concatenate(split3(q_ref[...]), axis=0).astype(BF16)
    hot3 = jnp.concatenate([hot, hot, hot], axis=0).astype(BF16)
    runs = bdot(table, hot3, TN)
    picked = [
        jnp.sum(jnp.where(in_lane, runs[c * LANES : (c + 1) * LANES], 0.0), axis=0, keepdims=True) for c in range(4)
    ]

    dist = [p[:, :edges] - p[:, edges:] for p in picked[:3]]
    radius = jnp.sqrt((dist[0] * dist[0] + dist[1] * dist[1] + dist[2] * dist[2]) + SOFTENING)
    inverse = 1.0 / radius
    unit = [d * inverse for d in dist]
    ratio = radius * (1.0 / CUTOFF)
    gap = 1.0 - ratio * ratio
    smooth = gap * gap
    edge = iota((1, edges), 1)
    limit = jnp.full((1, edges), counts_ref[0, 0, 0], jnp.int32)
    for k in range(1, blocks):
        limit = jnp.where(edge >= k * BLOCK_EDGES, counts_ref[0, 0, k], limit)
    live = (edge % BLOCK_EDGES < limit).astype(F32)
    order = (iota((8, edges), 0) + 1).astype(F32) * F32(math.pi / CUTOFF)
    angle = order * radius
    sines, cosines = jnp.sin(angle), jnp.cos(angle)
    basis = sines * inverse
    slope = (order * cosines - basis) * inverse
    kind = iota((8, edges), 0).astype(F32)
    features = jnp.concatenate(
        [
            basis,
            (kind == picked[3][:, edges:]).astype(F32),
            (kind == picked[3][:, :edges]).astype(F32),
        ],
        axis=0,
    )
    species = embc_ref.shape[0]
    w_ref[...] = jnp.zeros_like(w_ref)
    w_ref[0:8, :] = radw_ref[...]
    w_ref[8 : 8 + species, :] = embc_ref[...]
    w_ref[16 : 16 + species, :] = embn_ref[...]

    centre = cent_ref[0].astype(F32)
    weight = live * smooth
    zero = jnp.zeros((1, edges), F32)
    columns = jnp.transpose(jnp.concatenate([smooth, weight, live, centre] + [zero] * 4, axis=0))
    smooth_col, weight_col, live_col, centre_col = (columns[:, k : k + 1] for k in range(4))

    units = jnp.concatenate(unit + [zero] * 5, axis=0)
    units_s = split2(units)
    cosine = mm(units_s, units_s, TN)
    same = jnp.logical_and(centre_col == centre, live_col * live > 0.0)
    pairs = split2(jnp.where(same, cosine, 0.0))

    summed = mm6(thirds(features), thirds(w_ref[...]), TN)
    gate0 = sigmoid(summed)
    first = summed * gate0
    latent = first * smooth_col

    layers = envw_ref.shape[0]
    share = 1.0 / devices
    saved = []
    for l in range(layers):
        env_s, mix_s = split2(envw_ref[l]), split2(mixw_ref[l])
        weighted_s = split2(mm(split2(latent), env_s, NN))
        back = mm(pairs, weighted_s, NN)
        coupled_s = split2(latent * back)
        pre = mm(coupled_s, mix_s, NN)
        gate = sigmoid(pre)
        saved.append((env_s, mix_s, weighted_s, latent, back, coupled_s, pre, gate))
        latent = latent + pre * gate

    out_rows = jnp.broadcast_to(outw_ref[...], (8, LANES))
    latent_s = split2(latent)
    readout = mm6(thirds(out_rows), thirds(latent), NT)[0:1]
    energy = jnp.sum(weight * readout, axis=1, keepdims=True)
    grad_out = mm(split2(jnp.concatenate([weight] + [zero] * 7, axis=0)), latent_s, NN)

    dlatent = weight_col * outw_ref[...]
    dpairs = None
    for l in reversed(range(layers)):
        env_s, mix_s, weighted_s, latent, back, coupled_s, pre, gate = saved[l]
        dpre_s = split2(dlatent * (gate * (1.0 + pre * (1.0 - gate))))
        pack_ref[l * LANES : (l + 1) * LANES, :] = mm(coupled_s, dpre_s, TN) * share
        dcoupled = mm(dpre_s, mix_s, NT)
        dback_s = split2(dcoupled * latent)
        term = mm(dback_s, weighted_s, NT)
        dpairs = term if dpairs is None else dpairs + term
        dweighted_s = split2(mm(pairs, dback_s, NN))
        dlatent = dlatent + dcoupled * back + mm(dweighted_s, env_s, NT)
    rest = pack_ref.shape[0] - layers * LANES
    row = iota((rest, LANES), 0)
    tail = jnp.where(row == 0, grad_out[0:1], jnp.where(row == 1, energy, 0.0))
    pack_ref[layers * LANES :, :] = tail * share

    dpairs_s = split2(jnp.where(same, dpairs, 0.0))
    dunits = mm(units_s, dpairs_s, NT) + mm(units_s, dpairs_s, NN)
    dfirst = dlatent * first
    dsmooth = live * readout + mm(split2(jnp.ones((8, LANES), F32)), split2(dfirst), NT)[0:1]
    dsummed = dlatent * smooth_col * (gate0 * (1.0 + summed * (1.0 - gate0)))
    dbasis = mm(split2(w_ref[0:8, :]), split2(dsummed), NT)
    dradius = jnp.sum(dbasis * slope, axis=0, keepdims=True) - dsmooth * (gap * radius * F32(4.0 / CUTOFF**2))
    along = dunits[0:1] * unit[0] + dunits[1:2] * unit[1] + dunits[2:3] * unit[2]
    radial = dradius - along * inverse
    moves = []
    for c in range(3):
        push = dunits[c : c + 1] * inverse + unit[c] * radial
        moves.append(jnp.where(in_lane, jnp.concatenate([push, -push], axis=1), 0.0))
    moves = split3(jnp.concatenate(moves, axis=0))
    hot_b = hot.astype(BF16)
    pool = (bdot(hot_b, moves[0].astype(BF16), NT) + bdot(hot_b, moves[1].astype(BF16), NT)) + bdot(
        hot_b, moves[2].astype(BF16), NT
    )
    own_ref[...] = pool[0:own_rows]
    for s in range(9):
        rows = slice(own_rows + 4 * s, own_rows + 4 * s + 4)
        (a0_ref, a1_ref, a2_ref)[s // 3][s % 3] = pool[rows]


def force_kernel(send_ref, own_ref, down_ref, up_ref, left_ref, right_ref, out_ref):
    atoms, count = out_ref.shape[3], send_ref.shape[2]
    back = (down_ref[1] + up_ref[1]) + (left_ref[...] + right_ref[...])
    rows = []
    for c in range(3):
        lanes = slice(c * LANES, (c + 1) * LANES)
        rows.append(jnp.concatenate([back[j : j + 1, lanes] for j in range(count // LANES)], axis=1))
    rows.append(jnp.zeros((1, count), F32))
    values = jnp.concatenate(rows, axis=0)
    parts = jnp.concatenate(split3(values) + (jnp.zeros_like(values),), axis=0).astype(BF16)
    hot = (iota((atoms, count), 0) == send_ref[0]).astype(F32).astype(BF16)
    placed = bdot(parts, hot, NT)
    placed = (placed[0:4] + placed[4:8]) + placed[8:12]
    own = own_ref[...]
    for c in range(3):
        lanes = slice(c * LANES, (c + 1) * LANES)
        mine = jnp.concatenate([own[h : h + 1, lanes] for h in range(atoms // LANES)], axis=1)
        out_ref[c, 0] = -(mine + placed[c : c + 1])


def passed_along(block, axis, distance):
    count = lax.axis_size(axis)
    route = [((i - distance) % count, i) for i in range(count)]
    return lax.ppermute(block, axis, route)


def exchanged(shard, axes):
    return lax.all_to_all(shard, axes, 0, 0)


def summed_over(shard, axes):
    copies = jnp.broadcast_to(shard[None], (lax.axis_size(axes),) + shard.shape)
    return jnp.sum(exchanged(copies, axes), axis=0)


def summed_over_all(pack):
    near = lax.axis_size(NEAR)
    rows = pack.shape[0] // near
    part = jnp.sum(exchanged(pack.reshape(near, rows, LANES), NEAR), axis=0)
    part = summed_over(summed_over(part, MIDDLE), FAR)
    copies = jnp.broadcast_to(part[None], (near, rows, LANES))
    return exchanged(copies, NEAR).reshape(near * rows, LANES)


def body(
    positions,
    species,
    send_index,
    edge_centers,
    edge_neighbours,
    block_counts,
    emb_center,
    emb_neighbour,
    radial_w,
    env_w,
    mix_w,
    out_w,
):
    atoms = positions.shape[3]
    edges = edge_centers.shape[2]
    layers = env_w.shape[0]
    own_rows = atoms // LANES
    devices = lax.axis_size(ALL)
    tiles = 8 * lax.axis_size(NEAR)
    packed = (layers * LANES + 2 + tiles - 1) // tiles * tiles
    vmem = pl.BlockSpec(memory_space=pltpu.VMEM)

    exported = pl.pallas_call(
        export_kernel,
        out_shape=jax.ShapeDtypeStruct((4, 4 * LANES), F32),
        in_specs=[vmem] * 3,
        out_specs=vmem,
        name="export",
    )(positions, species, send_index)

    x0 = passed_along(exported, GX, 1)
    x2 = passed_along(exported, GX, -1)
    column = jnp.stack([x0, exported, x2])
    y0 = passed_along(column, GY, 1)
    y2 = passed_along(column, GY, -1)

    piece = jax.ShapeDtypeStruct((3, 4, 3 * LANES), F32)
    own, a0, a1, a2, pack = pl.pallas_call(
        lambda *refs: main_kernel(*refs, blocks=edges // BLOCK_EDGES, devices=devices),
        out_shape=(
            jax.ShapeDtypeStruct((own_rows, 3 * LANES), F32),
            piece,
            piece,
            piece,
            jax.ShapeDtypeStruct((packed, LANES), F32),
        ),
        in_specs=[pl.BlockSpec(memory_space=pltpu.SMEM)] + [vmem] * 14,
        out_specs=(vmem,) * 5,
        scratch_shapes=[
            pltpu.VMEM((own_rows + 36, 4 * LANES), F32),
            pltpu.VMEM((24, LANES), F32),
        ],
        name="edges",
    )(
        block_counts,
        positions,
        species,
        x0,
        x2,
        y0,
        y2,
        edge_centers,
        edge_neighbours,
        emb_center,
        emb_neighbour,
        radial_w,
        env_w,
        mix_w,
        out_w.reshape(1, LANES),
    )

    down = passed_along(a0, GX, -1)
    up = passed_along(a2, GX, 1)
    left = passed_along(a1[0] + down[0] + up[0], GY, -1)
    right = passed_along(a1[2] + down[2] + up[2], GY, 1)
    forces = pl.pallas_call(
        force_kernel,
        out_shape=jax.ShapeDtypeStruct(positions.shape, F32),
        in_specs=[vmem] * 6,
        out_specs=vmem,
        name="forces",
    )(send_index, own, down, up, left, right)

    total = summed_over_all(pack)
    top = layers * LANES
    return forces, total[:top].reshape(layers, LANES, LANES), total[top], total[top + 1, 0]


def solution(mesh):
    finer = Mesh(mesh.devices.reshape(4, 2, 2, 12, 4), ALL)
    sharded = P(GX, GY, None)
    placed = (P(None, GX, GY, None),) + (sharded,) * 5 + (P(),) * 6
    return jax.shard_map(
        body,
        mesh=finer,
        in_specs=placed,
        out_specs=(P(None, GX, GY, None), P(), P(), P()),
        check_vma=False,
    )
```

time: 503 us -> 129 us (0.26)
  the two profiles are of different devices: /device:TPU:1 before, /device:TPU:8 now
where the time goes in v1:
time: 129 us; the launch traced here: 128 us
  starting transfers between devices  45.8 us (36%)
  waiting for transfers between devices  36.3 us (28%)
  blocking collectives  24.1 us (19%)
  Pallas kernels  15 us (12%)
  local copies, waits for them, and re-layouts  4.89 us (4%)
    ppermute x8, starting transfers between devices, passed_along(): return lax.ppermute(block, axis, route)  38.6 us
    all_to_all x2, blocking collectives, exchanged(): return lax.all_to_all(shard, axes, 0, 0)  24.1 us
    ppermute x8, waiting for transfers between devices, passed_along(): return lax.ppermute(block, axis, route)  23.8 us
    all_to_all x2, waiting for transfers between devices, exchanged(): return lax.all_to_all(shard, axes, 0, 0)  12.5 us
    pallas_call x1, Pallas kernels, body(): pl.pallas_call(lambda *refs: main_kernel(*refs, blocks=edges // BLOCK_EDG...  11.9 us
    all_to_all x2, starting transfers between devices, exchanged(): return lax.all_to_all(shard, axes, 0, 0)  7.18 us
  transfers between devices with their start and end apart: 10, of which 4 were waited for; matrix products, arithmetic and copies ran while one was open for 1% of the time, Pallas kernels for 1%

profile of v1, /device:TPU:8, one launch (start us, length us, event | category | flops | bytes accessed | tf_op | source)
XLA Modules:
  0.0 127.7 jit_solution(16543243721726375340)
XLA Ops:
  0.6 1.5 %export.1 = f32[4,512]{1,0:T(4,128)} custom-call(f32[3,1,1,512]{3,2,1,0:T(1,128)} %refs_1_.1, s32[1,1,512]{2,1,0:T(1,128)} %refs_2_.1, s32[1,1,384]{2,1,0:T(1,128)} %send_ref.3), custom_call_target="tpu_custom_call" | custom-call | tf_op jit(solution)/shard_map/export/pallas_call | solution.py:320
  2.1 1.9 %collective-permute-start.1 = (f32[4,512]{1,0:T(4,128)}, f32[4,512]{1,0:T(4,128)S(1)}, u32[]{:S(2)}, u32[]{:S(2)}) collective-permute-start(f32[4,512]{1,0:T(4,128)} %export.1), channel_id=1, source_target_pairs={{96,0},{192,96},{288,192},{384,288},{480,384},{576,480},{672,576},... | collective-permute-start | bytes 24584 | tf_op jit(solution)/shard_map/ppermute | solution.py:276
  4.1 2.4 %collective-permute-start = (f32[4,512]{1,0:T(4,128)}, f32[4,512]{1,0:T(4,128)S(1)}, u32[]{:S(2)}, u32[]{:S(2)}) collective-permute-start(f32[4,512]{1,0:T(4,128)} %export.1), channel_id=1, source_target_pairs={{672,0},{0,96},{96,192},{192,288},{288,384},{384,480},{480,576},{5... | collective-permute-start | bytes 24584 | tf_op jit(solution)/shard_map/ppermute | solution.py:276
  6.5 0.0 collective-permute-done.1.refs_4_
  6.5 10.5 %collective-permute-done.refs_3_ = f32[4,512]{1,0:T(4,128)S(1)} collective-permute-done((f32[4,512]{1,0:T(4,128)}, f32[4,512]{1,0:T(4,128)S(1)}, u32[]{:S(2)}, u32[]{:S(2)}) %collective-permute-start) | collective-permute-done | bytes 8224 | tf_op jit(solution)/shard_map/ppermute | solution.py:276
  17.0 0.7 pad_maximum_fusion
  17.8 14.1 %collective-permute-start.3 = (f32[3,4,512]{2,1,0:T(4,128)S(1)}, f32[3,4,512]{2,1,0:T(4,128)S(1)}, u32[]{:S(2)}, u32[]{:S(2)}) collective-permute-start(f32[3,4,512]{2,1,0:T(4,128)S(1)} %pad_maximum_fusion), channel_id=1, source_target_pairs={{1,0},{2,1},{3,2},{4,3},{5,4},{6,5},{7,6},{8,7},{9,8},{10,9},{11,1... | collective-permute-start | bytes 73736 | tf_op jit(solution)/shard_map/ppermute | solution.py:276
  31.9 1.9 %collective-permute-start.2 = (f32[3,4,512]{2,1,0:T(4,128)S(1)}, f32[3,4,512]{2,1,0:T(4,128)S(1)}, u32[]{:S(2)}, u32[]{:S(2)}) collective-permute-start(f32[3,4,512]{2,1,0:T(4,128)S(1)} %pad_maximum_fusion), channel_id=1, source_target_pairs={{95,0},{0,1},{1,2},{2,3},{3,4},{4,5},{5,6},{6,7},{7,8},{8,9},{9,10... | collective-permute-start | bytes 73736 | tf_op jit(solution)/shard_map/ppermute | solution.py:276
  33.8 0.0 collective-permute-done.3.refs_6_
  33.8 11.9 %collective-permute-done.2.refs_5_ = f32[3,4,512]{2,1,0:T(4,128)S(1)} collective-permute-done((f32[3,4,512]{2,1,0:T(4,128)S(1)}, f32[3,4,512]{2,1,0:T(4,128)S(1)}, u32[]{:S(2)}, u32[]{:S(2)}) %collective-permute-start.2) | collective-permute-done | bytes 24608 | tf_op jit(solution)/shard_map/ppermute | solution.py:276
  45.8 0.6 copy-done.5
  46.4 11.9 %edges.1 = (f32[4,384]{1,0:T(4,128)}, f32[3,4,384]{2,1,0:T(4,128)}, f32[3,4,384]{2,1,0:T(4,128)}, f32[3,4,384]{2,1,0:T(4,128)}, f32[320,128]{1,0:T(8,128)}) custom-call(s32[1,1,4]{2,1,0:T(1,128)} %refs_0_.1, f32[3,1,1,512]{3,2,1,0:T(1,128)} %refs_1_.1, s32[1,1,512]{2,1,0:T(1,128)} %refs_2_.1, f32[4,512]{1,0:T(4,128)} %copy-done.3, f32[4,512]{1,0:T(4,128)} %copy-done.2, ...), custom_call_target="tpu_custom_call" | custom-call | tf_op jit(solution)/shard_map/edges/pallas_call | solution.py:335
  58.2 9.0 %all_to_all.20 = f32[8,40,128]{2,1,0:T(8,128)S(1)} all-to-all(f32[8,40,128]{2,1,0:T(8,128)} %bitcast.17), channel_id=1, replica_groups=mesh['gx_0'=4,'gx_1'=2,'gy_0'=2,'gy_1'=12,'gy_2'=4] {'gx_1','gy_2'}, dimensions={0} | all-to-all | bytes 327680 | tf_op jit(solution)/shard_map/all_to_all | solution.py:280
  67.3 15.1 %all_to_all.21 = f32[8,40,128]{2,1,0:T(8,128)S(1)} all-to-all(f32[8,40,128]{2,1,0:T(8,128)S(1)} %broadcast_in_dim.6), channel_id=1, replica_groups=mesh['gx_0'=4,'gx_1'=2,'gy_0'=2,'gy_1'=12,'gy_2'=4] {'gx_0','gy_0'}, dimensions={0} | all-to-all | bytes 327680 | tf_op jit(solution)/shard_map/all_to_all | solution.py:280
  82.4 0.7 broadcast_in_dim.7
  83.1 3.7 %all-to-all-start.2 = ((f32[12,40,128]{2,1,0:T(8,128)}), f32[12,40,128]{2,1,0:T(8,128)S(1)}, u32[]{:S(2)}, u32[]{:S(2)}) async-start(f32[12,40,128]{2,1,0:T(8,128)} %broadcast_in_dim.7), calls=%async_computation.2 | async-start | bytes 491520 | tf_op jit(solution)/shard_map/all_to_all | solution.py:280
  86.8 1.9 %collective-permute-start.4 = (f32[3,4,384]{2,1,0:T(4,128)S(1)}, f32[3,4,384]{2,1,0:T(4,128)S(1)}, u32[]{:S(2)}, u32[]{:S(2)}) collective-permute-start(f32[3,4,384]{2,1,0:T(4,128)S(1)} %copy-done.10), channel_id=1, source_target_pairs={{96,0},{192,96},{288,192},{384,288},{480,384},{576,480},{672,576},... | collective-permute-start | bytes 55304 | tf_op jit(solution)/shard_map/ppermute | solution.py:276
  88.7 2.4 %collective-permute-start.5 = (f32[3,4,384]{2,1,0:T(4,128)S(1)}, f32[3,4,384]{2,1,0:T(4,128)S(1)}, u32[]{:S(2)}, u32[]{:S(2)}) collective-permute-start(f32[3,4,384]{2,1,0:T(4,128)S(1)} %copy-done.9), channel_id=1, source_target_pairs={{672,0},{0,96},{96,192},{192,288},{288,384},{384,480},{480,576},{5... | collective-permute-start | bytes 55304 | tf_op jit(solution)/shard_map/ppermute | solution.py:276
  91.1 12.5 %all-to-all-done.2 = f32[12,40,128]{2,1,0:T(8,128)S(1)} async-done(((f32[12,40,128]{2,1,0:T(8,128)}), f32[12,40,128]{2,1,0:T(8,128)S(1)}, u32[]{:S(2)}, u32[]{:S(2)}) %all-to-all-start.2) | async-done | bytes 245792 | tf_op jit(solution)/shard_map/all_to_all | solution.py:280
  103.6 0.7 broadcast_in_dim.8
  104.3 3.5 %all-to-all-start.3 = ((f32[8,40,128]{2,1,0:T(8,128)}), f32[8,40,128]{2,1,0:T(8,128)S(1)}, u32[]{:S(2)}, u32[]{:S(2)}) async-start(f32[8,40,128]{2,1,0:T(8,128)} %broadcast_in_dim.8), calls=%async_computation.3 | async-start | bytes 327680 | tf_op jit(solution)/shard_map/all_to_all | solution.py:280
  107.8 0.0 copy-start
  107.9 0.6 copy-done
  108.4 0.0 copy-done.1
  108.5 3.8 %collective-permute-start.7 = (f32[4,384]{1,0:T(4,128)S(1)}, f32[4,384]{1,0:T(4,128)S(1)}, u32[]{:S(2)}, u32[]{:S(2)}) collective-permute-start(f32[4,384]{1,0:T(4,128)S(1)} %get-tuple-element.14), channel_id=1, source_target_pairs={{95,0},{0,1},{1,2},{2,3},{3,4},{4,5},{5,6},{6,7},{7,8},{8,9},{9,10... | collective-permute-start | bytes 18440 | tf_op jit(solution)/shard_map/ppermute | solution.py:276
  112.3 10.2 %collective-permute-start.6 = (f32[4,384]{1,0:T(4,128)S(1)}, f32[4,384]{1,0:T(4,128)S(1)}, u32[]{:S(2)}, u32[]{:S(2)}) collective-permute-start(f32[4,384]{1,0:T(4,128)S(1)} %get-tuple-element.15), channel_id=1, source_target_pairs={{1,0},{2,1},{3,2},{4,3},{5,4},{6,5},{7,6},{8,7},{9,8},{10,9},{11,1... | collective-permute-start | bytes 18440 | tf_op jit(solution)/shard_map/ppermute | solution.py:276
  122.4 1.3 %collective-permute-done.6.left_ref = f32[4,384]{1,0:T(4,128)S(1)} collective-permute-done((f32[4,384]{1,0:T(4,128)S(1)}, f32[4,384]{1,0:T(4,128)S(1)}, u32[]{:S(2)}, u32[]{:S(2)}) %collective-permute-start.6) | collective-permute-done | bytes 6176 | tf_op jit(solution)/shard_map/ppermute | solution.py:276
  123.8 0.6 copy-done.8
  124.3 1.6 %forces.1 = f32[3,1,1,512]{3,2,1,0:T(1,128)} custom-call(s32[1,1,384]{2,1,0:T(1,128)} %send_ref.3, f32[4,384]{1,0:T(4,128)} %get-tuple-element.9.own_ref, f32[3,4,384]{2,1,0:T(4,128)} %copy-done, f32[3,4,384]{2,1,0:T(4,128)} %copy-done.1, f32[4,384]{1,0:T(4,128)} %copy-done.8, f32[4,384]{1,0:T(4,128)} %copy-done.7), custom_call_target="tpu_custom_call" | custom-call | tf_op jit(solution)/shard_map/forces/pallas_call | solution.py:373
  126.0 0.5 slice.42
  126.5 0.5 slice_bitcast_fusion
  127.0 0.7 slice.40
  (26 shorter events, 0.1 us)
Async XLA Ops:
  2.1 4.3 %collective-permute-start.1 = (f32[4,512]{1,0:T(4,128)}, f32[4,512]{1,0:T(4,128)S(1)}, u32[]{:S(2)}, u32[]{:S(2)}) collective-permute-start(f32[4,512]{1,0:T(4,128)} %export.1), channel_id=1, source_target_pairs={{96,0},{192,96},{288,192},{384,288},{480,384},{576,480},{672,576},... | collective-permute-start | bytes 24584 | tf_op jit(solution)/shard_map/ppermute | solution.py:276
  4.1 13.0 %collective-permute-start = (f32[4,512]{1,0:T(4,128)}, f32[4,512]{1,0:T(4,128)S(1)}, u32[]{:S(2)}, u32[]{:S(2)}) collective-permute-start(f32[4,512]{1,0:T(4,128)} %export.1), channel_id=1, source_target_pairs={{672,0},{0,96},{96,192},{192,288},{288,384},{384,480},{480,576},{5... | collective-permute-start | bytes 24584 | tf_op jit(solution)/shard_map/ppermute | solution.py:276
  6.5 11.3 %copy-start.2 = (f32[4,512]{1,0:T(4,128)}, f32[4,512]{1,0:T(4,128)S(1)}, u32[]{:S(2)}) copy-start(f32[4,512]{1,0:T(4,128)S(1)} %collective-permute-done.1.refs_4_) | copy-start | bytes 24580
  17.0 0.7 copy-start.3
  17.8 16.1 %collective-permute-start.3 = (f32[3,4,512]{2,1,0:T(4,128)S(1)}, f32[3,4,512]{2,1,0:T(4,128)S(1)}, u32[]{:S(2)}, u32[]{:S(2)}) collective-permute-start(f32[3,4,512]{2,1,0:T(4,128)S(1)} %pad_maximum_fusion), channel_id=1, source_target_pairs={{1,0},{2,1},{3,2},{4,3},{5,4},{6,5},{7,6},{8,7},{9,8},{10,9},{11,1... | collective-permute-start | bytes 73736 | tf_op jit(solution)/shard_map/ppermute | solution.py:276
  31.9 13.9 %collective-permute-start.2 = (f32[3,4,512]{2,1,0:T(4,128)S(1)}, f32[3,4,512]{2,1,0:T(4,128)S(1)}, u32[]{:S(2)}, u32[]{:S(2)}) collective-permute-start(f32[3,4,512]{2,1,0:T(4,128)S(1)} %pad_maximum_fusion), channel_id=1, source_target_pairs={{95,0},{0,1},{1,2},{2,3},{3,4},{4,5},{5,6},{6,7},{7,8},{8,9},{9,10... | collective-permute-start | bytes 73736 | tf_op jit(solution)/shard_map/ppermute | solution.py:276
  33.8 11.9 %copy-start.4 = (f32[3,4,512]{2,1,0:T(4,128)}, f32[3,4,512]{2,1,0:T(4,128)S(1)}, u32[]{:S(2)}) copy-start(f32[3,4,512]{2,1,0:T(4,128)S(1)} %collective-permute-done.3.refs_6_) | copy-start | bytes 73732
  45.8 0.6 copy-start.5
  83.1 3.7 %copy-start.10 = (f32[3,4,384]{2,1,0:T(4,128)S(1)}, f32[3,4,384]{2,1,0:T(4,128)}, u32[]{:S(2)}) copy-start(f32[3,4,384]{2,1,0:T(4,128)} %get-tuple-element.10) | copy-start | bytes 55300
  83.1 5.6 %copy-start.9 = (f32[3,4,384]{2,1,0:T(4,128)S(1)}, f32[3,4,384]{2,1,0:T(4,128)}, u32[]{:S(2)}) copy-start(f32[3,4,384]{2,1,0:T(4,128)} %get-tuple-element.11) | copy-start | bytes 55300
  83.1 20.5 %all-to-all-start.2 = ((f32[12,40,128]{2,1,0:T(8,128)}), f32[12,40,128]{2,1,0:T(8,128)S(1)}, u32[]{:S(2)}, u32[]{:S(2)}) async-start(f32[12,40,128]{2,1,0:T(8,128)} %broadcast_in_dim.7), calls=%async_computation.2 | async-start | bytes 491520 | tf_op jit(solution)/shard_map/all_to_all | solution.py:280
  86.8 21.1 %collective-permute-start.4 = (f32[3,4,384]{2,1,0:T(4,128)S(1)}, f32[3,4,384]{2,1,0:T(4,128)S(1)}, u32[]{:S(2)}, u32[]{:S(2)}) collective-permute-start(f32[3,4,384]{2,1,0:T(4,128)S(1)} %copy-done.10), channel_id=1, source_target_pairs={{96,0},{192,96},{288,192},{384,288},{480,384},{576,480},{672,576},... | collective-permute-start | bytes 55304 | tf_op jit(solution)/shard_map/ppermute | solution.py:276
  88.7 19.1 %collective-permute-start.5 = (f32[3,4,384]{2,1,0:T(4,128)S(1)}, f32[3,4,384]{2,1,0:T(4,128)S(1)}, u32[]{:S(2)}, u32[]{:S(2)}) collective-permute-start(f32[3,4,384]{2,1,0:T(4,128)S(1)} %copy-done.9), channel_id=1, source_target_pairs={{672,0},{0,96},{96,192},{192,288},{288,384},{384,480},{480,576},{5... | collective-permute-start | bytes 55304 | tf_op jit(solution)/shard_map/ppermute | solution.py:276
  104.3 3.6 %copy-start.6 = (f32[3,4,384]{2,1,0:T(4,128)S(1)}, f32[3,4,384]{2,1,0:T(4,128)}, u32[]{:S(2)}) copy-start(f32[3,4,384]{2,1,0:T(4,128)} %get-tuple-element.12) | copy-start | bytes 55300
  104.3 21.7 %all-to-all-start.3 = ((f32[8,40,128]{2,1,0:T(8,128)}), f32[8,40,128]{2,1,0:T(8,128)S(1)}, u32[]{:S(2)}, u32[]{:S(2)}) async-start(f32[8,40,128]{2,1,0:T(8,128)} %broadcast_in_dim.8), calls=%async_computation.3 | async-start | bytes 327680 | tf_op jit(solution)/shard_map/all_to_all | solution.py:280
  107.8 0.6 copy-start
  107.9 0.6 copy-start.1
  108.5 14.0 %collective-permute-start.7 = (f32[4,384]{1,0:T(4,128)S(1)}, f32[4,384]{1,0:T(4,128)S(1)}, u32[]{:S(2)}, u32[]{:S(2)}) collective-permute-start(f32[4,384]{1,0:T(4,128)S(1)} %get-tuple-element.14), channel_id=1, source_target_pairs={{95,0},{0,1},{1,2},{2,3},{3,4},{4,5},{5,6},{6,7},{7,8},{8,9},{9,10... | collective-permute-start | bytes 18440 | tf_op jit(solution)/shard_map/ppermute | solution.py:276
  112.3 11.5 %collective-permute-start.6 = (f32[4,384]{1,0:T(4,128)S(1)}, f32[4,384]{1,0:T(4,128)S(1)}, u32[]{:S(2)}, u32[]{:S(2)}) collective-permute-start(f32[4,384]{1,0:T(4,128)S(1)} %get-tuple-element.15), channel_id=1, source_target_pairs={{1,0},{2,1},{3,2},{4,3},{5,4},{6,5},{7,6},{8,7},{9,8},{10,9},{11,1... | collective-permute-start | bytes 18440 | tf_op jit(solution)/shard_map/ppermute | solution.py:276
  122.4 1.3 %copy-start.7 = (f32[4,384]{1,0:T(4,128)}, f32[4,384]{1,0:T(4,128)S(1)}, u32[]{:S(2)}) copy-start(f32[4,384]{1,0:T(4,128)S(1)} %collective-permute-done.7.right_ref) | copy-start | bytes 18436
  123.8 0.6 copy-start.8

commit v2 on v1

--- a/solution.py
+++ b/solution.py
@@ -93,9 +93,9 @@
     embc_ref,
     embn_ref,
     radw_ref,
-    envw_ref,
-    mixw_ref,
     outw_ref,
+    envw_hbm,
+    mixw_hbm,
     own_ref,
     a0_ref,
     a1_ref,
@@ -103,10 +103,19 @@
     pack_ref,
     q_ref,
     w_ref,
+    envw_ref,
+    mixw_ref,
+    sems,
     *,
     blocks,
     devices,
 ):
+    loads = [
+        pltpu.make_async_copy(envw_hbm, envw_ref, sems.at[0]),
+        pltpu.make_async_copy(mixw_hbm, mixw_ref, sems.at[1]),
+    ]
+    for load in loads:
+        load.start()
     atoms = pos_ref.shape[3]
     edges = cent_ref.shape[2]
     own_rows = atoms // LANES
@@ -190,7 +199,10 @@
     first = summed * gate0
     latent = first * smooth_col
 
+    for load in loads:
+        load.wait()
     layers = envw_ref.shape[0]
+    chunk = layers * LANES // pack_ref.shape[0]
     share = 1.0 / devices
     saved = []
     for l in range(layers):
@@ -214,17 +226,21 @@
     for l in reversed(range(layers)):
         env_s, mix_s, weighted_s, latent, back, coupled_s, pre, gate = saved[l]
         dpre_s = split2(dlatent * (gate * (1.0 + pre * (1.0 - gate))))
-        pack_ref[l * LANES : (l + 1) * LANES, :] = mm(coupled_s, dpre_s, TN) * share
+        grad_mix = mm(coupled_s, dpre_s, TN) * share
+        step = min(chunk, LANES)
+        for k in range(0, LANES, step):
+            place, start = divmod(l * LANES + k, chunk)
+            pack_ref[place, start : start + step, :] = grad_mix[k : k + step]
         dcoupled = mm(dpre_s, mix_s, NT)
         dback_s = split2(dcoupled * latent)
         term = mm(dback_s, weighted_s, NT)
         dpairs = term if dpairs is None else dpairs + term
         dweighted_s = split2(mm(pairs, dback_s, NN))
         dlatent = dlatent + dcoupled * back + mm(dweighted_s, env_s, NT)
-    rest = pack_ref.shape[0] - layers * LANES
-    row = iota((rest, LANES), 0)
-    tail = jnp.where(row == 0, grad_out[0:1], jnp.where(row == 1, energy, 0.0))
-    pack_ref[layers * LANES :, :] = tail * share
+    row = iota((8, LANES), 0)
+    tail = jnp.where(row == 0, grad_out[0:1], jnp.where(row == 1, energy, 0.0)) * share
+    for k in range(pack_ref.shape[0]):
+        pack_ref[k, chunk:, :] = tail
 
     dpairs_s = split2(jnp.where(same, dpairs, 0.0))
     dunits = mm(units_s, dpairs_s, NT) + mm(units_s, dpairs_s, NN)
@@ -285,15 +301,6 @@
     return jnp.sum(exchanged(copies, axes), axis=0)
 
 
-def summed_over_all(pack):
-    near = lax.axis_size(NEAR)
-    rows = pack.shape[0] // near
-    part = jnp.sum(exchanged(pack.reshape(near, rows, LANES), NEAR), axis=0)
-    part = summed_over(summed_over(part, MIDDLE), FAR)
-    copies = jnp.broadcast_to(part[None], (near, rows, LANES))
-    return exchanged(copies, NEAR).reshape(near * rows, LANES)
-
-
 def body(
     positions,
     species,
@@ -313,13 +320,19 @@
     layers = env_w.shape[0]
     own_rows = atoms // LANES
     devices = lax.axis_size(ALL)
-    tiles = 8 * lax.axis_size(NEAR)
-    packed = (layers * LANES + 2 + tiles - 1) // tiles * tiles
+    near = lax.axis_size(NEAR)
+    chunk = layers * LANES // near
     vmem = pl.BlockSpec(memory_space=pltpu.VMEM)
+
+    def near_by(*arrays):
+        return [pltpu.with_memory_space_constraint(a, pltpu.VMEM) for a in arrays]
+
+    def result(*shape):
+        return pltpu.VMEM(shape, F32)
 
     exported = pl.pallas_call(
         export_kernel,
-        out_shape=jax.ShapeDtypeStruct((4, 4 * LANES), F32),
+        out_shape=result(4, 4 * LANES),
         in_specs=[vmem] * 3,
         out_specs=vmem,
         name="export",
@@ -331,56 +344,65 @@
     y0 = passed_along(column, GY, 1)
     y2 = passed_along(column, GY, -1)
 
-    piece = jax.ShapeDtypeStruct((3, 4, 3 * LANES), F32)
+    piece = result(3, 4, 3 * LANES)
     own, a0, a1, a2, pack = pl.pallas_call(
         lambda *refs: main_kernel(*refs, blocks=edges // BLOCK_EDGES, devices=devices),
         out_shape=(
-            jax.ShapeDtypeStruct((own_rows, 3 * LANES), F32),
+            result(own_rows, 3 * LANES),
             piece,
             piece,
             piece,
-            jax.ShapeDtypeStruct((packed, LANES), F32),
+            result(near, chunk + 8, LANES),
         ),
-        in_specs=[pl.BlockSpec(memory_space=pltpu.SMEM)] + [vmem] * 14,
+        in_specs=[pl.BlockSpec(memory_space=pltpu.SMEM)] + [vmem] * 12 + [pl.BlockSpec(memory_space=pl.ANY)] * 2,
         out_specs=(vmem,) * 5,
         scratch_shapes=[
             pltpu.VMEM((own_rows + 36, 4 * LANES), F32),
             pltpu.VMEM((24, LANES), F32),
+            pltpu.VMEM(env_w.shape, F32),
+            pltpu.VMEM(mix_w.shape, F32),
+            pltpu.SemaphoreType.DMA((2,)),
         ],
         name="edges",
     )(
         block_counts,
-        positions,
-        species,
-        x0,
-        x2,
-        y0,
-        y2,
-        edge_centers,
-        edge_neighbours,
-        emb_center,
-        emb_neighbour,
-        radial_w,
+        *near_by(
+            positions,
+            species,
+            x0,
+            x2,
+            y0,
+            y2,
+            edge_centers,
+            edge_neighbours,
+            emb_center,
+            emb_neighbour,
+            radial_w,
+            out_w.reshape(1, LANES),
+        ),
         env_w,
         mix_w,
-        out_w.reshape(1, LANES),
     )
 
     down = passed_along(a0, GX, -1)
     up = passed_along(a2, GX, 1)
+    part = jnp.sum(exchanged(pack, NEAR), axis=0)
+    part, down, up = lax.optimization_barrier((part, down, up))
+    part = summed_over(part, MIDDLE)
     left = passed_along(a1[0] + down[0] + up[0], GY, -1)
     right = passed_along(a1[2] + down[2] + up[2], GY, 1)
+    part = summed_over(part, FAR)
+    part, left, right = lax.optimization_barrier((part, left, right))
     forces = pl.pallas_call(
         force_kernel,
         out_shape=jax.ShapeDtypeStruct(positions.shape, F32),
         in_specs=[vmem] * 6,
         out_specs=vmem,
         name="forces",
-    )(send_index, own, down, up, left, right)
-
-    total = summed_over_all(pack)
-    top = layers * LANES
-    return forces, total[:top].reshape(layers, LANES, LANES), total[top], total[top + 1, 0]
+    )(send_index, *near_by(own, down, up, left, right))
+    shared = jnp.broadcast_to(part[None, :chunk], (near, chunk, LANES))
+    grad_mix = exchanged(shared, NEAR).reshape(layers, LANES, LANES)
+    return forces, grad_mix, part[chunk], part[chunk + 1, 0]
 
 
 def solution(mesh):

time: 129 us -> 114 us (0.88)
  the two profiles are of different devices: /device:TPU:8 before, /device:TPU:1 now
where the time goes in v2:
time: 114 us; the launch traced here: 113 us
  starting transfers between devices  68.8 us (60%)
  waiting for transfers between devices  16.7 us (15%)
  Pallas kernels  13.4 us (12%)
  blocking collectives  10.4 us (9%)
  local copies, waits for them, and re-layouts  3.12 us (3%)
    ppermute x8, starting transfers between devices, passed_along(): return lax.ppermute(block, axis, route)  48.8 us
    all_to_all x3, starting transfers between devices, exchanged(): return lax.all_to_all(shard, axes, 0, 0)  20 us
    ppermute x8, waiting for transfers between devices, passed_along(): return lax.ppermute(block, axis, route)  13.6 us
    pallas_call x1, Pallas kernels, body(): pl.pallas_call(lambda *refs: main_kernel(*refs, blocks=edges // BLOCK_EDG...  11 us
    all_to_all x1, blocking collectives, exchanged(): return lax.all_to_all(shard, axes, 0, 0)  10.4 us
    all_to_all x3, waiting for transfers between devices, exchanged(): return lax.all_to_all(shard, axes, 0, 0)  3.16 us
  transfers between devices with their start and end apart: 11, of which 5 were waited for; matrix products, arithmetic and copies ran while one was open for 0% of the time, Pallas kernels for 1%

profile of v2, /device:TPU:1, one launch (start us, length us, event | category | flops | bytes accessed | tf_op | source)
XLA Modules:
  0.0 113.4 jit_solution(7739849789684590777)
XLA Ops:
  0.6 0.9 export.1
  1.5 12.4 %collective-permute-start.1 = (f32[4,512]{1,0:T(4,128)S(1)}, f32[4,512]{1,0:T(4,128)S(1)}, u32[]{:S(2)}, u32[]{:S(2)}) collective-permute-start(f32[4,512]{1,0:T(4,128)S(1)} %export.1), channel_id=1, source_target_pairs={{96,0},{192,96},{288,192},{384,288},{480,384},{576,480},{672,576},... | collective-permute-start | bytes 24584 | tf_op jit(solution)/shard_map/ppermute | solution.py:292
  13.9 1.9 %collective-permute-start = (f32[4,512]{1,0:T(4,128)S(1)}, f32[4,512]{1,0:T(4,128)S(1)}, u32[]{:S(2)}, u32[]{:S(2)}) collective-permute-start(f32[4,512]{1,0:T(4,128)S(1)} %export.1), channel_id=1, source_target_pairs={{672,0},{0,96},{96,192},{192,288},{288,384},{384,480},{480,576},{5... | collective-permute-start | bytes 24584 | tf_op jit(solution)/shard_map/ppermute | solution.py:292
  15.8 0.0 collective-permute-done.1.refs_4_
  15.9 1.1 collective-permute-done.refs_3_
  17.0 0.0 copy-start.4
  17.0 0.0 copy-start.5
  17.0 0.0 copy-start.6
  17.0 0.0 copy-start.7
  17.1 13.6 %collective-permute-start.3 = (f32[3,4,512]{2,1,0:T(4,128)S(1)}, f32[3,4,512]{2,1,0:T(4,128)S(1)}, u32[]{:S(2)}, u32[]{:S(2)}) collective-permute-start(f32[3,4,512]{2,1,0:T(4,128)S(1)} %pad_maximum_fusion), channel_id=1, source_target_pairs={{1,0},{2,1},{3,2},{4,3},{5,4},{6,5},{7,6},{8,7},{9,8},{10,9},{11,1... | collective-permute-start | bytes 73736 | tf_op jit(solution)/shard_map/ppermute | solution.py:292
  30.7 1.9 %collective-permute-start.2 = (f32[3,4,512]{2,1,0:T(4,128)S(1)}, f32[3,4,512]{2,1,0:T(4,128)S(1)}, u32[]{:S(2)}, u32[]{:S(2)}) collective-permute-start(f32[3,4,512]{2,1,0:T(4,128)S(1)} %pad_maximum_fusion), channel_id=1, source_target_pairs={{95,0},{0,1},{1,2},{2,3},{3,4},{4,5},{5,6},{6,7},{7,8},{8,9},{9,10... | collective-permute-start | bytes 73736 | tf_op jit(solution)/shard_map/ppermute | solution.py:292
  32.6 10.9 %collective-permute-done.2.refs_5_ = f32[3,4,512]{2,1,0:T(4,128)S(1)} collective-permute-done((f32[3,4,512]{2,1,0:T(4,128)S(1)}, f32[3,4,512]{2,1,0:T(4,128)S(1)}, u32[]{:S(2)}, u32[]{:S(2)}) %collective-permute-start.2) | collective-permute-done | bytes 24608 | tf_op jit(solution)/shard_map/ppermute | solution.py:292
  43.6 11.0 %edges.1 = (f32[4,384]{1,0:T(4,128)S(1)}, f32[3,4,384]{2,1,0:T(4,128)S(1)}, f32[3,4,384]{2,1,0:T(4,128)S(1)}, f32[3,4,384]{2,1,0:T(4,128)S(1)}, f32[8,40,128]{2,1,0:T(8,128)}) custom-call(s32[1,1,4]{2,1,0:T(1,128)} %refs_0_.1, f32[3,1,1,512]{3,2,1,0:T(1,128)S(1)} %copy-done, s32[1,1,512]{2,1,0:T(1,128)S(1)} %copy-done.1, ...), custom_call_target="tpu_custom_call" | custom-call | tf_op jit(solution)/shard_map/edges/pallas_call | solution.py:348
  54.6 7.9 %all-to-all-start = ((f32[8,40,128]{2,1,0:T(8,128)}), f32[8,40,128]{2,1,0:T(8,128)S(1)}, u32[]{:S(2)}, u32[]{:S(2)}) async-start(f32[8,40,128]{2,1,0:T(8,128)} %get-tuple-element.16), calls=%async_computation | async-start | bytes 327680 | tf_op jit(solution)/shard_map/all_to_all | solution.py:296
  62.5 2.0 %collective-permute-start.4 = (f32[3,4,384]{2,1,0:T(4,128)S(1)}, f32[3,4,384]{2,1,0:T(4,128)S(1)}, u32[]{:S(2)}, u32[]{:S(2)}) collective-permute-start(f32[3,4,384]{2,1,0:T(4,128)S(1)} %get-tuple-element.17), channel_id=1, source_target_pairs={{96,0},{192,96},{288,192},{384,288},{480,384},{576,480},{672,576},... | collective-permute-start | bytes 55304 | tf_op jit(solution)/shard_map/ppermute | solution.py:292
  64.5 3.6 %collective-permute-start.5 = (f32[3,4,384]{2,1,0:T(4,128)S(1)}, f32[3,4,384]{2,1,0:T(4,128)S(1)}, u32[]{:S(2)}, u32[]{:S(2)}) collective-permute-start(f32[3,4,384]{2,1,0:T(4,128)S(1)} %get-tuple-element.18), channel_id=1, source_target_pairs={{672,0},{0,96},{96,192},{192,288},{288,384},{384,480},{480,576},{5... | collective-permute-start | bytes 55304 | tf_op jit(solution)/shard_map/ppermute | solution.py:292
  68.1 0.0 all-to-all-done
  68.1 0.0 collective-permute-done.4.down_ref
  68.1 0.8 collective-permute-done.5.up_ref
  69.0 10.4 %all_to_all.20 = f32[8,40,128]{2,1,0:T(8,128)S(1)} all-to-all(f32[8,40,128]{2,1,0:T(8,128)S(1)} %broadcast_in_dim.6), channel_id=1, replica_groups=mesh['gx_0'=4,'gx_1'=2,'gy_0'=2,'gy_1'=12,'gy_2'=4] {'gx_0','gy_0'}, dimensions={0} | all-to-all | bytes 327680 | tf_op jit(solution)/shard_map/all_to_all | solution.py:296
  79.4 0.7 broadcast_in_dim.7
  80.1 3.5 %all-to-all-start.2 = ((f32[12,40,128]{2,1,0:T(8,128)}), f32[12,40,128]{2,1,0:T(8,128)S(1)}, u32[]{:S(2)}, u32[]{:S(2)}) async-start(f32[12,40,128]{2,1,0:T(8,128)} %broadcast_in_dim.7), calls=%async_computation.2 | async-start | bytes 491520 | tf_op jit(solution)/shard_map/all_to_all | solution.py:296
  83.7 3.3 %collective-permute-start.7 = (f32[4,384]{1,0:T(4,128)S(1)}, f32[4,384]{1,0:T(4,128)S(1)}, u32[]{:S(2)}, u32[]{:S(2)}) collective-permute-start(f32[4,384]{1,0:T(4,128)S(1)} %get-tuple-element.26), channel_id=1, source_target_pairs={{95,0},{0,1},{1,2},{2,3},{3,4},{4,5},{5,6},{6,7},{7,8},{8,9},{9,10... | collective-permute-start | bytes 18440 | tf_op jit(solution)/shard_map/ppermute | solution.py:292
  86.9 10.1 %collective-permute-start.6 = (f32[4,384]{1,0:T(4,128)S(1)}, f32[4,384]{1,0:T(4,128)S(1)}, u32[]{:S(2)}, u32[]{:S(2)}) collective-permute-start(f32[4,384]{1,0:T(4,128)S(1)} %get-tuple-element.27), channel_id=1, source_target_pairs={{1,0},{2,1},{3,2},{4,3},{5,4},{6,5},{7,6},{8,7},{9,8},{10,9},{11,1... | collective-permute-start | bytes 18440 | tf_op jit(solution)/shard_map/ppermute | solution.py:292
  97.1 0.7 collective-permute-done.6.left_ref
  97.8 0.5 slice.35
  98.4 0.7 broadcast_in_dim.8
  99.0 8.5 %all-to-all-start.3 = ((f32[8,32,128]{2,1,0:T(8,128)}), f32[8,32,128]{2,1,0:T(8,128)S(1)}, u32[]{:S(2)}, u32[]{:S(2)}) async-start(f32[8,32,128]{2,1,0:T(8,128)} %broadcast_in_dim.8), calls=%async_computation.3 | async-start | bytes 262144 | tf_op jit(solution)/shard_map/all_to_all | solution.py:296
  107.6 1.5 %forces.1 = f32[3,1,1,512]{3,2,1,0:T(1,128)} custom-call(s32[1,1,384]{2,1,0:T(1,128)} %send_ref.3, f32[4,384]{1,0:T(4,128)S(1)} %get-tuple-element.15.own_ref, f32[3,4,384]{2,1,0:T(4,128)S(1)} %collective-permute-done.4.down_ref, f32[3,4,384]{2,1,0:T(4,128)S(1)} %collective-permute-done.5.up_ref, f32[4,384]{1,0:T(4,128)S(1)} %collective-permute-done.6.left_ref, ...), custom_call_target="tpu_custom_call" | custom-call | tf_op jit(solution)/shard_map/forces/pallas_call | solution.py:396
  109.1 0.5 slice_bitcast_fusion
  109.6 3.2 %all-to-all-done.3 = f32[8,32,128]{2,1,0:T(8,128)S(1)} async-done(((f32[8,32,128]{2,1,0:T(8,128)}), f32[8,32,128]{2,1,0:T(8,128)S(1)}, u32[]{:S(2)}, u32[]{:S(2)}) %all-to-all-start.3) | async-done | bytes 131104 | tf_op jit(solution)/shard_map/all_to_all | solution.py:296
  112.8 0.7 copy.17
  (22 shorter events, 0.1 us)
Async XLA Ops:
  1.5 14.3 %collective-permute-start.1 = (f32[4,512]{1,0:T(4,128)S(1)}, f32[4,512]{1,0:T(4,128)S(1)}, u32[]{:S(2)}, u32[]{:S(2)}) collective-permute-start(f32[4,512]{1,0:T(4,128)S(1)} %export.1), channel_id=1, source_target_pairs={{96,0},{192,96},{288,192},{384,288},{480,384},{576,480},{672,576},... | collective-permute-start | bytes 24584 | tf_op jit(solution)/shard_map/ppermute | solution.py:292
  13.9 3.1 %collective-permute-start = (f32[4,512]{1,0:T(4,128)S(1)}, f32[4,512]{1,0:T(4,128)S(1)}, u32[]{:S(2)}, u32[]{:S(2)}) collective-permute-start(f32[4,512]{1,0:T(4,128)S(1)} %export.1), channel_id=1, source_target_pairs={{672,0},{0,96},{96,192},{192,288},{288,384},{384,480},{480,576},{5... | collective-permute-start | bytes 24584 | tf_op jit(solution)/shard_map/ppermute | solution.py:292
  17.0 26.5 %copy-start = (f32[3,1,1,512]{3,2,1,0:T(1,128)S(1)}, f32[3,1,1,512]{3,2,1,0:T(1,128)}, u32[]{:S(2)}) copy-start(f32[3,1,1,512]{3,2,1,0:T(1,128)} %refs_1_.1) | copy-start | bytes 18436
  17.0 26.5 %copy-start.1 = (s32[1,1,512]{2,1,0:T(1,128)S(1)}, s32[1,1,512]{2,1,0:T(1,128)}, u32[]{:S(2)}) copy-start(s32[1,1,512]{2,1,0:T(1,128)} %refs_2_.1) | copy-start | bytes 6148
  17.0 26.5 %copy-start.2 = (f32[5,128]{1,0:T(8,128)S(1)}, f32[5,128]{1,0:T(8,128)}, u32[]{:S(2)}) copy-start(f32[5,128]{1,0:T(8,128)} %refs_9_.1) | copy-start | bytes 7684
  17.0 26.5 %copy-start.3 = (f32[5,128]{1,0:T(8,128)S(1)}, f32[5,128]{1,0:T(8,128)}, u32[]{:S(2)}) copy-start(f32[5,128]{1,0:T(8,128)} %refs_10_.1) | copy-start | bytes 7684
  17.0 26.5 %copy-start.4 = (f32[8,128]{1,0:T(8,128)S(1)}, f32[8,128]{1,0:T(8,128)}, u32[]{:S(2)}) copy-start(f32[8,128]{1,0:T(8,128)} %refs_11_.1) | copy-start | bytes 12292
  17.0 26.5 %copy-start.5 = (s32[1,1,512]{2,1,0:T(1,128)S(1)}, s32[1,1,512]{2,1,0:T(1,128)}, u32[]{:S(2)}) copy-start(s32[1,1,512]{2,1,0:T(1,128)} %refs_7_.1) | copy-start | bytes 6148
  17.0 26.5 %copy-start.6 = (s32[1,1,512]{2,1,0:T(1,128)S(1)}, s32[1,1,512]{2,1,0:T(1,128)}, u32[]{:S(2)}) copy-start(s32[1,1,512]{2,1,0:T(1,128)} %refs_8_.1) | copy-start | bytes 6148
  17.0 26.5 %copy-start.7 = (f32[128]{0:T(128)S(1)}, f32[128]{0:T(128)}, u32[]{:S(2)}) copy-start(f32[128]{0:T(128)} %param.23) | copy-start | bytes 1540
  17.1 15.5 %collective-permute-start.3 = (f32[3,4,512]{2,1,0:T(4,128)S(1)}, f32[3,4,512]{2,1,0:T(4,128)S(1)}, u32[]{:S(2)}, u32[]{:S(2)}) collective-permute-start(f32[3,4,512]{2,1,0:T(4,128)S(1)} %pad_maximum_fusion), channel_id=1, source_target_pairs={{1,0},{2,1},{3,2},{4,3},{5,4},{6,5},{7,6},{8,7},{9,8},{10,9},{11,1... | collective-permute-start | bytes 73736 | tf_op jit(solution)/shard_map/ppermute | solution.py:292
  30.7 12.9 %collective-permute-start.2 = (f32[3,4,512]{2,1,0:T(4,128)S(1)}, f32[3,4,512]{2,1,0:T(4,128)S(1)}, u32[]{:S(2)}, u32[]{:S(2)}) collective-permute-start(f32[3,4,512]{2,1,0:T(4,128)S(1)} %pad_maximum_fusion), channel_id=1, source_target_pairs={{95,0},{0,1},{1,2},{2,3},{3,4},{4,5},{5,6},{6,7},{7,8},{8,9},{9,10... | collective-permute-start | bytes 73736 | tf_op jit(solution)/shard_map/ppermute | solution.py:292
  54.6 13.5 %all-to-all-start = ((f32[8,40,128]{2,1,0:T(8,128)}), f32[8,40,128]{2,1,0:T(8,128)S(1)}, u32[]{:S(2)}, u32[]{:S(2)}) async-start(f32[8,40,128]{2,1,0:T(8,128)} %get-tuple-element.16), calls=%async_computation | async-start | bytes 327680 | tf_op jit(solution)/shard_map/all_to_all | solution.py:296
  62.5 5.6 %collective-permute-start.4 = (f32[3,4,384]{2,1,0:T(4,128)S(1)}, f32[3,4,384]{2,1,0:T(4,128)S(1)}, u32[]{:S(2)}, u32[]{:S(2)}) collective-permute-start(f32[3,4,384]{2,1,0:T(4,128)S(1)} %get-tuple-element.17), channel_id=1, source_target_pairs={{96,0},{192,96},{288,192},{384,288},{480,384},{576,480},{672,576},... | collective-permute-start | bytes 55304 | tf_op jit(solution)/shard_map/ppermute | solution.py:292
  64.5 4.4 %collective-permute-start.5 = (f32[3,4,384]{2,1,0:T(4,128)S(1)}, f32[3,4,384]{2,1,0:T(4,128)S(1)}, u32[]{:S(2)}, u32[]{:S(2)}) collective-permute-start(f32[3,4,384]{2,1,0:T(4,128)S(1)} %get-tuple-element.18), channel_id=1, source_target_pairs={{672,0},{0,96},{96,192},{192,288},{288,384},{384,480},{480,576},{5... | collective-permute-start | bytes 55304 | tf_op jit(solution)/shard_map/ppermute | solution.py:292
  80.1 17.0 %all-to-all-start.2 = ((f32[12,40,128]{2,1,0:T(8,128)}), f32[12,40,128]{2,1,0:T(8,128)S(1)}, u32[]{:S(2)}, u32[]{:S(2)}) async-start(f32[12,40,128]{2,1,0:T(8,128)} %broadcast_in_dim.7), calls=%async_computation.2 | async-start | bytes 491520 | tf_op jit(solution)/shard_map/all_to_all | solution.py:296
  83.7 13.5 %collective-permute-start.7 = (f32[4,384]{1,0:T(4,128)S(1)}, f32[4,384]{1,0:T(4,128)S(1)}, u32[]{:S(2)}, u32[]{:S(2)}) collective-permute-start(f32[4,384]{1,0:T(4,128)S(1)} %get-tuple-element.26), channel_id=1, source_target_pairs={{95,0},{0,1},{1,2},{2,3},{3,4},{4,5},{5,6},{6,7},{7,8},{8,9},{9,10... | collective-permute-start | bytes 18440 | tf_op jit(solution)/shard_map/ppermute | solution.py:292
  86.9 10.9 %collective-permute-start.6 = (f32[4,384]{1,0:T(4,128)S(1)}, f32[4,384]{1,0:T(4,128)S(1)}, u32[]{:S(2)}, u32[]{:S(2)}) collective-permute-start(f32[4,384]{1,0:T(4,128)S(1)} %get-tuple-element.27), channel_id=1, source_target_pairs={{1,0},{2,1},{3,2},{4,3},{5,4},{6,5},{7,6},{8,7},{9,8},{10,9},{11,1... | collective-permute-start | bytes 18440 | tf_op jit(solution)/shard_map/ppermute | solution.py:292
  99.0 13.7 %all-to-all-start.3 = ((f32[8,32,128]{2,1,0:T(8,128)}), f32[8,32,128]{2,1,0:T(8,128)S(1)}, u32[]{:S(2)}, u32[]{:S(2)}) async-start(f32[8,32,128]{2,1,0:T(8,128)} %broadcast_in_dim.8), calls=%async_computation.3 | async-start | bytes 262144 | tf_op jit(solution)/shard_map/all_to_all | solution.py:296

commit v3 on v2

--- a/solution.py
+++ b/solution.py
@@ -81,13 +81,14 @@
 
 
 def main_kernel(
+    side_ref,
     counts_ref,
     pos_ref,
     spec_ref,
-    x0_ref,
-    x2_ref,
-    y0_ref,
-    y2_ref,
+    xa_ref,
+    xb_ref,
+    ya_ref,
+    yb_ref,
     cent_ref,
     neigh_ref,
     embc_ref,
@@ -125,6 +126,8 @@
         row = pos_ref[c, 0] if c < 3 else spec_ref[0].astype(F32)
         for h in range(own_rows):
             q_ref[h : h + 1, c * LANES : (c + 1) * LANES] = row[:, h * LANES : (h + 1) * LANES]
+    turn_x = 2 * (side_ref[0] // 2) - 1
+    turn_y = 2 * (side_ref[0] % 2) - 1
     lane = iota((4, 4 * LANES), 1)
     for s in range(9):
         a, b = s // 3, s % 3
@@ -132,15 +135,17 @@
         if s == 4:
             q_ref[rows, :] = jnp.zeros((4, 4 * LANES), F32)
             continue
-        ghost = (y0_ref[a], None, y2_ref[a])[b] if b != 1 else (x0_ref, x2_ref)[a // 2][...]
-        shift = jnp.where(lane < LANES, F32((a - 1) * side), jnp.where(lane < 2 * LANES, F32((b - 1) * side), 0.0))
-        q_ref[rows, :] = ghost + shift
+        ghost = (ya_ref[a], None, yb_ref[a])[b] if b != 1 else (xa_ref, xb_ref)[a // 2][...]
+        shift_x = (turn_x * (a - 1)).astype(F32) * F32(side)
+        shift_y = (turn_y * (b - 1)).astype(F32) * F32(side)
+        q_ref[rows, :] = ghost + jnp.where(lane < LANES, shift_x, jnp.where(lane < 2 * LANES, shift_y, 0.0))
     total_rows = q_ref.shape[0]
 
     ends = jnp.concatenate([neigh_ref[0], cent_ref[0]], axis=1)
     at_row = iota((total_rows, 2 * edges), 0)
     past = at_row - own_rows
-    holds = jnp.where(past < 0, at_row, jnp.where(past % 4 == 3, -1, own_rows + 3 * (past // 4) + past % 4))
+    slot = 3 * (1 + turn_x * (past // 12 - 1)) + 1 + turn_y * (past // 4 % 3 - 1)
+    holds = jnp.where(past < 0, at_row, jnp.where(past % 4 == 3, -1, own_rows + 3 * slot + past % 4))
     hot = (holds == ends // LANES).astype(F32)
     in_lane = iota((LANES, 2 * edges), 0) == ends % LANES
     table = jnp.concatenate(split3(q_ref[...]), axis=0).astype(BF16)
@@ -266,7 +271,9 @@
         (a0_ref, a1_ref, a2_ref)[s // 3][s % 3] = pool[rows]
 
 
-def force_kernel(send_ref, own_ref, down_ref, up_ref, left_ref, right_ref, out_ref):
+def force_kernel(send_ref, own_ref, down_ref, up_ref, left_ref, right_ref, part_ref, out_ref, gout_ref, energy_ref):
+    gout_ref[...] = part_ref[0:1, :]
+    energy_ref[...] = part_ref[1:2, 0:1]
     atoms, count = out_ref.shape[3], send_ref.shape[2]
     back = (down_ref[1] + up_ref[1]) + (left_ref[...] + right_ref[...])
     rows = []
@@ -286,9 +293,9 @@
         out_ref[c, 0] = -(mine + placed[c : c + 1])
 
 
-def passed_along(block, axis, distance):
+def traded(block, axis, first):
     count = lax.axis_size(axis)
-    route = [((i - distance) % count, i) for i in range(count)]
+    route = [(i, (i + 1 if i % 2 == first else i - 1) % count) for i in range(count)]
     return lax.ppermute(block, axis, route)
 
 
@@ -338,11 +345,12 @@
         name="export",
     )(positions, species, send_index)
 
-    x0 = passed_along(exported, GX, 1)
-    x2 = passed_along(exported, GX, -1)
-    column = jnp.stack([x0, exported, x2])
-    y0 = passed_along(column, GY, 1)
-    y2 = passed_along(column, GY, -1)
+    side = (2 * (lax.axis_index(GX) % 2) + lax.axis_index(GY) % 2).reshape(1)
+    xb = traded(exported, GX, 1)
+    xa = traded(exported, GX, 0)
+    column = jnp.stack([xa, exported, xb])
+    yb = traded(column, GY, 1)
+    ya = traded(column, GY, 0)
 
     piece = result(3, 4, 3 * LANES)
     own, a0, a1, a2, pack = pl.pallas_call(
@@ -354,7 +362,7 @@
             piece,
             result(near, chunk + 8, LANES),
         ),
-        in_specs=[pl.BlockSpec(memory_space=pltpu.SMEM)] + [vmem] * 12 + [pl.BlockSpec(memory_space=pl.ANY)] * 2,
+        in_specs=[pl.BlockSpec(memory_space=pltpu.SMEM)] * 2 + [vmem] * 12 + [pl.BlockSpec(memory_space=pl.ANY)] * 2,
         out_specs=(vmem,) * 5,
         scratch_shapes=[
             pltpu.VMEM((own_rows + 36, 4 * LANES), F32),
@@ -365,14 +373,15 @@
         ],
         name="edges",
     )(
+        side,
         block_counts,
         *near_by(
             positions,
             species,
-            x0,
-            x2,
-            y0,
-            y2,
+            xa,
+            xb,
+            ya,
+            yb,
             edge_centers,
             edge_neighbours,
             emb_center,
@@ -384,25 +393,30 @@
         mix_w,
     )
 
-    down = passed_along(a0, GX, -1)
-    up = passed_along(a2, GX, 1)
+    over = traded(a2, GX, 1), traded(a0, GX, 0)
     part = jnp.sum(exchanged(pack, NEAR), axis=0)
-    part, down, up = lax.optimization_barrier((part, down, up))
     part = summed_over(part, MIDDLE)
-    left = passed_along(a1[0] + down[0] + up[0], GY, -1)
-    right = passed_along(a1[2] + down[2] + up[2], GY, 1)
+    part, over = lax.optimization_barrier((part, over))
+    across = (
+        traded(a1[2] + over[0][2] + over[1][2], GY, 1),
+        traded(a1[0] + over[0][0] + over[1][0], GY, 0),
+    )
     part = summed_over(part, FAR)
-    part, left, right = lax.optimization_barrier((part, left, right))
-    forces = pl.pallas_call(
+    part, across = lax.optimization_barrier((part, across))
+    forces, grad_out, energy = pl.pallas_call(
         force_kernel,
-        out_shape=jax.ShapeDtypeStruct(positions.shape, F32),
-        in_specs=[vmem] * 6,
-        out_specs=vmem,
+        out_shape=(
+            jax.ShapeDtypeStruct(positions.shape, F32),
+            jax.ShapeDtypeStruct((1, LANES), F32),
+            jax.ShapeDtypeStruct((1, 1), F32),
+        ),
+        in_specs=[vmem] * 7,
+        out_specs=(vmem,) * 3,
         name="forces",
-    )(send_index, *near_by(own, down, up, left, right))
+    )(send_index, *near_by(own, *over, *across, part[chunk:]))
     shared = jnp.broadcast_to(part[None, :chunk], (near, chunk, LANES))
     grad_mix = exchanged(shared, NEAR).reshape(layers, LANES, LANES)
-    return forces, grad_mix, part[chunk], part[chunk + 1, 0]
+    return forces, grad_mix, grad_out.reshape(LANES), energy.reshape(())
 
 
 def solution(mesh):

time: 114 us -> 103 us (0.904)
  starting transfers between devices: 68.8 us -> 61.4 us
  waiting for transfers between devices: 16.7 us -> 12.2 us
    ppermute x8, waiting for transfers between devices: 13.6 us -> 5.31 us  [traded(): return lax.ppermute(block, axis, route)]
    all_to_all x3, starting transfers between devices: 20 us -> 13.9 us  [exchanged(): return lax.all_to_all(shard, axes, 0, 0)]
    all_to_all x3, waiting for transfers between devices: 3.16 us -> 6.91 us  [exchanged(): return lax.all_to_all(shard, axes, 0, 0)]
    ppermute x8, starting transfers between devices: 48.8 us -> 47.6 us  [traded(): return lax.ppermute(block, axis, route)]
  transfers between devices with their start and end apart: 11 -> 11, of which waited for: 5 -> 6; matrix products, arithmetic and copies ran while one was open for 0% -> 0% of each run, Pallas kernels for 1% -> 1%
where the time goes in v3:
time: 103 us; the launch traced here: 102 us
  starting transfers between devices  61.4 us (60%)
  Pallas kernels  13.4 us (13%)
  waiting for transfers between devices  12.2 us (12%)
  blocking collectives  10.8 us (10%)
  local copies, waits for them, and re-layouts  3.37 us (3%)
    ppermute x8, starting transfers between devices, traded(): return lax.ppermute(block, axis, route)  47.6 us
    all_to_all x3, starting transfers between devices, exchanged(): return lax.all_to_all(shard, axes, 0, 0)  13.9 us
    pallas_call x1, Pallas kernels, body(): pl.pallas_call(lambda *refs: main_kernel(*refs, blocks=edges // BLOCK_EDG...  11 us
    all_to_all x1, blocking collectives, exchanged(): return lax.all_to_all(shard, axes, 0, 0)  10.8 us
    all_to_all x3, waiting for transfers between devices, exchanged(): return lax.all_to_all(shard, axes, 0, 0)  6.91 us
    ppermute x8, waiting for transfers between devices, traded(): return lax.ppermute(block, axis, route)  5.31 us
  transfers between devices with their start and end apart: 11, of which 6 were waited for; matrix products, arithmetic and copies ran while one was open for 0% of the time, Pallas kernels for 1%

profile of v3, /device:TPU:1, one launch (start us, length us, event | category | flops | bytes accessed | tf_op | source)
XLA Modules:
  0.0 102.2 jit_solution(4822313871830286262)
XLA Ops:
  0.6 0.9 export.1
  1.5 4.6 %collective-permute-start.1 = (f32[4,512]{1,0:T(4,128)S(1)}, f32[4,512]{1,0:T(4,128)S(1)}, u32[]{:S(2)}, u32[]{:S(2)}) collective-permute-start(f32[4,512]{1,0:T(4,128)S(1)} %export.1), channel_id=1, source_target_pairs={{0,672},{96,192},{192,96},{288,384},{384,288},{480,576},{576,480},... | collective-permute-start | bytes 24584 | tf_op jit(solution)/shard_map/ppermute | solution.py:299
  6.1 9.7 %collective-permute-start = (f32[4,512]{1,0:T(4,128)S(1)}, f32[4,512]{1,0:T(4,128)S(1)}, u32[]{:S(2)}, u32[]{:S(2)}) collective-permute-start(f32[4,512]{1,0:T(4,128)S(1)} %export.1), channel_id=1, source_target_pairs={{0,96},{96,0},{192,288},{288,192},{384,480},{480,384},{576,672},{6... | collective-permute-start | bytes 24584 | tf_op jit(solution)/shard_map/ppermute | solution.py:299
  15.9 0.8 collective-permute-done.refs_4_
  16.7 13.4 %collective-permute-start.3 = (f32[3,4,512]{2,1,0:T(4,128)S(1)}, f32[3,4,512]{2,1,0:T(4,128)S(1)}, u32[]{:S(2)}, u32[]{:S(2)}) collective-permute-start(f32[3,4,512]{2,1,0:T(4,128)S(1)} %pad_maximum_fusion), channel_id=1, source_target_pairs={{0,95},{1,2},{2,1},{3,4},{4,3},{5,6},{6,5},{7,8},{8,7},{9,10},{10,... | collective-permute-start | bytes 73736 | tf_op jit(solution)/shard_map/ppermute | solution.py:299
  30.1 1.9 %collective-permute-start.2 = (f32[3,4,512]{2,1,0:T(4,128)S(1)}, f32[3,4,512]{2,1,0:T(4,128)S(1)}, u32[]{:S(2)}, u32[]{:S(2)}) collective-permute-start(f32[3,4,512]{2,1,0:T(4,128)S(1)} %pad_maximum_fusion), channel_id=1, source_target_pairs={{0,1},{1,0},{2,3},{3,2},{4,5},{5,4},{6,7},{7,6},{8,9},{9,8},{10,11... | collective-permute-start | bytes 73736 | tf_op jit(solution)/shard_map/ppermute | solution.py:299
  32.0 0.0 copy-start.6
  32.0 0.0 copy-start.5
  32.0 0.0 copy-start.4
  32.1 0.0 copy-start.3
  32.1 0.0 copy-start
  32.1 0.0 copy-start.1
  32.1 2.5 %collective-permute-done.2.refs_6_ = f32[3,4,512]{2,1,0:T(4,128)S(1)} collective-permute-done((f32[3,4,512]{2,1,0:T(4,128)S(1)}, f32[3,4,512]{2,1,0:T(4,128)S(1)}, u32[]{:S(2)}, u32[]{:S(2)}) %collective-permute-start.2) | collective-permute-done | bytes 24608 | tf_op jit(solution)/shard_map/ppermute | solution.py:299
  34.7 0.6 copy-done.7
  35.3 11.0 %edges.1 = (f32[4,384]{1,0:T(4,128)S(1)}, f32[3,4,384]{2,1,0:T(4,128)S(1)}, f32[3,4,384]{2,1,0:T(4,128)S(1)}, f32[3,4,384]{2,1,0:T(4,128)S(1)}, f32[8,40,128]{2,1,0:T(8,128)S(1)}) custom-call(s32[1]{0:T(128)} %bitcast.refs_0_, s32[1,1,4]{2,1,0:T(1,128)} %refs_1_.1, f32[3,1,1,512]{3,2,1,0:T(1,128)S(1)} %copy-done, s32[1,1,512]{2,1,0:T(1,128)S(1)} %copy-done.1, ...), custom_call_target="tpu_custom_call" | custom-call | tf_op jit(solution)/shard_map/edges/pallas_call | solution.py:356
  46.3 10.8 %all_to_all.20 = f32[8,40,128]{2,1,0:T(8,128)S(1)} all-to-all(f32[8,40,128]{2,1,0:T(8,128)S(1)} %get-tuple-element.19), channel_id=1, replica_groups=mesh['gx_0'=4,'gx_1'=2,'gy_0'=2,'gy_1'=12,'gy_2'=4] {'gx_1','gy_2'}, dimensions={0} | all-to-all | bytes 327680 | tf_op jit(solution)/shard_map/all_to_all | solution.py:303
  57.1 0.7 broadcast_in_dim.6
  57.8 3.4 %all-to-all-start.1 = ((f32[8,40,128]{2,1,0:T(8,128)}), f32[8,40,128]{2,1,0:T(8,128)S(1)}, u32[]{:S(2)}, u32[]{:S(2)}) async-start(f32[8,40,128]{2,1,0:T(8,128)} %broadcast_in_dim.6), calls=%async_computation.1 | async-start | bytes 327680 | tf_op jit(solution)/shard_map/all_to_all | solution.py:303
  61.2 3.7 %collective-permute-start.4 = (f32[3,4,384]{2,1,0:T(4,128)S(1)}, f32[3,4,384]{2,1,0:T(4,128)S(1)}, u32[]{:S(2)}, u32[]{:S(2)}) collective-permute-start(f32[3,4,384]{2,1,0:T(4,128)S(1)} %get-tuple-element.20), channel_id=1, source_target_pairs={{0,672},{96,192},{192,96},{288,384},{384,288},{480,576},{576,480},... | collective-permute-start | bytes 55304 | tf_op jit(solution)/shard_map/ppermute | solution.py:299
  64.9 3.7 %collective-permute-start.5 = (f32[3,4,384]{2,1,0:T(4,128)S(1)}, f32[3,4,384]{2,1,0:T(4,128)S(1)}, u32[]{:S(2)}, u32[]{:S(2)}) collective-permute-start(f32[3,4,384]{2,1,0:T(4,128)S(1)} %get-tuple-element.21), channel_id=1, source_target_pairs={{0,96},{96,0},{192,288},{288,192},{384,480},{480,384},{576,672},{6... | collective-permute-start | bytes 55304 | tf_op jit(solution)/shard_map/ppermute | solution.py:299
  68.6 0.8 collective-permute-done.5.up_ref
  69.4 0.7 broadcast_in_dim.7
  70.1 4.7 %all-to-all-start.2 = ((f32[12,40,128]{2,1,0:T(8,128)}), f32[12,40,128]{2,1,0:T(8,128)S(1)}, u32[]{:S(2)}, u32[]{:S(2)}) async-start(f32[12,40,128]{2,1,0:T(8,128)} %broadcast_in_dim.7), calls=%async_computation.2 | async-start | bytes 491520 | tf_op jit(solution)/shard_map/all_to_all | solution.py:303
  74.9 2.6 %collective-permute-start.7 = (f32[4,384]{1,0:T(4,128)S(1)}, f32[4,384]{1,0:T(4,128)S(1)}, u32[]{:S(2)}, u32[]{:S(2)}) collective-permute-start(f32[4,384]{1,0:T(4,128)S(1)} %get-tuple-element.32), channel_id=1, source_target_pairs={{0,1},{1,0},{2,3},{3,2},{4,5},{5,4},{6,7},{7,6},{8,9},{9,8},{10,11... | collective-permute-start | bytes 18440 | tf_op jit(solution)/shard_map/ppermute | solution.py:299
  77.4 8.0 %collective-permute-start.6 = (f32[4,384]{1,0:T(4,128)S(1)}, f32[4,384]{1,0:T(4,128)S(1)}, u32[]{:S(2)}, u32[]{:S(2)}) collective-permute-start(f32[4,384]{1,0:T(4,128)S(1)} %get-tuple-element.33), channel_id=1, source_target_pairs={{0,95},{1,2},{2,1},{3,4},{4,3},{5,6},{6,5},{7,8},{8,7},{9,10},{10,... | collective-permute-start | bytes 18440 | tf_op jit(solution)/shard_map/ppermute | solution.py:299
  85.4 3.2 %all-to-all-done.2 = f32[12,40,128]{2,1,0:T(8,128)S(1)} async-done(((f32[12,40,128]{2,1,0:T(8,128)}), f32[12,40,128]{2,1,0:T(8,128)S(1)}, u32[]{:S(2)}, u32[]{:S(2)}) %all-to-all-start.2) | async-done | bytes 245792 | tf_op jit(solution)/shard_map/all_to_all | solution.py:303
  88.7 1.2 %collective-permute-done.6.left_ref = f32[4,384]{1,0:T(4,128)S(1)} collective-permute-done((f32[4,384]{1,0:T(4,128)S(1)}, f32[4,384]{1,0:T(4,128)S(1)}, u32[]{:S(2)}, u32[]{:S(2)}) %collective-permute-start.6) | collective-permute-done | bytes 6176 | tf_op jit(solution)/shard_map/ppermute | solution.py:299
  89.9 0.7 broadcast_in_dim.8
  90.6 5.8 %all-to-all-start.3 = ((f32[8,32,128]{2,1,0:T(8,128)}), f32[8,32,128]{2,1,0:T(8,128)S(1)}, u32[]{:S(2)}, u32[]{:S(2)}) async-start(f32[8,32,128]{2,1,0:T(8,128)} %broadcast_in_dim.8), calls=%async_computation.3 | async-start | bytes 262144 | tf_op jit(solution)/shard_map/all_to_all | solution.py:303
  96.4 1.5 %forces.1 = (f32[3,1,1,512]{3,2,1,0:T(1,128)}, f32[1,128]{1,0:T(1,128)}, f32[1,1]{1,0:T(1,128)}) custom-call(s32[1,1,384]{2,1,0:T(1,128)} %send_ref.3, f32[4,384]{1,0:T(4,128)S(1)} %get-tuple-element.18.own_ref, f32[3,4,384]{2,1,0:T(4,128)S(1)} %collective-permute-done.4.down_ref, f32[3,4,384]{2,1,0:T(4,128)S(1)} %collective-permute-done.5.up_ref, ...), custom_call_target="tpu_custom_call" | custom-call | tf_op jit(solution)/shard_map/forces/pallas_call | solution.py:406
  97.9 3.7 %all-to-all-done.3 = f32[8,32,128]{2,1,0:T(8,128)S(1)} async-done(((f32[8,32,128]{2,1,0:T(8,128)}), f32[8,32,128]{2,1,0:T(8,128)S(1)}, u32[]{:S(2)}, u32[]{:S(2)}) %all-to-all-start.3) | async-done | bytes 131104 | tf_op jit(solution)/shard_map/all_to_all | solution.py:303
  101.6 0.7 copy.17
  (21 shorter events, 0.1 us)
Async XLA Ops:
  1.5 14.3 %collective-permute-start.1 = (f32[4,512]{1,0:T(4,128)S(1)}, f32[4,512]{1,0:T(4,128)S(1)}, u32[]{:S(2)}, u32[]{:S(2)}) collective-permute-start(f32[4,512]{1,0:T(4,128)S(1)} %export.1), channel_id=1, source_target_pairs={{0,672},{96,192},{192,96},{288,384},{384,288},{480,576},{576,480},... | collective-permute-start | bytes 24584 | tf_op jit(solution)/shard_map/ppermute | solution.py:299
  6.1 10.5 %collective-permute-start = (f32[4,512]{1,0:T(4,128)S(1)}, f32[4,512]{1,0:T(4,128)S(1)}, u32[]{:S(2)}, u32[]{:S(2)}) collective-permute-start(f32[4,512]{1,0:T(4,128)S(1)} %export.1), channel_id=1, source_target_pairs={{0,96},{96,0},{192,288},{288,192},{384,480},{480,384},{576,672},{6... | collective-permute-start | bytes 24584 | tf_op jit(solution)/shard_map/ppermute | solution.py:299
  16.7 15.5 %collective-permute-start.3 = (f32[3,4,512]{2,1,0:T(4,128)S(1)}, f32[3,4,512]{2,1,0:T(4,128)S(1)}, u32[]{:S(2)}, u32[]{:S(2)}) collective-permute-start(f32[3,4,512]{2,1,0:T(4,128)S(1)} %pad_maximum_fusion), channel_id=1, source_target_pairs={{0,95},{1,2},{2,1},{3,4},{4,3},{5,6},{6,5},{7,8},{8,7},{9,10},{10,... | collective-permute-start | bytes 73736 | tf_op jit(solution)/shard_map/ppermute | solution.py:299
  30.1 4.6 %collective-permute-start.2 = (f32[3,4,512]{2,1,0:T(4,128)S(1)}, f32[3,4,512]{2,1,0:T(4,128)S(1)}, u32[]{:S(2)}, u32[]{:S(2)}) collective-permute-start(f32[3,4,512]{2,1,0:T(4,128)S(1)} %pad_maximum_fusion), channel_id=1, source_target_pairs={{0,1},{1,0},{2,3},{3,2},{4,5},{5,4},{6,7},{7,6},{8,9},{9,8},{10,11... | collective-permute-start | bytes 73736 | tf_op jit(solution)/shard_map/ppermute | solution.py:299
  32.0 2.6 %copy-start.6 = (s32[1,1,512]{2,1,0:T(1,128)S(1)}, s32[1,1,512]{2,1,0:T(1,128)}, u32[]{:S(2)}) copy-start(s32[1,1,512]{2,1,0:T(1,128)} %refs_9_.1) | copy-start | bytes 6148
  32.0 2.6 %copy-start.5 = (s32[1,1,512]{2,1,0:T(1,128)S(1)}, s32[1,1,512]{2,1,0:T(1,128)}, u32[]{:S(2)}) copy-start(s32[1,1,512]{2,1,0:T(1,128)} %refs_8_.1) | copy-start | bytes 6148
  32.0 2.6 %copy-start.4 = (f32[8,128]{1,0:T(8,128)S(1)}, f32[8,128]{1,0:T(8,128)}, u32[]{:S(2)}) copy-start(f32[8,128]{1,0:T(8,128)} %refs_12_.1) | copy-start | bytes 12292
  32.1 2.6 %copy-start.3 = (f32[5,128]{1,0:T(8,128)S(1)}, f32[5,128]{1,0:T(8,128)}, u32[]{:S(2)}) copy-start(f32[5,128]{1,0:T(8,128)} %refs_11_.1) | copy-start | bytes 7684
  32.1 2.6 %copy-start.2 = (f32[5,128]{1,0:T(8,128)S(1)}, f32[5,128]{1,0:T(8,128)}, u32[]{:S(2)}) copy-start(f32[5,128]{1,0:T(8,128)} %refs_10_.1) | copy-start | bytes 7684
  32.1 2.6 %copy-start = (f32[3,1,1,512]{3,2,1,0:T(1,128)S(1)}, f32[3,1,1,512]{3,2,1,0:T(1,128)}, u32[]{:S(2)}) copy-start(f32[3,1,1,512]{3,2,1,0:T(1,128)} %refs_2_.1) | copy-start | bytes 18436
  32.1 2.6 %copy-start.1 = (s32[1,1,512]{2,1,0:T(1,128)S(1)}, s32[1,1,512]{2,1,0:T(1,128)}, u32[]{:S(2)}) copy-start(s32[1,1,512]{2,1,0:T(1,128)} %refs_3_.1) | copy-start | bytes 6148
  34.6 0.7 copy-start.7
  57.8 10.8 %all-to-all-start.1 = ((f32[8,40,128]{2,1,0:T(8,128)}), f32[8,40,128]{2,1,0:T(8,128)S(1)}, u32[]{:S(2)}, u32[]{:S(2)}) async-start(f32[8,40,128]{2,1,0:T(8,128)} %broadcast_in_dim.6), calls=%async_computation.1 | async-start | bytes 327680 | tf_op jit(solution)/shard_map/all_to_all | solution.py:303
  61.2 7.4 %collective-permute-start.4 = (f32[3,4,384]{2,1,0:T(4,128)S(1)}, f32[3,4,384]{2,1,0:T(4,128)S(1)}, u32[]{:S(2)}, u32[]{:S(2)}) collective-permute-start(f32[3,4,384]{2,1,0:T(4,128)S(1)} %get-tuple-element.20), channel_id=1, source_target_pairs={{0,672},{96,192},{192,96},{288,384},{384,288},{480,576},{576,480},... | collective-permute-start | bytes 55304 | tf_op jit(solution)/shard_map/ppermute | solution.py:299
  64.9 4.5 %collective-permute-start.5 = (f32[3,4,384]{2,1,0:T(4,128)S(1)}, f32[3,4,384]{2,1,0:T(4,128)S(1)}, u32[]{:S(2)}, u32[]{:S(2)}) collective-permute-start(f32[3,4,384]{2,1,0:T(4,128)S(1)} %get-tuple-element.21), channel_id=1, source_target_pairs={{0,96},{96,0},{192,288},{288,192},{384,480},{480,384},{576,672},{6... | collective-permute-start | bytes 55304 | tf_op jit(solution)/shard_map/ppermute | solution.py:299
  70.1 18.6 %all-to-all-start.2 = ((f32[12,40,128]{2,1,0:T(8,128)}), f32[12,40,128]{2,1,0:T(8,128)S(1)}, u32[]{:S(2)}, u32[]{:S(2)}) async-start(f32[12,40,128]{2,1,0:T(8,128)} %broadcast_in_dim.7), calls=%async_computation.2 | async-start | bytes 491520 | tf_op jit(solution)/shard_map/all_to_all | solution.py:303
  74.9 13.8 %collective-permute-start.7 = (f32[4,384]{1,0:T(4,128)S(1)}, f32[4,384]{1,0:T(4,128)S(1)}, u32[]{:S(2)}, u32[]{:S(2)}) collective-permute-start(f32[4,384]{1,0:T(4,128)S(1)} %get-tuple-element.32), channel_id=1, source_target_pairs={{0,1},{1,0},{2,3},{3,2},{4,5},{5,4},{6,7},{7,6},{8,9},{9,8},{10,11... | collective-permute-start | bytes 18440 | tf_op jit(solution)/shard_map/ppermute | solution.py:299
  77.4 12.5 %collective-permute-start.6 = (f32[4,384]{1,0:T(4,128)S(1)}, f32[4,384]{1,0:T(4,128)S(1)}, u32[]{:S(2)}, u32[]{:S(2)}) collective-permute-start(f32[4,384]{1,0:T(4,128)S(1)} %get-tuple-element.33), channel_id=1, source_target_pairs={{0,95},{1,2},{2,1},{3,4},{4,3},{5,6},{6,5},{7,8},{8,7},{9,10},{10,... | collective-permute-start | bytes 18440 | tf_op jit(solution)/shard_map/ppermute | solution.py:299
  90.6 11.0 %all-to-all-start.3 = ((f32[8,32,128]{2,1,0:T(8,128)}), f32[8,32,128]{2,1,0:T(8,128)S(1)}, u32[]{:S(2)}, u32[]{:S(2)}) async-start(f32[8,32,128]{2,1,0:T(8,128)} %broadcast_in_dim.8), calls=%async_computation.3 | async-start | bytes 262144 | tf_op jit(solution)/shard_map/all_to_all | solution.py:303

commit v4 on v3

--- a/solution.py
+++ b/solution.py
@@ -49,17 +49,56 @@
     return hi, mid, rest - mid
 
 
-def mm(a, b, dims):
-    return bdot(a[0], b[0], dims) + (bdot(a[0], b[1], dims) + bdot(a[1], b[0], dims))
-
-
-def mm6(a, b, dims):
-    small = bdot(a[0], b[2], dims) + bdot(a[1], b[1], dims) + bdot(a[2], b[0], dims)
-    return bdot(a[0], b[0], dims) + (bdot(a[0], b[1], dims) + bdot(a[1], b[0], dims) + small)
-
-
 def thirds(x):
     return tuple(part.astype(BF16) for part in split3(x))
+
+
+def stack(parts, axis):
+    return jnp.concatenate([part.astype(F32) for part in parts], axis=axis).astype(BF16)
+
+
+def halves(out):
+    return out[:, :LANES] + out[:, LANES:]
+
+
+def mm_square(a, b, dims):
+    left = jnp.concatenate(a, axis=1)
+    if dims == NN:
+        row = jnp.concatenate(b, axis=1)
+        return halves(bdot(left, jnp.concatenate([row, row], axis=0), NN))
+    column = jnp.concatenate(b, axis=0)
+    return halves(bdot(left, jnp.concatenate([column, column], axis=1), NT))
+
+
+def mm_wide(a, b):
+    return halves(bdot(a[0], jnp.concatenate(b, axis=1), NN)) + bdot(a[1], b[0], NN)
+
+
+def mm_turned(a, b):
+    out = bdot(jnp.concatenate(a, axis=1), jnp.concatenate(b, axis=1), TN)
+    return halves(out[:LANES] + out[LANES:])
+
+
+def mm_thin(a, b, dims):
+    count = a.shape[0]
+    rows = split2(a)
+    out = bdot(stack(rows, 0), b[0], dims)
+    return (out[:count] + out[count:]) + bdot(rows[0], b[1], dims)
+
+
+def mm_thin6(a, b, dims):
+    count = a.shape[0]
+    rows = thirds(a)
+    one = bdot(stack(rows, 0), b[0], dims)
+    two = bdot(stack(rows[:2], 0), b[1], dims)
+    small = one[2 * count :] + two[count:] + bdot(rows[0], b[2], dims)
+    return one[:count] + (one[count : 2 * count] + two[:count] + small)
+
+
+def mm_deep(a, b, pairs):
+    left = stack([a[i] for i, _ in pairs], 0)
+    right = stack([b[j] for _, j in pairs], 0)
+    return bdot(left, right, TN)
 
 
 def sigmoid(x):
@@ -195,11 +234,12 @@
 
     units = jnp.concatenate(unit + [zero] * 5, axis=0)
     units_s = split2(units)
-    cosine = mm(units_s, units_s, TN)
+    cosine = mm_deep(units_s, units_s, ((0, 1), (1, 0), (0, 0)))
     same = jnp.logical_and(centre_col == centre, live_col * live > 0.0)
     pairs = split2(jnp.where(same, cosine, 0.0))
 
-    summed = mm6(thirds(features), thirds(w_ref[...]), TN)
+    terms = ((0, 2), (1, 1), (2, 0), (0, 1), (1, 0), (0, 0))
+    summed = mm_deep(thirds(features), thirds(w_ref[...]), terms)
     gate0 = sigmoid(summed)
     first = summed * gate0
     latent = first * smooth_col
@@ -212,59 +252,61 @@
     saved = []
     for l in range(layers):
         env_s, mix_s = split2(envw_ref[l]), split2(mixw_ref[l])
-        weighted_s = split2(mm(split2(latent), env_s, NN))
-        back = mm(pairs, weighted_s, NN)
+        weighted_s = split2(mm_square(split2(latent), env_s, NN))
+        back = mm_wide(pairs, weighted_s)
         coupled_s = split2(latent * back)
-        pre = mm(coupled_s, mix_s, NN)
+        pre = mm_square(coupled_s, mix_s, NN)
         gate = sigmoid(pre)
         saved.append((env_s, mix_s, weighted_s, latent, back, coupled_s, pre, gate))
         latent = latent + pre * gate
 
     out_rows = jnp.broadcast_to(outw_ref[...], (8, LANES))
     latent_s = split2(latent)
-    readout = mm6(thirds(out_rows), thirds(latent), NT)[0:1]
+    readout = mm_thin6(out_rows, thirds(latent), NT)[0:1]
     energy = jnp.sum(weight * readout, axis=1, keepdims=True)
-    grad_out = mm(split2(jnp.concatenate([weight] + [zero] * 7, axis=0)), latent_s, NN)
+    grad_out = mm_thin(jnp.concatenate([weight] + [zero] * 7, axis=0), latent_s, NN)
 
     dlatent = weight_col * outw_ref[...]
-    dpairs = None
+    lefts, rights = [], []
     for l in reversed(range(layers)):
         env_s, mix_s, weighted_s, latent, back, coupled_s, pre, gate = saved[l]
         dpre_s = split2(dlatent * (gate * (1.0 + pre * (1.0 - gate))))
-        grad_mix = mm(coupled_s, dpre_s, TN) * share
+        grad_mix = mm_turned(coupled_s, dpre_s) * share
         step = min(chunk, LANES)
         for k in range(0, LANES, step):
             place, start = divmod(l * LANES + k, chunk)
             pack_ref[place, start : start + step, :] = grad_mix[k : k + step]
-        dcoupled = mm(dpre_s, mix_s, NT)
+        dcoupled = mm_square(dpre_s, mix_s, NT)
         dback_s = split2(dcoupled * latent)
-        term = mm(dback_s, weighted_s, NT)
-        dpairs = term if dpairs is None else dpairs + term
-        dweighted_s = split2(mm(pairs, dback_s, NN))
-        dlatent = dlatent + dcoupled * back + mm(dweighted_s, env_s, NT)
+        lefts += [dback_s[0], dback_s[1], dback_s[0]]
+        rights += [weighted_s[0], weighted_s[0], weighted_s[1]]
+        dweighted_s = split2(mm_wide(pairs, dback_s))
+        dlatent = dlatent + dcoupled * back + mm_square(dweighted_s, env_s, NT)
     row = iota((8, LANES), 0)
     tail = jnp.where(row == 0, grad_out[0:1], jnp.where(row == 1, energy, 0.0)) * share
     for k in range(pack_ref.shape[0]):
         pack_ref[k, chunk:, :] = tail
 
+    dpairs = bdot(jnp.concatenate(lefts, axis=1), jnp.concatenate(rights, axis=1), NT)
     dpairs_s = split2(jnp.where(same, dpairs, 0.0))
-    dunits = mm(units_s, dpairs_s, NT) + mm(units_s, dpairs_s, NN)
-    dfirst = dlatent * first
-    dsmooth = live * readout + mm(split2(jnp.ones((8, LANES), F32)), split2(dfirst), NT)[0:1]
+    dunits = mm_thin(units, dpairs_s, NT) + mm_thin(units, dpairs_s, NN)
+    dfirst_s = split2(dlatent * first)
+    ones = jnp.ones((8, LANES), F32).astype(BF16)
+    dsmooth = live * readout + (bdot(ones, dfirst_s[0], NT) + bdot(ones, dfirst_s[1], NT))[0:1]
     dsummed = dlatent * smooth_col * (gate0 * (1.0 + summed * (1.0 - gate0)))
-    dbasis = mm(split2(w_ref[0:8, :]), split2(dsummed), NT)
+    dbasis = mm_thin(w_ref[0:8, :], split2(dsummed), NT)
     dradius = jnp.sum(dbasis * slope, axis=0, keepdims=True) - dsmooth * (gap * radius * F32(4.0 / CUTOFF**2))
     along = dunits[0:1] * unit[0] + dunits[1:2] * unit[1] + dunits[2:3] * unit[2]
     radial = dradius - along * inverse
-    moves = []
+    units_in = in_lane.astype(F32).astype(BF16)
+    hot_b = hot.astype(BF16)
+    high, low = [], []
     for c in range(3):
         push = dunits[c : c + 1] * inverse + unit[c] * radial
-        moves.append(jnp.where(in_lane, jnp.concatenate([push, -push], axis=1), 0.0))
-    moves = split3(jnp.concatenate(moves, axis=0))
-    hot_b = hot.astype(BF16)
-    pool = (bdot(hot_b, moves[0].astype(BF16), NT) + bdot(hot_b, moves[1].astype(BF16), NT)) + bdot(
-        hot_b, moves[2].astype(BF16), NT
-    )
+        for parts, piece in zip((high, low), split2(push)):
+            wide = piece.astype(F32)
+            parts.append(units_in * jnp.concatenate([wide, -wide], axis=1).astype(BF16))
+    pool = bdot(hot_b, jnp.concatenate(high, axis=0), NT) + bdot(hot_b, jnp.concatenate(low, axis=0), NT)
     own_ref[...] = pool[0:own_rows]
     for s in range(9):
         rows = slice(own_rows + 4 * s, own_rows + 4 * s + 4)

time: 103 us -> 98.9 us (0.960)
  Pallas kernels: 13.4 us -> 9.38 us
    pallas_call x1, Pallas kernels: 11 us -> 6.95 us  [body(): pl.pallas_call(lambda *refs: main_kernel(*refs, blocks=edges // BLOCK_EDG...]
  transfers between devices with their start and end apart: 11 -> 11, of which waited for: 6 -> 6; matrix products, arithmetic and copies ran while one was open for 0% -> 0% of each run, Pallas kernels for 1% -> 2%
where the time goes in v4:
time: 98.9 us; the launch traced here: 98.2 us
  starting transfers between devices  61.4 us (62%)
  waiting for transfers between devices  12.2 us (12%)
  blocking collectives  10.8 us (11%)
  Pallas kernels  9.38 us (9%)
  local copies, waits for them, and re-layouts  3.37 us (3%)
    ppermute x8, starting transfers between devices, traded(): return lax.ppermute(block, axis, route)  47.6 us
    all_to_all x3, starting transfers between devices, exchanged(): return lax.all_to_all(shard, axes, 0, 0)  13.9 us
    all_to_all x1, blocking collectives, exchanged(): return lax.all_to_all(shard, axes, 0, 0)  10.8 us
    pallas_call x1, Pallas kernels, body(): pl.pallas_call(lambda *refs: main_kernel(*refs, blocks=edges // BLOCK_EDG...  6.95 us
    all_to_all x3, waiting for transfers between devices, exchanged(): return lax.all_to_all(shard, axes, 0, 0)  6.91 us
    ppermute x8, waiting for transfers between devices, traded(): return lax.ppermute(block, axis, route)  5.31 us
  transfers between devices with their start and end apart: 11, of which 6 were waited for; matrix products, arithmetic and copies ran while one was open for 0% of the time, Pallas kernels for 2%

profile of v4, /device:TPU:1, one launch (start us, length us, event | category | flops | bytes accessed | tf_op | source)
XLA Modules:
  0.0 98.2 jit_solution(16284164303291760022)
XLA Ops:
  0.6 0.9 export.1
  1.5 4.6 %collective-permute-start.1 = (f32[4,512]{1,0:T(4,128)S(1)}, f32[4,512]{1,0:T(4,128)S(1)}, u32[]{:S(2)}, u32[]{:S(2)}) collective-permute-start(f32[4,512]{1,0:T(4,128)S(1)} %export.1), channel_id=1, source_target_pairs={{0,672},{96,192},{192,96},{288,384},{384,288},{480,576},{576,480},... | collective-permute-start | bytes 24584 | tf_op jit(solution)/shard_map/ppermute | solution.py:341
  6.1 9.7 %collective-permute-start = (f32[4,512]{1,0:T(4,128)S(1)}, f32[4,512]{1,0:T(4,128)S(1)}, u32[]{:S(2)}, u32[]{:S(2)}) collective-permute-start(f32[4,512]{1,0:T(4,128)S(1)} %export.1), channel_id=1, source_target_pairs={{0,96},{96,0},{192,288},{288,192},{384,480},{480,384},{576,672},{6... | collective-permute-start | bytes 24584 | tf_op jit(solution)/shard_map/ppermute | solution.py:341
  15.9 0.8 collective-permute-done.refs_4_
  16.7 13.4 %collective-permute-start.3 = (f32[3,4,512]{2,1,0:T(4,128)S(1)}, f32[3,4,512]{2,1,0:T(4,128)S(1)}, u32[]{:S(2)}, u32[]{:S(2)}) collective-permute-start(f32[3,4,512]{2,1,0:T(4,128)S(1)} %pad_maximum_fusion), channel_id=1, source_target_pairs={{0,95},{1,2},{2,1},{3,4},{4,3},{5,6},{6,5},{7,8},{8,7},{9,10},{10,... | collective-permute-start | bytes 73736 | tf_op jit(solution)/shard_map/ppermute | solution.py:341
  30.1 1.9 %collective-permute-start.2 = (f32[3,4,512]{2,1,0:T(4,128)S(1)}, f32[3,4,512]{2,1,0:T(4,128)S(1)}, u32[]{:S(2)}, u32[]{:S(2)}) collective-permute-start(f32[3,4,512]{2,1,0:T(4,128)S(1)} %pad_maximum_fusion), channel_id=1, source_target_pairs={{0,1},{1,0},{2,3},{3,2},{4,5},{5,4},{6,7},{7,6},{8,9},{9,8},{10,11... | collective-permute-start | bytes 73736 | tf_op jit(solution)/shard_map/ppermute | solution.py:341
  32.0 0.0 copy-start.6
  32.0 0.0 copy-start.5
  32.0 0.0 copy-start.4
  32.1 0.0 copy-start.3
  32.1 0.0 copy-start
  32.1 0.0 copy-start.1
  32.1 2.5 %collective-permute-done.2.refs_6_ = f32[3,4,512]{2,1,0:T(4,128)S(1)} collective-permute-done((f32[3,4,512]{2,1,0:T(4,128)S(1)}, f32[3,4,512]{2,1,0:T(4,128)S(1)}, u32[]{:S(2)}, u32[]{:S(2)}) %collective-permute-start.2) | collective-permute-done | bytes 24608 | tf_op jit(solution)/shard_map/ppermute | solution.py:341
  34.7 0.6 copy-done.7
  35.3 7.0 %edges.1 = (f32[4,384]{1,0:T(4,128)S(1)}, f32[3,4,384]{2,1,0:T(4,128)S(1)}, f32[3,4,384]{2,1,0:T(4,128)S(1)}, f32[3,4,384]{2,1,0:T(4,128)S(1)}, f32[8,40,128]{2,1,0:T(8,128)S(1)}) custom-call(s32[1]{0:T(128)} %bitcast.refs_0_, s32[1,1,4]{2,1,0:T(1,128)} %refs_1_.1, f32[3,1,1,512]{3,2,1,0:T(1,128)S(1)} %copy-done, s32[1,1,512]{2,1,0:T(1,128)S(1)} %copy-done.1, ...), custom_call_target="tpu_custom_call" | custom-call | tf_op jit(solution)/shard_map/edges/pallas_call | solution.py:398
  42.2 10.8 %all_to_all.20 = f32[8,40,128]{2,1,0:T(8,128)S(1)} all-to-all(f32[8,40,128]{2,1,0:T(8,128)S(1)} %get-tuple-element.19), channel_id=1, replica_groups=mesh['gx_0'=4,'gx_1'=2,'gy_0'=2,'gy_1'=12,'gy_2'=4] {'gx_1','gy_2'}, dimensions={0} | all-to-all | bytes 327680 | tf_op jit(solution)/shard_map/all_to_all | solution.py:345
  53.1 0.7 broadcast_in_dim.6
  53.8 3.4 %all-to-all-start.1 = ((f32[8,40,128]{2,1,0:T(8,128)}), f32[8,40,128]{2,1,0:T(8,128)S(1)}, u32[]{:S(2)}, u32[]{:S(2)}) async-start(f32[8,40,128]{2,1,0:T(8,128)} %broadcast_in_dim.6), calls=%async_computation.1 | async-start | bytes 327680 | tf_op jit(solution)/shard_map/all_to_all | solution.py:345
  57.1 3.7 %collective-permute-start.4 = (f32[3,4,384]{2,1,0:T(4,128)S(1)}, f32[3,4,384]{2,1,0:T(4,128)S(1)}, u32[]{:S(2)}, u32[]{:S(2)}) collective-permute-start(f32[3,4,384]{2,1,0:T(4,128)S(1)} %get-tuple-element.20), channel_id=1, source_target_pairs={{0,672},{96,192},{192,96},{288,384},{384,288},{480,576},{576,480},... | collective-permute-start | bytes 55304 | tf_op jit(solution)/shard_map/ppermute | solution.py:341
  60.9 3.7 %collective-permute-start.5 = (f32[3,4,384]{2,1,0:T(4,128)S(1)}, f32[3,4,384]{2,1,0:T(4,128)S(1)}, u32[]{:S(2)}, u32[]{:S(2)}) collective-permute-start(f32[3,4,384]{2,1,0:T(4,128)S(1)} %get-tuple-element.21), channel_id=1, source_target_pairs={{0,96},{96,0},{192,288},{288,192},{384,480},{480,384},{576,672},{6... | collective-permute-start | bytes 55304 | tf_op jit(solution)/shard_map/ppermute | solution.py:341
  64.6 0.8 collective-permute-done.5.up_ref
  65.4 0.7 broadcast_in_dim.7
  66.1 4.7 %all-to-all-start.2 = ((f32[12,40,128]{2,1,0:T(8,128)}), f32[12,40,128]{2,1,0:T(8,128)S(1)}, u32[]{:S(2)}, u32[]{:S(2)}) async-start(f32[12,40,128]{2,1,0:T(8,128)} %broadcast_in_dim.7), calls=%async_computation.2 | async-start | bytes 491520 | tf_op jit(solution)/shard_map/all_to_all | solution.py:345
  70.8 2.6 %collective-permute-start.7 = (f32[4,384]{1,0:T(4,128)S(1)}, f32[4,384]{1,0:T(4,128)S(1)}, u32[]{:S(2)}, u32[]{:S(2)}) collective-permute-start(f32[4,384]{1,0:T(4,128)S(1)} %get-tuple-element.32), channel_id=1, source_target_pairs={{0,1},{1,0},{2,3},{3,2},{4,5},{5,4},{6,7},{7,6},{8,9},{9,8},{10,11... | collective-permute-start | bytes 18440 | tf_op jit(solution)/shard_map/ppermute | solution.py:341
  73.4 8.0 %collective-permute-start.6 = (f32[4,384]{1,0:T(4,128)S(1)}, f32[4,384]{1,0:T(4,128)S(1)}, u32[]{:S(2)}, u32[]{:S(2)}) collective-permute-start(f32[4,384]{1,0:T(4,128)S(1)} %get-tuple-element.33), channel_id=1, source_target_pairs={{0,95},{1,2},{2,1},{3,4},{4,3},{5,6},{6,5},{7,8},{8,7},{9,10},{10,... | collective-permute-start | bytes 18440 | tf_op jit(solution)/shard_map/ppermute | solution.py:341
  81.4 3.2 %all-to-all-done.2 = f32[12,40,128]{2,1,0:T(8,128)S(1)} async-done(((f32[12,40,128]{2,1,0:T(8,128)}), f32[12,40,128]{2,1,0:T(8,128)S(1)}, u32[]{:S(2)}, u32[]{:S(2)}) %all-to-all-start.2) | async-done | bytes 245792 | tf_op jit(solution)/shard_map/all_to_all | solution.py:345
  84.7 1.2 %collective-permute-done.6.left_ref = f32[4,384]{1,0:T(4,128)S(1)} collective-permute-done((f32[4,384]{1,0:T(4,128)S(1)}, f32[4,384]{1,0:T(4,128)S(1)}, u32[]{:S(2)}, u32[]{:S(2)}) %collective-permute-start.6) | collective-permute-done | bytes 6176 | tf_op jit(solution)/shard_map/ppermute | solution.py:341
  85.9 0.7 broadcast_in_dim.8
  86.6 5.8 %all-to-all-start.3 = ((f32[8,32,128]{2,1,0:T(8,128)}), f32[8,32,128]{2,1,0:T(8,128)S(1)}, u32[]{:S(2)}, u32[]{:S(2)}) async-start(f32[8,32,128]{2,1,0:T(8,128)} %broadcast_in_dim.8), calls=%async_computation.3 | async-start | bytes 262144 | tf_op jit(solution)/shard_map/all_to_all | solution.py:345
  92.3 1.5 %forces.1 = (f32[3,1,1,512]{3,2,1,0:T(1,128)}, f32[1,128]{1,0:T(1,128)}, f32[1,1]{1,0:T(1,128)}) custom-call(s32[1,1,384]{2,1,0:T(1,128)} %send_ref.3, f32[4,384]{1,0:T(4,128)S(1)} %get-tuple-element.18.own_ref, f32[3,4,384]{2,1,0:T(4,128)S(1)} %collective-permute-done.4.down_ref, f32[3,4,384]{2,1,0:T(4,128)S(1)} %collective-permute-done.5.up_ref, ...), custom_call_target="tpu_custom_call" | custom-call | tf_op jit(solution)/shard_map/forces/pallas_call | solution.py:448
  93.9 3.7 %all-to-all-done.3 = f32[8,32,128]{2,1,0:T(8,128)S(1)} async-done(((f32[8,32,128]{2,1,0:T(8,128)}), f32[8,32,128]{2,1,0:T(8,128)S(1)}, u32[]{:S(2)}, u32[]{:S(2)}) %all-to-all-start.3) | async-done | bytes 131104 | tf_op jit(solution)/shard_map/all_to_all | solution.py:345
  97.5 0.7 copy.17
  (21 shorter events, 0.1 us)
Async XLA Ops:
  1.5 14.3 %collective-permute-start.1 = (f32[4,512]{1,0:T(4,128)S(1)}, f32[4,512]{1,0:T(4,128)S(1)}, u32[]{:S(2)}, u32[]{:S(2)}) collective-permute-start(f32[4,512]{1,0:T(4,128)S(1)} %export.1), channel_id=1, source_target_pairs={{0,672},{96,192},{192,96},{288,384},{384,288},{480,576},{576,480},... | collective-permute-start | bytes 24584 | tf_op jit(solution)/shard_map/ppermute | solution.py:341
  6.1 10.5 %collective-permute-start = (f32[4,512]{1,0:T(4,128)S(1)}, f32[4,512]{1,0:T(4,128)S(1)}, u32[]{:S(2)}, u32[]{:S(2)}) collective-permute-start(f32[4,512]{1,0:T(4,128)S(1)} %export.1), channel_id=1, source_target_pairs={{0,96},{96,0},{192,288},{288,192},{384,480},{480,384},{576,672},{6... | collective-permute-start | bytes 24584 | tf_op jit(solution)/shard_map/ppermute | solution.py:341
  16.7 15.5 %collective-permute-start.3 = (f32[3,4,512]{2,1,0:T(4,128)S(1)}, f32[3,4,512]{2,1,0:T(4,128)S(1)}, u32[]{:S(2)}, u32[]{:S(2)}) collective-permute-start(f32[3,4,512]{2,1,0:T(4,128)S(1)} %pad_maximum_fusion), channel_id=1, source_target_pairs={{0,95},{1,2},{2,1},{3,4},{4,3},{5,6},{6,5},{7,8},{8,7},{9,10},{10,... | collective-permute-start | bytes 73736 | tf_op jit(solution)/shard_map/ppermute | solution.py:341
  30.1 4.6 %collective-permute-start.2 = (f32[3,4,512]{2,1,0:T(4,128)S(1)}, f32[3,4,512]{2,1,0:T(4,128)S(1)}, u32[]{:S(2)}, u32[]{:S(2)}) collective-permute-start(f32[3,4,512]{2,1,0:T(4,128)S(1)} %pad_maximum_fusion), channel_id=1, source_target_pairs={{0,1},{1,0},{2,3},{3,2},{4,5},{5,4},{6,7},{7,6},{8,9},{9,8},{10,11... | collective-permute-start | bytes 73736 | tf_op jit(solution)/shard_map/ppermute | solution.py:341
  32.0 2.6 %copy-start.6 = (s32[1,1,512]{2,1,0:T(1,128)S(1)}, s32[1,1,512]{2,1,0:T(1,128)}, u32[]{:S(2)}) copy-start(s32[1,1,512]{2,1,0:T(1,128)} %refs_9_.1) | copy-start | bytes 6148
  32.0 2.6 %copy-start.5 = (s32[1,1,512]{2,1,0:T(1,128)S(1)}, s32[1,1,512]{2,1,0:T(1,128)}, u32[]{:S(2)}) copy-start(s32[1,1,512]{2,1,0:T(1,128)} %refs_8_.1) | copy-start | bytes 6148
  32.0 2.6 %copy-start.4 = (f32[8,128]{1,0:T(8,128)S(1)}, f32[8,128]{1,0:T(8,128)}, u32[]{:S(2)}) copy-start(f32[8,128]{1,0:T(8,128)} %refs_12_.1) | copy-start | bytes 12292
  32.1 2.6 %copy-start.3 = (f32[5,128]{1,0:T(8,128)S(1)}, f32[5,128]{1,0:T(8,128)}, u32[]{:S(2)}) copy-start(f32[5,128]{1,0:T(8,128)} %refs_11_.1) | copy-start | bytes 7684
  32.1 2.6 %copy-start.2 = (f32[5,128]{1,0:T(8,128)S(1)}, f32[5,128]{1,0:T(8,128)}, u32[]{:S(2)}) copy-start(f32[5,128]{1,0:T(8,128)} %refs_10_.1) | copy-start | bytes 7684
  32.1 2.6 %copy-start = (f32[3,1,1,512]{3,2,1,0:T(1,128)S(1)}, f32[3,1,1,512]{3,2,1,0:T(1,128)}, u32[]{:S(2)}) copy-start(f32[3,1,1,512]{3,2,1,0:T(1,128)} %refs_2_.1) | copy-start | bytes 18436
  32.1 2.6 %copy-start.1 = (s32[1,1,512]{2,1,0:T(1,128)S(1)}, s32[1,1,512]{2,1,0:T(1,128)}, u32[]{:S(2)}) copy-start(s32[1,1,512]{2,1,0:T(1,128)} %refs_3_.1) | copy-start | bytes 6148
  34.6 0.7 copy-start.7
  53.8 10.8 %all-to-all-start.1 = ((f32[8,40,128]{2,1,0:T(8,128)}), f32[8,40,128]{2,1,0:T(8,128)S(1)}, u32[]{:S(2)}, u32[]{:S(2)}) async-start(f32[8,40,128]{2,1,0:T(8,128)} %broadcast_in_dim.6), calls=%async_computation.1 | async-start | bytes 327680 | tf_op jit(solution)/shard_map/all_to_all | solution.py:345
  57.1 7.4 %collective-permute-start.4 = (f32[3,4,384]{2,1,0:T(4,128)S(1)}, f32[3,4,384]{2,1,0:T(4,128)S(1)}, u32[]{:S(2)}, u32[]{:S(2)}) collective-permute-start(f32[3,4,384]{2,1,0:T(4,128)S(1)} %get-tuple-element.20), channel_id=1, source_target_pairs={{0,672},{96,192},{192,96},{288,384},{384,288},{480,576},{576,480},... | collective-permute-start | bytes 55304 | tf_op jit(solution)/shard_map/ppermute | solution.py:341
  60.9 4.5 %collective-permute-start.5 = (f32[3,4,384]{2,1,0:T(4,128)S(1)}, f32[3,4,384]{2,1,0:T(4,128)S(1)}, u32[]{:S(2)}, u32[]{:S(2)}) collective-permute-start(f32[3,4,384]{2,1,0:T(4,128)S(1)} %get-tuple-element.21), channel_id=1, source_target_pairs={{0,96},{96,0},{192,288},{288,192},{384,480},{480,384},{576,672},{6... | collective-permute-start | bytes 55304 | tf_op jit(solution)/shard_map/ppermute | solution.py:341
  66.1 18.6 %all-to-all-start.2 = ((f32[12,40,128]{2,1,0:T(8,128)}), f32[12,40,128]{2,1,0:T(8,128)S(1)}, u32[]{:S(2)}, u32[]{:S(2)}) async-start(f32[12,40,128]{2,1,0:T(8,128)} %broadcast_in_dim.7), calls=%async_computation.2 | async-start | bytes 491520 | tf_op jit(solution)/shard_map/all_to_all | solution.py:345
  70.8 13.8 %collective-permute-start.7 = (f32[4,384]{1,0:T(4,128)S(1)}, f32[4,384]{1,0:T(4,128)S(1)}, u32[]{:S(2)}, u32[]{:S(2)}) collective-permute-start(f32[4,384]{1,0:T(4,128)S(1)} %get-tuple-element.32), channel_id=1, source_target_pairs={{0,1},{1,0},{2,3},{3,2},{4,5},{5,4},{6,7},{7,6},{8,9},{9,8},{10,11... | collective-permute-start | bytes 18440 | tf_op jit(solution)/shard_map/ppermute | solution.py:341
  73.4 12.5 %collective-permute-start.6 = (f32[4,384]{1,0:T(4,128)S(1)}, f32[4,384]{1,0:T(4,128)S(1)}, u32[]{:S(2)}, u32[]{:S(2)}) collective-permute-start(f32[4,384]{1,0:T(4,128)S(1)} %get-tuple-element.33), channel_id=1, source_target_pairs={{0,95},{1,2},{2,1},{3,4},{4,3},{5,6},{6,5},{7,8},{8,7},{9,10},{10,... | collective-permute-start | bytes 18440 | tf_op jit(solution)/shard_map/ppermute | solution.py:341
  86.6 11.0 %all-to-all-start.3 = ((f32[8,32,128]{2,1,0:T(8,128)}), f32[8,32,128]{2,1,0:T(8,128)S(1)}, u32[]{:S(2)}, u32[]{:S(2)}) async-start(f32[8,32,128]{2,1,0:T(8,128)} %broadcast_in_dim.8), calls=%async_computation.3 | async-start | bytes 262144 | tf_op jit(solution)/shard_map/all_to_all | solution.py:345

commit v5 on v4

--- a/solution.py
+++ b/solution.py
@@ -103,6 +103,20 @@
 
 def sigmoid(x):
     return 1.0 / (1.0 + jnp.exp(-x))
+
+
+def pool_places(side_ref, neigh_ref, cent_ref, own_rows, total_rows):
+    turn_x = 2 * (side_ref[0] // 2) - 1
+    turn_y = 2 * (side_ref[0] % 2) - 1
+    ends = jnp.concatenate([neigh_ref[0], cent_ref[0]], axis=1)
+    count = ends.shape[1]
+    at_row = iota((total_rows, count), 0)
+    past = at_row - own_rows
+    slot = 3 * (1 + turn_x * (past // 12 - 1)) + 1 + turn_y * (past // 4 % 3 - 1)
+    holds = jnp.where(past < 0, at_row, jnp.where(past % 4 == 3, -1, own_rows + 3 * slot + past % 4))
+    hot = (holds == ends // LANES).astype(F32)
+    in_lane = iota((LANES, count), 0) == ends % LANES
+    return hot, in_lane
 
 
 def export_kernel(pos_ref, spec_ref, send_ref, out_ref):
@@ -133,16 +147,17 @@
     embc_ref,
     embn_ref,
     radw_ref,
-    outw_ref,
+    outw_hbm,
     envw_hbm,
     mixw_hbm,
-    own_ref,
-    a0_ref,
-    a1_ref,
-    a2_ref,
     pack_ref,
+    rows_ref,
+    columns_ref,
+    pieces_ref,
+    drift_ref,
     q_ref,
     w_ref,
+    outw_ref,
     envw_ref,
     mixw_ref,
     sems,
@@ -153,6 +168,7 @@
     loads = [
         pltpu.make_async_copy(envw_hbm, envw_ref, sems.at[0]),
         pltpu.make_async_copy(mixw_hbm, mixw_ref, sems.at[1]),
+        pltpu.make_async_copy(outw_hbm, outw_ref, sems.at[2]),
     ]
     for load in loads:
         load.start()
@@ -180,13 +196,7 @@
         q_ref[rows, :] = ghost + jnp.where(lane < LANES, shift_x, jnp.where(lane < 2 * LANES, shift_y, 0.0))
     total_rows = q_ref.shape[0]
 
-    ends = jnp.concatenate([neigh_ref[0], cent_ref[0]], axis=1)
-    at_row = iota((total_rows, 2 * edges), 0)
-    past = at_row - own_rows
-    slot = 3 * (1 + turn_x * (past // 12 - 1)) + 1 + turn_y * (past // 4 % 3 - 1)
-    holds = jnp.where(past < 0, at_row, jnp.where(past % 4 == 3, -1, own_rows + 3 * slot + past % 4))
-    hot = (holds == ends // LANES).astype(F32)
-    in_lane = iota((LANES, 2 * edges), 0) == ends % LANES
+    hot, in_lane = pool_places(side_ref, neigh_ref, cent_ref, own_rows, total_rows)
     table = jnp.concatenate(split3(q_ref[...]), axis=0).astype(BF16)
     hot3 = jnp.concatenate([hot, hot, hot], axis=0).astype(BF16)
     runs = bdot(table, hot3, TN)
@@ -230,6 +240,7 @@
     weight = live * smooth
     zero = jnp.zeros((1, edges), F32)
     columns = jnp.transpose(jnp.concatenate([smooth, weight, live, centre] + [zero] * 4, axis=0))
+    columns_ref[...] = columns
     smooth_col, weight_col, live_col, centre_col = (columns[:, k : k + 1] for k in range(4))
 
     units = jnp.concatenate(unit + [zero] * 5, axis=0)
@@ -267,7 +278,6 @@
     grad_out = mm_thin(jnp.concatenate([weight] + [zero] * 7, axis=0), latent_s, NN)
 
     dlatent = weight_col * outw_ref[...]
-    lefts, rights = [], []
     for l in reversed(range(layers)):
         env_s, mix_s, weighted_s, latent, back, coupled_s, pre, gate = saved[l]
         dpre_s = split2(dlatent * (gate * (1.0 + pre * (1.0 - gate))))
@@ -278,8 +288,8 @@
             pack_ref[place, start : start + step, :] = grad_mix[k : k + step]
         dcoupled = mm_square(dpre_s, mix_s, NT)
         dback_s = split2(dcoupled * latent)
-        lefts += [dback_s[0], dback_s[1], dback_s[0]]
-        rights += [weighted_s[0], weighted_s[0], weighted_s[1]]
+        for k, piece in enumerate(dback_s + weighted_s):
+            pieces_ref[4 * l + k] = piece
         dweighted_s = split2(mm_wide(pairs, dback_s))
         dlatent = dlatent + dcoupled * back + mm_square(dweighted_s, env_s, NT)
     row = iota((8, LANES), 0)
@@ -287,17 +297,51 @@
     for k in range(pack_ref.shape[0]):
         pack_ref[k, chunk:, :] = tail
 
+    drift_ref[0] = dlatent * first
+    drift_ref[1] = dlatent * smooth_col * (gate0 * (1.0 + summed * (1.0 - gate0)))
+    rows_ref[0:8, :] = slope
+    rows_ref[8:16, :] = jnp.concatenate(unit + [inverse, live, live * readout, gap * radius, centre], axis=0)
+
+
+def push_kernel(
+    side_ref,
+    cent_ref,
+    neigh_ref,
+    radw_ref,
+    rows_ref,
+    columns_ref,
+    pieces_ref,
+    drift_ref,
+    own_ref,
+    a0_ref,
+    a1_ref,
+    a2_ref,
+):
+    own_rows = own_ref.shape[0]
+    total_rows = own_rows + 36
+    edges = cent_ref.shape[2]
+    slope = rows_ref[0:8, :]
+    unit = [rows_ref[8 + c : 9 + c, :] for c in range(3)]
+    inverse, live, lived, widened, centre = (rows_ref[k : k + 1, :] for k in range(11, 16))
+    live_col, centre_col = columns_ref[:, 2:3], columns_ref[:, 3:4]
+    same = jnp.logical_and(centre_col == centre, live_col * live > 0.0)
+    units = jnp.concatenate(unit + [jnp.zeros((1, edges), F32)] * 5, axis=0)
+    lefts, rights = [], []
+    for l in range(pieces_ref.shape[0] // 4):
+        dback_s, weighted_s = (pieces_ref[4 * l], pieces_ref[4 * l + 1]), (pieces_ref[4 * l + 2], pieces_ref[4 * l + 3])
+        lefts += [dback_s[0], dback_s[1], dback_s[0]]
+        rights += [weighted_s[0], weighted_s[0], weighted_s[1]]
     dpairs = bdot(jnp.concatenate(lefts, axis=1), jnp.concatenate(rights, axis=1), NT)
     dpairs_s = split2(jnp.where(same, dpairs, 0.0))
     dunits = mm_thin(units, dpairs_s, NT) + mm_thin(units, dpairs_s, NN)
-    dfirst_s = split2(dlatent * first)
+    dfirst_s = split2(drift_ref[0])
     ones = jnp.ones((8, LANES), F32).astype(BF16)
-    dsmooth = live * readout + (bdot(ones, dfirst_s[0], NT) + bdot(ones, dfirst_s[1], NT))[0:1]
-    dsummed = dlatent * smooth_col * (gate0 * (1.0 + summed * (1.0 - gate0)))
-    dbasis = mm_thin(w_ref[0:8, :], split2(dsummed), NT)
-    dradius = jnp.sum(dbasis * slope, axis=0, keepdims=True) - dsmooth * (gap * radius * F32(4.0 / CUTOFF**2))
+    dsmooth = lived + (bdot(ones, dfirst_s[0], NT) + bdot(ones, dfirst_s[1], NT))[0:1]
+    dbasis = mm_thin(radw_ref[...], split2(drift_ref[1]), NT)
+    dradius = jnp.sum(dbasis * slope, axis=0, keepdims=True) - dsmooth * (widened * F32(4.0 / CUTOFF**2))
     along = dunits[0:1] * unit[0] + dunits[1:2] * unit[1] + dunits[2:3] * unit[2]
     radial = dradius - along * inverse
+    hot, in_lane = pool_places(side_ref, neigh_ref, cent_ref, own_rows, total_rows)
     units_in = in_lane.astype(F32).astype(BF16)
     hot_b = hot.astype(BF16)
     high, low = [], []
@@ -341,13 +385,30 @@
     return lax.ppermute(block, axis, route)
 
 
+def sum_kernel(in_ref, *out_refs):
+    total = in_ref[0]
+    for k in range(1, in_ref.shape[0]):
+        total = total + in_ref[k]
+    rows = out_refs[0].shape[1]
+    for k in range(out_refs[0].shape[0]):
+        out_refs[0][k] = total[:rows]
+    if len(out_refs) > 1:
+        out_refs[1][...] = total[rows:]
+
+
+def summed(copies, *shapes):
+    vmem = pl.BlockSpec(memory_space=pltpu.VMEM)
+    return pl.pallas_call(
+        sum_kernel,
+        out_shape=tuple(pltpu.VMEM(shape, F32) for shape in shapes),
+        in_specs=[vmem],
+        out_specs=(vmem,) * len(shapes),
+        name="sums",
+    )(pltpu.with_memory_space_constraint(copies, pltpu.VMEM))
+
+
 def exchanged(shard, axes):
     return lax.all_to_all(shard, axes, 0, 0)
-
-
-def summed_over(shard, axes):
-    copies = jnp.broadcast_to(shard[None], (lax.axis_size(axes),) + shard.shape)
-    return jnp.sum(exchanged(copies, axes), axis=0)
 
 
 def body(
@@ -395,23 +456,26 @@
     ya = traded(column, GY, 0)
 
     piece = result(3, 4, 3 * LANES)
-    own, a0, a1, a2, pack = pl.pallas_call(
+    scalars = pl.BlockSpec(memory_space=pltpu.SMEM)
+    anywhere = pl.BlockSpec(memory_space=pl.ANY)
+    pack, *kept = pl.pallas_call(
         lambda *refs: main_kernel(*refs, blocks=edges // BLOCK_EDGES, devices=devices),
         out_shape=(
-            result(own_rows, 3 * LANES),
-            piece,
-            piece,
-            piece,
             result(near, chunk + 8, LANES),
+            result(16, edges),
+            result(edges, 8),
+            pltpu.VMEM((4 * layers, edges, LANES), BF16),
+            result(2, edges, LANES),
         ),
-        in_specs=[pl.BlockSpec(memory_space=pltpu.SMEM)] * 2 + [vmem] * 12 + [pl.BlockSpec(memory_space=pl.ANY)] * 2,
+        in_specs=[scalars] * 2 + [vmem] * 11 + [anywhere] * 3,
         out_specs=(vmem,) * 5,
         scratch_shapes=[
             pltpu.VMEM((own_rows + 36, 4 * LANES), F32),
             pltpu.VMEM((24, LANES), F32),
+            pltpu.VMEM((1, LANES), F32),
             pltpu.VMEM(env_w.shape, F32),
             pltpu.VMEM(mix_w.shape, F32),
-            pltpu.SemaphoreType.DMA((2,)),
+            pltpu.SemaphoreType.DMA((3,)),
         ],
         name="edges",
     )(
@@ -429,22 +493,33 @@
             emb_center,
             emb_neighbour,
             radial_w,
-            out_w.reshape(1, LANES),
         ),
+        out_w.reshape(1, LANES),
         env_w,
         mix_w,
     )
-
+    parts = exchanged(pack, NEAR)
+    own, a0, a1, a2 = pl.pallas_call(
+        push_kernel,
+        out_shape=(result(own_rows, 3 * LANES), piece, piece, piece),
+        in_specs=[scalars] + [vmem] * 7,
+        out_specs=(vmem,) * 4,
+        cost_estimate=pl.CostEstimate(flops=1_000_000_000, bytes_accessed=2_000_000, transcendentals=0),
+        name="pushes",
+    )(side, *near_by(edge_centers, edge_neighbours, radial_w, *kept))
+
+    parts, own, a0, a1, a2 = lax.optimization_barrier((parts, own, a0, a1, a2))
+    (copies,) = summed(parts, (lax.axis_size(MIDDLE), chunk + 8, LANES))
     over = traded(a2, GX, 1), traded(a0, GX, 0)
-    part = jnp.sum(exchanged(pack, NEAR), axis=0)
-    part = summed_over(part, MIDDLE)
-    part, over = lax.optimization_barrier((part, over))
+    (copies,) = summed(exchanged(copies, MIDDLE), (lax.axis_size(FAR), chunk + 8, LANES))
+    copies, over = lax.optimization_barrier((copies, over))
     across = (
         traded(a1[2] + over[0][2] + over[1][2], GY, 1),
         traded(a1[0] + over[0][0] + over[1][0], GY, 0),
     )
-    part = summed_over(part, FAR)
-    part, across = lax.optimization_barrier((part, across))
+    parts = exchanged(copies, FAR)
+    parts, across = lax.optimization_barrier((parts, across))
+    shared, rest = summed(parts, (near, chunk, LANES), (8, LANES))
     forces, grad_out, energy = pl.pallas_call(
         force_kernel,
         out_shape=(
@@ -455,8 +530,7 @@
         in_specs=[vmem] * 7,
         out_specs=(vmem,) * 3,
         name="forces",
-    )(send_index, *near_by(own, *over, *across, part[chunk:]))
-    shared = jnp.broadcast_to(part[None, :chunk], (near, chunk, LANES))
+    )(send_index, *near_by(own, *over, *across, rest))
     grad_mix = exchanged(shared, NEAR).reshape(layers, LANES, LANES)
     return forces, grad_mix, grad_out.reshape(LANES), energy.reshape(())
 

time: 98.9 us -> 100 us (1.011)
  blocking collectives: 10.8 us -> 0 us
  starting transfers between devices: 61.4 us -> 71.7 us
  Pallas kernels: 9.38 us -> 12.1 us
  local copies, waits for them, and re-layouts: 3.37 us -> 0.7 us
  waiting for transfers between devices: 12.2 us -> 14.1 us
    all_to_all x1 -> x0, blocking collectives: 10.8 us -> none  [exchanged(): return lax.all_to_all(shard, axes, 0, 0)]
    all_to_all x3 -> x4, starting transfers between devices: 13.9 us -> 24.2 us  [exchanged(): return lax.all_to_all(shard, axes, 0, 0)]
    pallas_call x0 -> x4, Pallas kernels: none -> 4.12 us  [the longest x3 2.08 us: summed(): pl.pallas_call(sum_kernel, out_shape=tuple((pltpu.VMEM(shape, F32) for sh...]
    broadcast_in_dim x3 -> x0, local copies, waits for them, and re-layouts: 2.07 us -> none  [the longest x2 1.4 us: summed_over(): copies = jnp.broadcast_to(shard[None], (lax.axis_size(axes),) + shard.shape)]
    ppermute x8, waiting for transfers between devices: 5.31 us -> 7.02 us  [traded(): return lax.ppermute(block, axis, route)]
    pallas_call x1, Pallas kernels: 6.95 us -> 5.55 us  [body(): pl.pallas_call(lambda *refs: main_kernel(*refs, blocks=edges // BLOCK_EDG...]
    all_to_all x3 -> x4, waiting for transfers between devices: 6.91 us -> 7.13 us  [exchanged(): return lax.all_to_all(shard, axes, 0, 0)]
  transfers between devices with their start and end apart: 11 -> 12, of which waited for: 6 -> 7; matrix products, arithmetic and copies ran while one was open for 0% -> 0% of each run, Pallas kernels for 2% -> 4%
where the time goes in v5:
time: 100 us; the launch traced here: 99.5 us
  starting transfers between devices  71.7 us (72%)
  waiting for transfers between devices  14.1 us (14%)
  Pallas kernels  12.1 us (12%)
    ppermute x8, starting transfers between devices, traded(): return lax.ppermute(block, axis, route)  47.5 us
    all_to_all x4, starting transfers between devices, exchanged(): return lax.all_to_all(shard, axes, 0, 0)  24.2 us
    all_to_all x4, waiting for transfers between devices, exchanged(): return lax.all_to_all(shard, axes, 0, 0)  7.13 us
    ppermute x8, waiting for transfers between devices, traded(): return lax.ppermute(block, axis, route)  7.02 us
    pallas_call x1, Pallas kernels, body(): pl.pallas_call(lambda *refs: main_kernel(*refs, blocks=edges // BLOCK_EDG...  5.55 us
    pallas_call x3, Pallas kernels, summed(): pl.pallas_call(sum_kernel, out_shape=tuple((pltpu.VMEM(shape, F32) for sh...  2.08 us
    pallas_call x1, Pallas kernels, body(): pl.pallas_call(push_kernel, out_shape=(result(own_rows, 3 * LANES), piece...  2.04 us
  transfers between devices with their start and end apart: 12, of which 7 were waited for; matrix products, arithmetic and copies ran while one was open for 0% of the time, Pallas kernels for 4%

profile of v5, /device:TPU:1, one launch (start us, length us, event | category | flops | bytes accessed | tf_op | source)
XLA Modules:
  0.0 99.5 jit_solution(11520459471001588210)
XLA Ops:
  0.6 0.9 export.1
  1.5 12.4 %collective-permute-start = (f32[4,512]{1,0:T(4,128)S(1)}, f32[4,512]{1,0:T(4,128)S(1)}, u32[]{:S(2)}, u32[]{:S(2)}) collective-permute-start(f32[4,512]{1,0:T(4,128)S(1)} %export.1), channel_id=1, source_target_pairs={{0,96},{96,0},{192,288},{288,192},{384,480},{480,384},{576,672},{6... | collective-permute-start | bytes 24584 | tf_op jit(solution)/shard_map/ppermute | solution.py:385
  13.9 1.9 %collective-permute-start.1 = (f32[4,512]{1,0:T(4,128)S(1)}, f32[4,512]{1,0:T(4,128)S(1)}, u32[]{:S(2)}, u32[]{:S(2)}) collective-permute-start(f32[4,512]{1,0:T(4,128)S(1)} %export.1), channel_id=1, source_target_pairs={{0,672},{96,192},{192,96},{288,384},{384,288},{480,576},{576,480},... | collective-permute-start | bytes 24584 | tf_op jit(solution)/shard_map/ppermute | solution.py:385
  15.9 3.0 %collective-permute-done.1.refs_5_ = f32[4,512]{1,0:T(4,128)S(1)} collective-permute-done((f32[4,512]{1,0:T(4,128)S(1)}, f32[4,512]{1,0:T(4,128)S(1)}, u32[]{:S(2)}, u32[]{:S(2)}) %collective-permute-start.1) | collective-permute-done | bytes 8224 | tf_op jit(solution)/shard_map/ppermute | solution.py:385
  18.9 1.9 %collective-permute-start.2 = (f32[3,4,512]{2,1,0:T(4,128)S(1)}, f32[3,4,512]{2,1,0:T(4,128)S(1)}, u32[]{:S(2)}, u32[]{:S(2)}) collective-permute-start(f32[3,4,512]{2,1,0:T(4,128)S(1)} %pad_maximum_fusion), channel_id=1, source_target_pairs={{0,1},{1,0},{2,3},{3,2},{4,5},{5,4},{6,7},{7,6},{8,9},{9,8},{10,11... | collective-permute-start | bytes 73736 | tf_op jit(solution)/shard_map/ppermute | solution.py:385
  20.8 13.3 %collective-permute-start.3 = (f32[3,4,512]{2,1,0:T(4,128)S(1)}, f32[3,4,512]{2,1,0:T(4,128)S(1)}, u32[]{:S(2)}, u32[]{:S(2)}) collective-permute-start(f32[3,4,512]{2,1,0:T(4,128)S(1)} %pad_maximum_fusion), channel_id=1, source_target_pairs={{0,95},{1,2},{2,1},{3,4},{4,3},{5,6},{6,5},{7,8},{8,7},{9,10},{10,... | collective-permute-start | bytes 73736 | tf_op jit(solution)/shard_map/ppermute | solution.py:385
  34.2 0.0 copy-start.6
  34.2 0.0 copy-start.5
  34.2 0.0 copy-start.4
  34.2 0.0 copy-start.2
  34.3 0.0 copy-start.1
  34.3 1.2 %collective-permute-done.3.refs_7_ = f32[3,4,512]{2,1,0:T(4,128)S(1)} collective-permute-done((f32[3,4,512]{2,1,0:T(4,128)S(1)}, f32[3,4,512]{2,1,0:T(4,128)S(1)}, u32[]{:S(2)}, u32[]{:S(2)}) %collective-permute-start.3) | collective-permute-done | bytes 24608 | tf_op jit(solution)/shard_map/ppermute | solution.py:385
  35.5 5.5 %edges.1 = (f32[8,40,128]{2,1,0:T(8,128)}, f32[16,512]{1,0:T(8,128)S(1)}, f32[512,8]{1,0:T(8,128)S(1)}, bf16[8,512,128]{2,1,0:T(8,128)(2,1)S(1)}, f32[2,512,128]{2,1,0:T(8,128)S(1)}) custom-call(s32[1]{0:T(128)} %bitcast.refs_0_.side_ref, s32[1,1,4]{2,1,0:T(1,128)} %refs_1_.1, f32[3,1,1,512]{3,2,1,0:T(1,128)S(1)} %copy-done, s32[1,1,512]{2,1,0:T(1,128)S(1)} %copy-done.1, ...), custom_call_target="tpu_custom_call" | custom-call | tf_op jit(solution)/shard_map/edges/pallas_call | solution.py:461
  41.0 6.2 %all-to-all-start = ((f32[8,40,128]{2,1,0:T(8,128)}), f32[8,40,128]{2,1,0:T(8,128)S(1)}, u32[]{:S(2)}, u32[]{:S(2)}) async-start(f32[8,40,128]{2,1,0:T(8,128)} %get-tuple-element.29), calls=%async_computation | async-start | bytes 327680 | tf_op jit(solution)/shard_map/all_to_all | solution.py:411
  47.2 2.0 %pushes.1 = (f32[4,384]{1,0:T(4,128)S(1)}, f32[3,4,384]{2,1,0:T(4,128)S(1)}, f32[3,4,384]{2,1,0:T(4,128)S(1)}, f32[3,4,384]{2,1,0:T(4,128)S(1)}) custom-call(s32[1]{0:T(128)} %bitcast.refs_0_.side_ref, s32[1,1,512]{2,1,0:T(1,128)S(1)} %copy-done.5, s32[1,1,512]{2,1,0:T(1,128)S(1)} %copy-done.6, f32[8,128]{1,0:T(8,128)S(1)} %copy-done.4, ...), custom_call_target="tpu_custom_call" | custom-call | flops 1000000000 | bytes 2000000 | tf_op jit(solution)/shard_map/pushes/pallas_call | solution.py:502
  49.3 3.5 %all-to-all-done.in_ref = f32[8,40,128]{2,1,0:T(8,128)S(1)} async-done(((f32[8,40,128]{2,1,0:T(8,128)}), f32[8,40,128]{2,1,0:T(8,128)S(1)}, u32[]{:S(2)}, u32[]{:S(2)}) %all-to-all-start) | async-done | bytes 163872 | tf_op jit(solution)/shard_map/all_to_all | solution.py:411
  52.7 0.7 sums.3
  53.4 3.4 %all-to-all-start.1 = ((f32[8,40,128]{2,1,0:T(8,128)}), f32[8,40,128]{2,1,0:T(8,128)S(1)}, u32[]{:S(2)}, u32[]{:S(2)}) async-start(f32[8,40,128]{2,1,0:T(8,128)} %sums.3), calls=%async_computation.1 | async-start | bytes 327680 | tf_op jit(solution)/shard_map/all_to_all | solution.py:411
  56.8 3.7 %collective-permute-start.4 = (f32[3,4,384]{2,1,0:T(4,128)S(1)}, f32[3,4,384]{2,1,0:T(4,128)S(1)}, u32[]{:S(2)}, u32[]{:S(2)}) collective-permute-start(f32[3,4,384]{2,1,0:T(4,128)S(1)} %get-tuple-element.40), channel_id=1, source_target_pairs={{0,672},{96,192},{192,96},{288,384},{384,288},{480,576},{576,480},... | collective-permute-start | bytes 55304 | tf_op jit(solution)/shard_map/ppermute | solution.py:385
  60.5 3.7 %collective-permute-start.5 = (f32[3,4,384]{2,1,0:T(4,128)S(1)}, f32[3,4,384]{2,1,0:T(4,128)S(1)}, u32[]{:S(2)}, u32[]{:S(2)}) collective-permute-start(f32[3,4,384]{2,1,0:T(4,128)S(1)} %get-tuple-element.41), channel_id=1, source_target_pairs={{0,96},{96,0},{192,288},{288,192},{384,480},{480,384},{576,672},{6... | collective-permute-start | bytes 55304 | tf_op jit(solution)/shard_map/ppermute | solution.py:385
  64.2 0.7 sums.4
  64.9 0.1 collective-permute-done.5.up_ref
  65.0 7.9 %all-to-all-start.2 = ((f32[12,40,128]{2,1,0:T(8,128)}), f32[12,40,128]{2,1,0:T(8,128)S(1)}, u32[]{:S(2)}, u32[]{:S(2)}) async-start(f32[12,40,128]{2,1,0:T(8,128)} %sums.4), calls=%async_computation.2 | async-start | bytes 491520 | tf_op jit(solution)/shard_map/all_to_all | solution.py:411
  73.0 8.6 %collective-permute-start.6 = (f32[4,384]{1,0:T(4,128)S(1)}, f32[4,384]{1,0:T(4,128)S(1)}, u32[]{:S(2)}, u32[]{:S(2)}) collective-permute-start(f32[4,384]{1,0:T(4,128)S(1)} %get-tuple-element.55), channel_id=1, source_target_pairs={{0,95},{1,2},{2,1},{3,4},{4,3},{5,6},{6,5},{7,8},{8,7},{9,10},{10,... | collective-permute-start | bytes 18440 | tf_op jit(solution)/shard_map/ppermute | solution.py:385
  81.6 1.9 %collective-permute-start.7 = (f32[4,384]{1,0:T(4,128)S(1)}, f32[4,384]{1,0:T(4,128)S(1)}, u32[]{:S(2)}, u32[]{:S(2)}) collective-permute-start(f32[4,384]{1,0:T(4,128)S(1)} %get-tuple-element.54), channel_id=1, source_target_pairs={{0,1},{1,0},{2,3},{3,2},{4,5},{5,4},{6,7},{7,6},{8,9},{9,8},{10,11... | collective-permute-start | bytes 18440 | tf_op jit(solution)/shard_map/ppermute | solution.py:385
  83.5 2.0 %collective-permute-done.6.left_ref = f32[4,384]{1,0:T(4,128)S(1)} collective-permute-done((f32[4,384]{1,0:T(4,128)S(1)}, f32[4,384]{1,0:T(4,128)S(1)}, u32[]{:S(2)}, u32[]{:S(2)}) %collective-permute-start.6) | collective-permute-done | bytes 6176 | tf_op jit(solution)/shard_map/ppermute | solution.py:385
  85.6 0.7 collective-permute-done.7.right_ref
  86.3 0.7 sums.5
  87.0 6.7 %all-to-all-start.3 = ((f32[8,32,128]{2,1,0:T(8,128)}), f32[8,32,128]{2,1,0:T(8,128)S(1)}, u32[]{:S(2)}, u32[]{:S(2)}) async-start(f32[8,32,128]{2,1,0:T(8,128)} %get-tuple-element.51), calls=%async_computation.3 | async-start | bytes 262144 | tf_op jit(solution)/shard_map/all_to_all | solution.py:411
  93.7 1.5 %forces.1 = (f32[3,1,1,512]{3,2,1,0:T(1,128)}, f32[1,128]{1,0:T(1,128)}, f32[1,1]{1,0:T(1,128)}) custom-call(s32[1,1,384]{2,1,0:T(1,128)} %send_ref.3, f32[4,384]{1,0:T(4,128)S(1)} %get-tuple-element.38.own_ref, f32[3,4,384]{2,1,0:T(4,128)S(1)} %collective-permute-done.4.down_ref, f32[3,4,384]{2,1,0:T(4,128)S(1)} %collective-permute-done.5.up_ref, ...), custom_call_target="tpu_custom_call" | custom-call | tf_op jit(solution)/shard_map/forces/pallas_call | solution.py:523
  95.2 3.7 %all-to-all-done.3 = f32[8,32,128]{2,1,0:T(8,128)S(1)} async-done(((f32[8,32,128]{2,1,0:T(8,128)}), f32[8,32,128]{2,1,0:T(8,128)S(1)}, u32[]{:S(2)}, u32[]{:S(2)}) %all-to-all-start.3) | async-done | bytes 131104 | tf_op jit(solution)/shard_map/all_to_all | solution.py:411
  98.9 0.7 copy.17
  (16 shorter events, 0.1 us)
Async XLA Ops:
  1.5 14.3 %collective-permute-start = (f32[4,512]{1,0:T(4,128)S(1)}, f32[4,512]{1,0:T(4,128)S(1)}, u32[]{:S(2)}, u32[]{:S(2)}) collective-permute-start(f32[4,512]{1,0:T(4,128)S(1)} %export.1), channel_id=1, source_target_pairs={{0,96},{96,0},{192,288},{288,192},{384,480},{480,384},{576,672},{6... | collective-permute-start | bytes 24584 | tf_op jit(solution)/shard_map/ppermute | solution.py:385
  13.9 5.0 %collective-permute-start.1 = (f32[4,512]{1,0:T(4,128)S(1)}, f32[4,512]{1,0:T(4,128)S(1)}, u32[]{:S(2)}, u32[]{:S(2)}) collective-permute-start(f32[4,512]{1,0:T(4,128)S(1)} %export.1), channel_id=1, source_target_pairs={{0,672},{96,192},{192,96},{288,384},{384,288},{480,576},{576,480},... | collective-permute-start | bytes 24584 | tf_op jit(solution)/shard_map/ppermute | solution.py:385
  18.9 15.4 %collective-permute-start.2 = (f32[3,4,512]{2,1,0:T(4,128)S(1)}, f32[3,4,512]{2,1,0:T(4,128)S(1)}, u32[]{:S(2)}, u32[]{:S(2)}) collective-permute-start(f32[3,4,512]{2,1,0:T(4,128)S(1)} %pad_maximum_fusion), channel_id=1, source_target_pairs={{0,1},{1,0},{2,3},{3,2},{4,5},{5,4},{6,7},{7,6},{8,9},{9,8},{10,11... | collective-permute-start | bytes 73736 | tf_op jit(solution)/shard_map/ppermute | solution.py:385
  20.8 14.6 %collective-permute-start.3 = (f32[3,4,512]{2,1,0:T(4,128)S(1)}, f32[3,4,512]{2,1,0:T(4,128)S(1)}, u32[]{:S(2)}, u32[]{:S(2)}) collective-permute-start(f32[3,4,512]{2,1,0:T(4,128)S(1)} %pad_maximum_fusion), channel_id=1, source_target_pairs={{0,95},{1,2},{2,1},{3,4},{4,3},{5,6},{6,5},{7,8},{8,7},{9,10},{10,... | collective-permute-start | bytes 73736 | tf_op jit(solution)/shard_map/ppermute | solution.py:385
  34.2 1.3 %copy-start.6 = (s32[1,1,512]{2,1,0:T(1,128)S(1)}, s32[1,1,512]{2,1,0:T(1,128)}, u32[]{:S(2)}) copy-start(s32[1,1,512]{2,1,0:T(1,128)} %neigh_ref.1) | copy-start | bytes 6148
  34.2 1.3 %copy-start.5 = (s32[1,1,512]{2,1,0:T(1,128)S(1)}, s32[1,1,512]{2,1,0:T(1,128)}, u32[]{:S(2)}) copy-start(s32[1,1,512]{2,1,0:T(1,128)} %cent_ref.1) | copy-start | bytes 6148
  34.2 1.2 %copy-start.4 = (f32[8,128]{1,0:T(8,128)S(1)}, f32[8,128]{1,0:T(8,128)}, u32[]{:S(2)}) copy-start(f32[8,128]{1,0:T(8,128)} %radw_ref.1) | copy-start | bytes 12292
  34.2 1.2 %copy-start.3 = (f32[5,128]{1,0:T(8,128)S(1)}, f32[5,128]{1,0:T(8,128)}, u32[]{:S(2)}) copy-start(f32[5,128]{1,0:T(8,128)} %refs_11_.1) | copy-start | bytes 7684
  34.2 1.2 %copy-start.2 = (f32[5,128]{1,0:T(8,128)S(1)}, f32[5,128]{1,0:T(8,128)}, u32[]{:S(2)}) copy-start(f32[5,128]{1,0:T(8,128)} %refs_10_.1) | copy-start | bytes 7684
  34.2 1.2 %copy-start = (f32[3,1,1,512]{3,2,1,0:T(1,128)S(1)}, f32[3,1,1,512]{3,2,1,0:T(1,128)}, u32[]{:S(2)}) copy-start(f32[3,1,1,512]{3,2,1,0:T(1,128)} %refs_2_.1) | copy-start | bytes 18436
  34.3 1.2 %copy-start.1 = (s32[1,1,512]{2,1,0:T(1,128)S(1)}, s32[1,1,512]{2,1,0:T(1,128)}, u32[]{:S(2)}) copy-start(s32[1,1,512]{2,1,0:T(1,128)} %refs_3_.1) | copy-start | bytes 6148
  41.0 11.7 %all-to-all-start = ((f32[8,40,128]{2,1,0:T(8,128)}), f32[8,40,128]{2,1,0:T(8,128)S(1)}, u32[]{:S(2)}, u32[]{:S(2)}) async-start(f32[8,40,128]{2,1,0:T(8,128)} %get-tuple-element.29), calls=%async_computation | async-start | bytes 327680 | tf_op jit(solution)/shard_map/all_to_all | solution.py:411
  53.4 10.8 %all-to-all-start.1 = ((f32[8,40,128]{2,1,0:T(8,128)}), f32[8,40,128]{2,1,0:T(8,128)S(1)}, u32[]{:S(2)}, u32[]{:S(2)}) async-start(f32[8,40,128]{2,1,0:T(8,128)} %sums.3), calls=%async_computation.1 | async-start | bytes 327680 | tf_op jit(solution)/shard_map/all_to_all | solution.py:411
  56.8 8.1 %collective-permute-start.4 = (f32[3,4,384]{2,1,0:T(4,128)S(1)}, f32[3,4,384]{2,1,0:T(4,128)S(1)}, u32[]{:S(2)}, u32[]{:S(2)}) collective-permute-start(f32[3,4,384]{2,1,0:T(4,128)S(1)} %get-tuple-element.40), channel_id=1, source_target_pairs={{0,672},{96,192},{192,96},{288,384},{384,288},{480,576},{576,480},... | collective-permute-start | bytes 55304 | tf_op jit(solution)/shard_map/ppermute | solution.py:385
  60.5 4.5 %collective-permute-start.5 = (f32[3,4,384]{2,1,0:T(4,128)S(1)}, f32[3,4,384]{2,1,0:T(4,128)S(1)}, u32[]{:S(2)}, u32[]{:S(2)}) collective-permute-start(f32[3,4,384]{2,1,0:T(4,128)S(1)} %get-tuple-element.41), channel_id=1, source_target_pairs={{0,96},{96,0},{192,288},{288,192},{384,480},{480,384},{576,672},{6... | collective-permute-start | bytes 55304 | tf_op jit(solution)/shard_map/ppermute | solution.py:385
  65.0 21.3 %all-to-all-start.2 = ((f32[12,40,128]{2,1,0:T(8,128)}), f32[12,40,128]{2,1,0:T(8,128)S(1)}, u32[]{:S(2)}, u32[]{:S(2)}) async-start(f32[12,40,128]{2,1,0:T(8,128)} %sums.4), calls=%async_computation.2 | async-start | bytes 491520 | tf_op jit(solution)/shard_map/all_to_all | solution.py:411
  73.0 12.6 %collective-permute-start.6 = (f32[4,384]{1,0:T(4,128)S(1)}, f32[4,384]{1,0:T(4,128)S(1)}, u32[]{:S(2)}, u32[]{:S(2)}) collective-permute-start(f32[4,384]{1,0:T(4,128)S(1)} %get-tuple-element.55), channel_id=1, source_target_pairs={{0,95},{1,2},{2,1},{3,4},{4,3},{5,6},{6,5},{7,8},{8,7},{9,10},{10,... | collective-permute-start | bytes 18440 | tf_op jit(solution)/shard_map/ppermute | solution.py:385
  81.6 4.7 %collective-permute-start.7 = (f32[4,384]{1,0:T(4,128)S(1)}, f32[4,384]{1,0:T(4,128)S(1)}, u32[]{:S(2)}, u32[]{:S(2)}) collective-permute-start(f32[4,384]{1,0:T(4,128)S(1)} %get-tuple-element.54), channel_id=1, source_target_pairs={{0,1},{1,0},{2,3},{3,2},{4,5},{5,4},{6,7},{7,6},{8,9},{9,8},{10,11... | collective-permute-start | bytes 18440 | tf_op jit(solution)/shard_map/ppermute | solution.py:385
  87.0 11.9 %all-to-all-start.3 = ((f32[8,32,128]{2,1,0:T(8,128)}), f32[8,32,128]{2,1,0:T(8,128)S(1)}, u32[]{:S(2)}, u32[]{:S(2)}) async-start(f32[8,32,128]{2,1,0:T(8,128)} %get-tuple-element.51), calls=%async_computation.3 | async-start | bytes 262144 | tf_op jit(solution)/shard_map/all_to_all | solution.py:411

commit v6 on v5

--- a/solution.py
+++ b/solution.py
@@ -282,10 +282,10 @@
         env_s, mix_s, weighted_s, latent, back, coupled_s, pre, gate = saved[l]
         dpre_s = split2(dlatent * (gate * (1.0 + pre * (1.0 - gate))))
         grad_mix = mm_turned(coupled_s, dpre_s) * share
-        step = min(chunk, LANES)
-        for k in range(0, LANES, step):
-            place, start = divmod(l * LANES + k, chunk)
-            pack_ref[place, start : start + step, :] = grad_mix[k : k + step]
+        for k in range(LANES):
+            place, q = divmod(l * LANES + k, chunk)
+            row, run = divmod(q, chunk // 4)
+            pack_ref[place, row : row + 1, run * LANES : (run + 1) * LANES] = grad_mix[k : k + 1]
         dcoupled = mm_square(dpre_s, mix_s, NT)
         dback_s = split2(dcoupled * latent)
         for k, piece in enumerate(dback_s + weighted_s):
@@ -295,7 +295,7 @@
     row = iota((8, LANES), 0)
     tail = jnp.where(row == 0, grad_out[0:1], jnp.where(row == 1, energy, 0.0)) * share
     for k in range(pack_ref.shape[0]):
-        pack_ref[k, chunk:, :] = tail
+        pack_ref[k, :, chunk // 4 * LANES :] = tail[0:4]
 
     drift_ref[0] = dlatent * first
     drift_ref[1] = dlatent * smooth_col * (gate0 * (1.0 + summed * (1.0 - gate0)))
@@ -389,11 +389,15 @@
     total = in_ref[0]
     for k in range(1, in_ref.shape[0]):
         total = total + in_ref[k]
-    rows = out_refs[0].shape[1]
+    first = total
+    if len(out_refs) > 1:
+        runs = out_refs[0].shape[1] // 4
+        first = jnp.concatenate(
+            [total[r : r + 1, k * LANES : (k + 1) * LANES] for r in range(4) for k in range(runs)], axis=0
+        )
+        out_refs[1][...] = total[:, runs * LANES :]
     for k in range(out_refs[0].shape[0]):
-        out_refs[0][k] = total[:rows]
-    if len(out_refs) > 1:
-        out_refs[1][...] = total[rows:]
+        out_refs[0][k] = first
 
 
 def summed(copies, *shapes):
@@ -461,7 +465,7 @@
     pack, *kept = pl.pallas_call(
         lambda *refs: main_kernel(*refs, blocks=edges // BLOCK_EDGES, devices=devices),
         out_shape=(
-            result(near, chunk + 8, LANES),
+            result(near, 4, (chunk // 4 + 1) * LANES),
             result(16, edges),
             result(edges, 8),
             pltpu.VMEM((4 * layers, edges, LANES), BF16),
@@ -509,9 +513,9 @@
     )(side, *near_by(edge_centers, edge_neighbours, radial_w, *kept))
 
     parts, own, a0, a1, a2 = lax.optimization_barrier((parts, own, a0, a1, a2))
-    (copies,) = summed(parts, (lax.axis_size(MIDDLE), chunk + 8, LANES))
+    (copies,) = summed(parts, (lax.axis_size(MIDDLE),) + pack.shape[1:])
     over = traded(a2, GX, 1), traded(a0, GX, 0)
-    (copies,) = summed(exchanged(copies, MIDDLE), (lax.axis_size(FAR), chunk + 8, LANES))
+    (copies,) = summed(exchanged(copies, MIDDLE), (lax.axis_size(FAR),) + pack.shape[1:])
     copies, over = lax.optimization_barrier((copies, over))
     across = (
         traded(a1[2] + over[0][2] + over[1][2], GY, 1),
@@ -519,7 +523,7 @@
     )
     parts = exchanged(copies, FAR)
     parts, across = lax.optimization_barrier((parts, across))
-    shared, rest = summed(parts, (near, chunk, LANES), (8, LANES))
+    shared, rest = summed(parts, (near, chunk, LANES), (4, LANES))
     forces, grad_out, energy = pl.pallas_call(
         force_kernel,
         out_shape=(

time: 100 us -> 100 us (level)
  no operation moved by 1% of the time
where the time goes in v6:
time: 100 us; the launch traced here: 99.4 us
  starting transfers between devices  71.7 us (72%)
  waiting for transfers between devices  14 us (14%)
  Pallas kernels  12.1 us (12%)
    ppermute x8, starting transfers between devices, traded(): return lax.ppermute(block, axis, route)  47.5 us
    all_to_all x4, starting transfers between devices, exchanged(): return lax.all_to_all(shard, axes, 0, 0)  24.2 us
    ppermute x8, waiting for transfers between devices, traded(): return lax.ppermute(block, axis, route)  7.02 us
    all_to_all x4, waiting for transfers between devices, exchanged(): return lax.all_to_all(shard, axes, 0, 0)  6.96 us
    pallas_call x1, Pallas kernels, body(): pl.pallas_call(lambda *refs: main_kernel(*refs, blocks=edges // BLOCK_EDG...  5.56 us
    pallas_call x3, Pallas kernels, summed(): pl.pallas_call(sum_kernel, out_shape=tuple((pltpu.VMEM(shape, F32) for sh...  2.08 us
    pallas_call x1, Pallas kernels, body(): pl.pallas_call(push_kernel, out_shape=(result(own_rows, 3 * LANES), piece...  2.03 us
  transfers between devices with their start and end apart: 12, of which 7 were waited for; matrix products, arithmetic and copies ran while one was open for 0% of the time, Pallas kernels for 4%

profile of v6, /device:TPU:1, one launch (start us, length us, event | category | flops | bytes accessed | tf_op | source)
XLA Modules:
  0.0 99.4 jit_solution(6240926282435143075)
XLA Ops:
  0.6 0.9 export.1
  1.5 12.4 %collective-permute-start = (f32[4,512]{1,0:T(4,128)S(1)}, f32[4,512]{1,0:T(4,128)S(1)}, u32[]{:S(2)}, u32[]{:S(2)}) collective-permute-start(f32[4,512]{1,0:T(4,128)S(1)} %export.1), channel_id=1, source_target_pairs={{0,96},{96,0},{192,288},{288,192},{384,480},{480,384},{576,672},{6... | collective-permute-start | bytes 24584 | tf_op jit(solution)/shard_map/ppermute | solution.py:385
  13.9 1.9 %collective-permute-start.1 = (f32[4,512]{1,0:T(4,128)S(1)}, f32[4,512]{1,0:T(4,128)S(1)}, u32[]{:S(2)}, u32[]{:S(2)}) collective-permute-start(f32[4,512]{1,0:T(4,128)S(1)} %export.1), channel_id=1, source_target_pairs={{0,672},{96,192},{192,96},{288,384},{384,288},{480,576},{576,480},... | collective-permute-start | bytes 24584 | tf_op jit(solution)/shard_map/ppermute | solution.py:385
  15.9 3.0 %collective-permute-done.1.refs_5_ = f32[4,512]{1,0:T(4,128)S(1)} collective-permute-done((f32[4,512]{1,0:T(4,128)S(1)}, f32[4,512]{1,0:T(4,128)S(1)}, u32[]{:S(2)}, u32[]{:S(2)}) %collective-permute-start.1) | collective-permute-done | bytes 8224 | tf_op jit(solution)/shard_map/ppermute | solution.py:385
  18.9 1.9 %collective-permute-start.2 = (f32[3,4,512]{2,1,0:T(4,128)S(1)}, f32[3,4,512]{2,1,0:T(4,128)S(1)}, u32[]{:S(2)}, u32[]{:S(2)}) collective-permute-start(f32[3,4,512]{2,1,0:T(4,128)S(1)} %pad_maximum_fusion), channel_id=1, source_target_pairs={{0,1},{1,0},{2,3},{3,2},{4,5},{5,4},{6,7},{7,6},{8,9},{9,8},{10,11... | collective-permute-start | bytes 73736 | tf_op jit(solution)/shard_map/ppermute | solution.py:385
  20.8 13.3 %collective-permute-start.3 = (f32[3,4,512]{2,1,0:T(4,128)S(1)}, f32[3,4,512]{2,1,0:T(4,128)S(1)}, u32[]{:S(2)}, u32[]{:S(2)}) collective-permute-start(f32[3,4,512]{2,1,0:T(4,128)S(1)} %pad_maximum_fusion), channel_id=1, source_target_pairs={{0,95},{1,2},{2,1},{3,4},{4,3},{5,6},{6,5},{7,8},{8,7},{9,10},{10,... | collective-permute-start | bytes 73736 | tf_op jit(solution)/shard_map/ppermute | solution.py:385
  34.2 0.0 copy-start.6
  34.2 0.0 copy-start.5
  34.2 0.0 copy-start.4
  34.2 0.0 copy-start.3
  34.2 0.0 copy-start
  34.3 1.2 %collective-permute-done.3.refs_7_ = f32[3,4,512]{2,1,0:T(4,128)S(1)} collective-permute-done((f32[3,4,512]{2,1,0:T(4,128)S(1)}, f32[3,4,512]{2,1,0:T(4,128)S(1)}, u32[]{:S(2)}, u32[]{:S(2)}) %collective-permute-start.3) | collective-permute-done | bytes 24608 | tf_op jit(solution)/shard_map/ppermute | solution.py:385
  35.5 5.6 %edges.1 = (f32[8,4,1152]{2,1,0:T(4,128)}, f32[16,512]{1,0:T(8,128)S(1)}, f32[512,8]{1,0:T(8,128)S(1)}, bf16[8,512,128]{2,1,0:T(8,128)(2,1)S(1)}, f32[2,512,128]{2,1,0:T(8,128)S(1)}) custom-call(s32[1]{0:T(128)} %bitcast.refs_0_.side_ref, s32[1,1,4]{2,1,0:T(1,128)} %refs_1_.1, f32[3,1,1,512]{3,2,1,0:T(1,128)S(1)} %copy-done, s32[1,1,512]{2,1,0:T(1,128)S(1)} %copy-done.1, ...), custom_call_target="tpu_custom_call" | custom-call | tf_op jit(solution)/shard_map/edges/pallas_call | solution.py:465
  41.0 6.2 %all-to-all-start = ((f32[8,4,1152]{2,1,0:T(4,128)}), f32[8,4,1152]{2,1,0:T(4,128)S(1)}, u32[]{:S(2)}, u32[]{:S(2)}) async-start(f32[8,4,1152]{2,1,0:T(4,128)} %get-tuple-element.29), calls=%async_computation | async-start | bytes 294912 | tf_op jit(solution)/shard_map/all_to_all | solution.py:415
  47.2 2.0 %pushes.1 = (f32[4,384]{1,0:T(4,128)S(1)}, f32[3,4,384]{2,1,0:T(4,128)S(1)}, f32[3,4,384]{2,1,0:T(4,128)S(1)}, f32[3,4,384]{2,1,0:T(4,128)S(1)}) custom-call(s32[1]{0:T(128)} %bitcast.refs_0_.side_ref, s32[1,1,512]{2,1,0:T(1,128)S(1)} %copy-done.5, s32[1,1,512]{2,1,0:T(1,128)S(1)} %copy-done.6, f32[8,128]{1,0:T(8,128)S(1)} %copy-done.4, ...), custom_call_target="tpu_custom_call" | custom-call | flops 1000000000 | bytes 2000000 | tf_op jit(solution)/shard_map/pushes/pallas_call | solution.py:506
  49.3 3.3 %all-to-all-done.in_ref = f32[8,4,1152]{2,1,0:T(4,128)S(1)} async-done(((f32[8,4,1152]{2,1,0:T(4,128)}), f32[8,4,1152]{2,1,0:T(4,128)S(1)}, u32[]{:S(2)}, u32[]{:S(2)}) %all-to-all-start) | async-done | bytes 147488 | tf_op jit(solution)/shard_map/all_to_all | solution.py:415
  52.5 0.7 sums.3
  53.2 3.4 %all-to-all-start.1 = ((f32[8,4,1152]{2,1,0:T(4,128)}), f32[8,4,1152]{2,1,0:T(4,128)S(1)}, u32[]{:S(2)}, u32[]{:S(2)}) async-start(f32[8,4,1152]{2,1,0:T(4,128)} %sums.3), calls=%async_computation.1 | async-start | bytes 294912 | tf_op jit(solution)/shard_map/all_to_all | solution.py:415
  56.6 3.8 %collective-permute-start.4 = (f32[3,4,384]{2,1,0:T(4,128)S(1)}, f32[3,4,384]{2,1,0:T(4,128)S(1)}, u32[]{:S(2)}, u32[]{:S(2)}) collective-permute-start(f32[3,4,384]{2,1,0:T(4,128)S(1)} %get-tuple-element.40), channel_id=1, source_target_pairs={{0,672},{96,192},{192,96},{288,384},{384,288},{480,576},{576,480},... | collective-permute-start | bytes 55304 | tf_op jit(solution)/shard_map/ppermute | solution.py:385
  60.4 3.6 %collective-permute-start.5 = (f32[3,4,384]{2,1,0:T(4,128)S(1)}, f32[3,4,384]{2,1,0:T(4,128)S(1)}, u32[]{:S(2)}, u32[]{:S(2)}) collective-permute-start(f32[3,4,384]{2,1,0:T(4,128)S(1)} %get-tuple-element.41), channel_id=1, source_target_pairs={{0,96},{96,0},{192,288},{288,192},{384,480},{480,384},{576,672},{6... | collective-permute-start | bytes 55304 | tf_op jit(solution)/shard_map/ppermute | solution.py:385
  64.0 0.7 sums.4
  64.8 0.1 collective-permute-done.5.up_ref
  64.8 7.9 %all-to-all-start.2 = ((f32[12,4,1152]{2,1,0:T(4,128)}), f32[12,4,1152]{2,1,0:T(4,128)S(1)}, u32[]{:S(2)}, u32[]{:S(2)}) async-start(f32[12,4,1152]{2,1,0:T(4,128)} %sums.4), calls=%async_computation.2 | async-start | bytes 442368 | tf_op jit(solution)/shard_map/all_to_all | solution.py:415
  72.8 8.6 %collective-permute-start.6 = (f32[4,384]{1,0:T(4,128)S(1)}, f32[4,384]{1,0:T(4,128)S(1)}, u32[]{:S(2)}, u32[]{:S(2)}) collective-permute-start(f32[4,384]{1,0:T(4,128)S(1)} %get-tuple-element.55), channel_id=1, source_target_pairs={{0,95},{1,2},{2,1},{3,4},{4,3},{5,6},{6,5},{7,8},{8,7},{9,10},{10,... | collective-permute-start | bytes 18440 | tf_op jit(solution)/shard_map/ppermute | solution.py:385
  81.4 1.9 %collective-permute-start.7 = (f32[4,384]{1,0:T(4,128)S(1)}, f32[4,384]{1,0:T(4,128)S(1)}, u32[]{:S(2)}, u32[]{:S(2)}) collective-permute-start(f32[4,384]{1,0:T(4,128)S(1)} %get-tuple-element.54), channel_id=1, source_target_pairs={{0,1},{1,0},{2,3},{3,2},{4,5},{5,4},{6,7},{7,6},{8,9},{9,8},{10,11... | collective-permute-start | bytes 18440 | tf_op jit(solution)/shard_map/ppermute | solution.py:385
  83.4 2.0 %collective-permute-done.6.left_ref = f32[4,384]{1,0:T(4,128)S(1)} collective-permute-done((f32[4,384]{1,0:T(4,128)S(1)}, f32[4,384]{1,0:T(4,128)S(1)}, u32[]{:S(2)}, u32[]{:S(2)}) %collective-permute-start.6) | collective-permute-done | bytes 6176 | tf_op jit(solution)/shard_map/ppermute | solution.py:385
  85.4 0.7 collective-permute-done.7.right_ref
  86.1 0.7 sums.5
  86.8 6.7 %all-to-all-start.3 = ((f32[8,32,128]{2,1,0:T(8,128)}), f32[8,32,128]{2,1,0:T(8,128)S(1)}, u32[]{:S(2)}, u32[]{:S(2)}) async-start(f32[8,32,128]{2,1,0:T(8,128)} %get-tuple-element.51), calls=%async_computation.3 | async-start | bytes 262144 | tf_op jit(solution)/shard_map/all_to_all | solution.py:415
  93.5 1.5 %forces.1 = (f32[3,1,1,512]{3,2,1,0:T(1,128)}, f32[1,128]{1,0:T(1,128)}, f32[1,1]{1,0:T(1,128)}) custom-call(s32[1,1,384]{2,1,0:T(1,128)} %send_ref.3, f32[4,384]{1,0:T(4,128)S(1)} %get-tuple-element.38.own_ref, f32[3,4,384]{2,1,0:T(4,128)S(1)} %collective-permute-done.4.down_ref, f32[3,4,384]{2,1,0:T(4,128)S(1)} %collective-permute-done.5.up_ref, ...), custom_call_target="tpu_custom_call" | custom-call | tf_op jit(solution)/shard_map/forces/pallas_call | solution.py:527
  95.0 3.7 %all-to-all-done.3 = f32[8,32,128]{2,1,0:T(8,128)S(1)} async-done(((f32[8,32,128]{2,1,0:T(8,128)}), f32[8,32,128]{2,1,0:T(8,128)S(1)}, u32[]{:S(2)}, u32[]{:S(2)}) %all-to-all-start.3) | async-done | bytes 131104 | tf_op jit(solution)/shard_map/all_to_all | solution.py:415
  98.7 0.7 copy.17
  (16 shorter events, 0.1 us)
Async XLA Ops:
  1.5 14.3 %collective-permute-start = (f32[4,512]{1,0:T(4,128)S(1)}, f32[4,512]{1,0:T(4,128)S(1)}, u32[]{:S(2)}, u32[]{:S(2)}) collective-permute-start(f32[4,512]{1,0:T(4,128)S(1)} %export.1), channel_id=1, source_target_pairs={{0,96},{96,0},{192,288},{288,192},{384,480},{480,384},{576,672},{6... | collective-permute-start | bytes 24584 | tf_op jit(solution)/shard_map/ppermute | solution.py:385
  13.9 5.0 %collective-permute-start.1 = (f32[4,512]{1,0:T(4,128)S(1)}, f32[4,512]{1,0:T(4,128)S(1)}, u32[]{:S(2)}, u32[]{:S(2)}) collective-permute-start(f32[4,512]{1,0:T(4,128)S(1)} %export.1), channel_id=1, source_target_pairs={{0,672},{96,192},{192,96},{288,384},{384,288},{480,576},{576,480},... | collective-permute-start | bytes 24584 | tf_op jit(solution)/shard_map/ppermute | solution.py:385
  18.9 15.4 %collective-permute-start.2 = (f32[3,4,512]{2,1,0:T(4,128)S(1)}, f32[3,4,512]{2,1,0:T(4,128)S(1)}, u32[]{:S(2)}, u32[]{:S(2)}) collective-permute-start(f32[3,4,512]{2,1,0:T(4,128)S(1)} %pad_maximum_fusion), channel_id=1, source_target_pairs={{0,1},{1,0},{2,3},{3,2},{4,5},{5,4},{6,7},{7,6},{8,9},{9,8},{10,11... | collective-permute-start | bytes 73736 | tf_op jit(solution)/shard_map/ppermute | solution.py:385
  20.8 14.6 %collective-permute-start.3 = (f32[3,4,512]{2,1,0:T(4,128)S(1)}, f32[3,4,512]{2,1,0:T(4,128)S(1)}, u32[]{:S(2)}, u32[]{:S(2)}) collective-permute-start(f32[3,4,512]{2,1,0:T(4,128)S(1)} %pad_maximum_fusion), channel_id=1, source_target_pairs={{0,95},{1,2},{2,1},{3,4},{4,3},{5,6},{6,5},{7,8},{8,7},{9,10},{10,... | collective-permute-start | bytes 73736 | tf_op jit(solution)/shard_map/ppermute | solution.py:385
  34.2 1.3 %copy-start.6 = (s32[1,1,512]{2,1,0:T(1,128)S(1)}, s32[1,1,512]{2,1,0:T(1,128)}, u32[]{:S(2)}) copy-start(s32[1,1,512]{2,1,0:T(1,128)} %neigh_ref.1) | copy-start | bytes 6148
  34.2 1.3 %copy-start.5 = (s32[1,1,512]{2,1,0:T(1,128)S(1)}, s32[1,1,512]{2,1,0:T(1,128)}, u32[]{:S(2)}) copy-start(s32[1,1,512]{2,1,0:T(1,128)} %cent_ref.1) | copy-start | bytes 6148
  34.2 1.2 %copy-start.4 = (f32[8,128]{1,0:T(8,128)S(1)}, f32[8,128]{1,0:T(8,128)}, u32[]{:S(2)}) copy-start(f32[8,128]{1,0:T(8,128)} %radw_ref.1) | copy-start | bytes 12292
  34.2 1.2 %copy-start.3 = (f32[5,128]{1,0:T(8,128)S(1)}, f32[5,128]{1,0:T(8,128)}, u32[]{:S(2)}) copy-start(f32[5,128]{1,0:T(8,128)} %refs_11_.1) | copy-start | bytes 7684
  34.2 1.2 %copy-start.2 = (f32[5,128]{1,0:T(8,128)S(1)}, f32[5,128]{1,0:T(8,128)}, u32[]{:S(2)}) copy-start(f32[5,128]{1,0:T(8,128)} %refs_10_.1) | copy-start | bytes 7684
  34.2 1.2 %copy-start = (f32[3,1,1,512]{3,2,1,0:T(1,128)S(1)}, f32[3,1,1,512]{3,2,1,0:T(1,128)}, u32[]{:S(2)}) copy-start(f32[3,1,1,512]{3,2,1,0:T(1,128)} %refs_2_.1) | copy-start | bytes 18436
  34.3 1.2 %copy-start.1 = (s32[1,1,512]{2,1,0:T(1,128)S(1)}, s32[1,1,512]{2,1,0:T(1,128)}, u32[]{:S(2)}) copy-start(s32[1,1,512]{2,1,0:T(1,128)} %refs_3_.1) | copy-start | bytes 6148
  41.0 11.5 %all-to-all-start = ((f32[8,4,1152]{2,1,0:T(4,128)}), f32[8,4,1152]{2,1,0:T(4,128)S(1)}, u32[]{:S(2)}, u32[]{:S(2)}) async-start(f32[8,4,1152]{2,1,0:T(4,128)} %get-tuple-element.29), calls=%async_computation | async-start | bytes 294912 | tf_op jit(solution)/shard_map/all_to_all | solution.py:415
  53.2 10.8 %all-to-all-start.1 = ((f32[8,4,1152]{2,1,0:T(4,128)}), f32[8,4,1152]{2,1,0:T(4,128)S(1)}, u32[]{:S(2)}, u32[]{:S(2)}) async-start(f32[8,4,1152]{2,1,0:T(4,128)} %sums.3), calls=%async_computation.1 | async-start | bytes 294912 | tf_op jit(solution)/shard_map/all_to_all | solution.py:415
  56.6 8.1 %collective-permute-start.4 = (f32[3,4,384]{2,1,0:T(4,128)S(1)}, f32[3,4,384]{2,1,0:T(4,128)S(1)}, u32[]{:S(2)}, u32[]{:S(2)}) collective-permute-start(f32[3,4,384]{2,1,0:T(4,128)S(1)} %get-tuple-element.40), channel_id=1, source_target_pairs={{0,672},{96,192},{192,96},{288,384},{384,288},{480,576},{576,480},... | collective-permute-start | bytes 55304 | tf_op jit(solution)/shard_map/ppermute | solution.py:385
  60.4 4.5 %collective-permute-start.5 = (f32[3,4,384]{2,1,0:T(4,128)S(1)}, f32[3,4,384]{2,1,0:T(4,128)S(1)}, u32[]{:S(2)}, u32[]{:S(2)}) collective-permute-start(f32[3,4,384]{2,1,0:T(4,128)S(1)} %get-tuple-element.41), channel_id=1, source_target_pairs={{0,96},{96,0},{192,288},{288,192},{384,480},{480,384},{576,672},{6... | collective-permute-start | bytes 55304 | tf_op jit(solution)/shard_map/ppermute | solution.py:385
  64.8 21.3 %all-to-all-start.2 = ((f32[12,4,1152]{2,1,0:T(4,128)}), f32[12,4,1152]{2,1,0:T(4,128)S(1)}, u32[]{:S(2)}, u32[]{:S(2)}) async-start(f32[12,4,1152]{2,1,0:T(4,128)} %sums.4), calls=%async_computation.2 | async-start | bytes 442368 | tf_op jit(solution)/shard_map/all_to_all | solution.py:415
  72.8 12.6 %collective-permute-start.6 = (f32[4,384]{1,0:T(4,128)S(1)}, f32[4,384]{1,0:T(4,128)S(1)}, u32[]{:S(2)}, u32[]{:S(2)}) collective-permute-start(f32[4,384]{1,0:T(4,128)S(1)} %get-tuple-element.55), channel_id=1, source_target_pairs={{0,95},{1,2},{2,1},{3,4},{4,3},{5,6},{6,5},{7,8},{8,7},{9,10},{10,... | collective-permute-start | bytes 18440 | tf_op jit(solution)/shard_map/ppermute | solution.py:385
  81.4 4.7 %collective-permute-start.7 = (f32[4,384]{1,0:T(4,128)S(1)}, f32[4,384]{1,0:T(4,128)S(1)}, u32[]{:S(2)}, u32[]{:S(2)}) collective-permute-start(f32[4,384]{1,0:T(4,128)S(1)} %get-tuple-element.54), channel_id=1, source_target_pairs={{0,1},{1,0},{2,3},{3,2},{4,5},{5,4},{6,7},{7,6},{8,9},{9,8},{10,11... | collective-permute-start | bytes 18440 | tf_op jit(solution)/shard_map/ppermute | solution.py:385
  86.8 11.9 %all-to-all-start.3 = ((f32[8,32,128]{2,1,0:T(8,128)}), f32[8,32,128]{2,1,0:T(8,128)S(1)}, u32[]{:S(2)}, u32[]{:S(2)}) async-start(f32[8,32,128]{2,1,0:T(8,128)} %get-tuple-element.51), calls=%async_computation.3 | async-start | bytes 262144 | tf_op jit(solution)/shard_map/all_to_all | solution.py:415
